TPU v7x, 32 devices: a whole 2x2x4 slice. The times are simulated.
32 devices in a mesh: dp: 8 (over z, x), head: 4 (over y, core).
Axes of the slice: x: 2, y: 2, z: 4, core: 2. Of those that a mesh axis runs over, the one named last changes fastest.
Arguments:
- input_segments: float32 [16384, 32], P(('dp', 'head')), may hold values from -6 to 6
- filler_flags: int32 [16384, 32], P(('dp', 'head')), may hold values 0 or 1
- sequence_owner: int32 [16384], P(('dp', 'head')), may hold values from 0 to 127, never falling along the last dimension, each value on 1 to 256 neighbouring positions
- prediction_adjoint: bfloat16 [16384, 1280], P('dp', 'head'), may hold values from -6 to 6
- quadratic_params: float32 [6, 1280, 1280], P(None, ('dp', 'head')), may hold values from -0.3354102 to 0.3354102, as said below
- quadratic_velocity: float32 [6, 1280, 1280], P(None, ('dp', 'head')), may hold values from -384 to 384
- quadratic_mean: float32 [6, 1280, 1280], P(None, ('dp', 'head')), may hold values from -0.15625 to 0.15625
- perceptron_params: float32 [2, 1280, 5120], P(None, ('dp', 'head')), may hold values from -0.15625 to 0.15625
- perceptron_velocity: float32 [2, 1280, 5120], P(None, ('dp', 'head')), may hold values from -384 to 384
- perceptron_mean: float32 [2, 1280, 5120], P(None, ('dp', 'head')), may hold values from -0.15625 to 0.15625
- embedder_params: float32 [2, 1280, 64], P(None, ('dp', 'head')), may hold values from -0.75 to 0.75
- embedder_velocity: float32 [2, 1280, 64], P(None, ('dp', 'head')), may hold values from -384 to 384
- embedder_mean: float32 [2, 1280, 64], P(None, ('dp', 'head')), may hold values from -0.75 to 0.75
- bias_gain_params: float32 [5, 1280], P(None, ('dp', 'head')), may hold values from -1.6 to 1.6, as said below
- bias_gain_velocity: float32 [5, 1280], P(None, ('dp', 'head')), may hold values from -384 to 384
- bias_gain_mean: float32 [5, 1280], P(None, ('dp', 'head')), may hold values from -1.6 to 1.6, as said below
- readout_params: float32 [2, 1280, 1280], P(None, 'dp', 'head'), may hold values from -0.15625 to 0.15625
- readout_velocity: float32 [2, 1280, 1280], P(None, 'dp', 'head'), may hold values from -384 to 384
- readout_mean: float32 [2, 1280, 1280], P(None, 'dp', 'head'), may hold values from -0.15625 to 0.15625
Outputs:
- prediction: bfloat16 [16384, 1280], P('dp', 'head')
- segment_derivative: float32 [16384, 32], P(('dp', 'head'))
- quadratic_params_fresh: float32 [6, 1280, 1280], P(None, ('dp', 'head'))
- quadratic_velocity_fresh: float32 [6, 1280, 1280], P(None, ('dp', 'head'))
- quadratic_mean_fresh: float32 [6, 1280, 1280], P(None, ('dp', 'head'))
- perceptron_params_fresh: float32 [2, 1280, 5120], P(None, ('dp', 'head'))
- perceptron_velocity_fresh: float32 [2, 1280, 5120], P(None, ('dp', 'head'))
- perceptron_mean_fresh: float32 [2, 1280, 5120], P(None, ('dp', 'head'))
- embedder_params_fresh: float32 [2, 1280, 64], P(None, ('dp', 'head'))
- embedder_velocity_fresh: float32 [2, 1280, 64], P(None, ('dp', 'head'))
- embedder_mean_fresh: float32 [2, 1280, 64], P(None, ('dp', 'head'))
- bias_gain_params_fresh: float32 [5, 1280], P(None, ('dp', 'head'))
- bias_gain_velocity_fresh: float32 [5, 1280], P(None, ('dp', 'head'))
- bias_gain_mean_fresh: float32 [5, 1280], P(None, ('dp', 'head'))
- readout_params_fresh: float32 [2, 1280, 1280], P(None, 'dp', 'head')
- readout_velocity_fresh: float32 [2, 1280, 1280], P(None, 'dp', 'head')
- readout_mean_fresh: float32 [2, 1280, 1280], P(None, 'dp', 'head')
Inputs may be any that keep to these rules, and one draw needn't show every extreme that they name: quadratic_params entries lie within this range. bias_gain_params entries lie within this range. bias_gain_mean entries lie within this range.
All inputs are finite; a program needn't handle non-finite values. No bound on the sum of `filler_flags` on one device may be relied on, other than what follows from the above.
Results may differ from a plain program's by a relative error of at most 0.019.
Values may be sent and summed in bfloat16 or wider, within the bound.
A program may use at most 448 MiB of HBM per device.

v0:
```python
import jax
import jax.numpy as jnp
from jax import lax
from jax.sharding import PartitionSpec as P

D = 1280
HEADS = 16
HEAD_DIM = 80
PATCH = 32
SEQ = 512


EPSILON = 1e-06
MOMENTUM = 0.9
AVG_DECAY = 0.9


def matrix_multiply(left_mat, right_mat):
    return jnp.dot(left_mat, right_mat, preferred_element_type=jnp.float32)


def flipped_bilinear(left_mat, right_mat):
    return lax.dot_general(
        left_mat, right_mat, (((1,), (1,)), ((), ())), preferred_element_type=jnp.float32
    )


def bilinear_flipped(left_mat, right_mat):
    return lax.dot_general(
        left_mat, right_mat, (((0,), (0,)), ((), ())), preferred_element_type=jnp.float32
    )


def rounded(values_in):
    return values_in.astype(jnp.bfloat16)


def rms_gain(values_in, gains_in):
    return (
        values_in
        * lax.rsqrt(jnp.mean(values_in * values_in, axis=-1, keepdims=True) + EPSILON)
        * gains_in
    )


def silu_slope(values_in):
    logistic = jax.nn.sigmoid(values_in)
    return logistic * (1.0 + values_in * (1.0 - logistic))


def rope_tables():
    half_dim = HEAD_DIM // 2
    position = jnp.arange(SEQ, dtype=jnp.float32)[:, None]
    spacing = 10000.0 ** (-jnp.arange(half_dim, dtype=jnp.float32) / half_dim)
    angles = position * spacing[None, :]
    return (jnp.cos(angles), jnp.sin(angles))


def rotate(heads_in, cosines, sines):
    half_dim = heads_in.shape[-1] // 2
    lower_half = heads_in[..., :half_dim]
    upper_half = heads_in[..., half_dim:]
    cos_rows = cosines[:, None, :]
    sin_rows = sines[:, None, :]
    return jnp.concatenate(
        [
            lower_half * cos_rows - upper_half * sin_rows,
            upper_half * cos_rows + lower_half * sin_rows,
        ],
        axis=-1,
    )


def masked_scores(query_heads, key_heads, segments):
    scores = jnp.einsum(
        "qhd,khd->hqk", query_heads, key_heads, preferred_element_type=jnp.float32
    ) * HEAD_DIM ** (-0.5)
    places = jnp.arange(SEQ)
    allowed = (places[:, None] >= places[None, :]) & (segments[:, None] == segments[None, :])
    return jnp.where(allowed[None], scores, -1e30)


def attend(bundle):
    query_heads, key_heads, value_heads, segments = bundle
    scores = masked_scores(query_heads, key_heads, segments)
    row_max = jnp.max(scores, axis=-1, keepdims=True)
    expo = jnp.exp(scores - row_max)
    row_total = jnp.sum(expo, axis=-1, keepdims=True)
    probability = expo / row_total
    mixed = jnp.einsum(
        "hqk,khd->qhd", rounded(probability), value_heads, preferred_element_type=jnp.float32
    )
    return (rounded(mixed), (row_max + jnp.log(row_total))[..., 0])


def attend_back(bundle):
    query_heads, key_heads, value_heads, segments, log_totals, grad_mixed = bundle
    scores = masked_scores(query_heads, key_heads, segments)
    probability = jnp.exp(scores - log_totals[..., None])
    grad_probs = jnp.einsum(
        "qhd,khd->hqk", grad_mixed, value_heads, preferred_element_type=jnp.float32
    )
    grad_values = jnp.einsum(
        "hqk,qhd->khd", rounded(probability), grad_mixed, preferred_element_type=jnp.float32
    )
    inner_sum = jnp.sum(probability * grad_probs, axis=-1, keepdims=True)
    grad_scores = rounded(probability * (grad_probs - inner_sum))
    grad_queries = jnp.einsum(
        "hqk,khd->qhd", grad_scores, key_heads, preferred_element_type=jnp.float32
    ) * HEAD_DIM ** (-0.5)
    grad_keys = jnp.einsum(
        "hqk,qhd->khd", grad_scores, query_heads, preferred_element_type=jnp.float32
    ) * HEAD_DIM ** (-0.5)
    return (grad_queries, grad_keys, grad_values)


def update(master, moment, average, gradient, rate):
    moment_new = MOMENTUM * moment + gradient
    master_new = master - rate * (gradient + MOMENTUM * moment_new)
    average_new = AVG_DECAY * average + (1.0 - AVG_DECAY) * master_new
    return (master_new, moment_new, average_new)


def on_device(
    input_segments,
    filler_flags,
    sequence_owner,
    prediction_adjoint,
    quadratic_params,
    quadratic_velocity,
    quadratic_mean,
    perceptron_params,
    perceptron_velocity,
    perceptron_mean,
    embedder_params,
    embedder_velocity,
    embedder_mean,
    bias_gain_params,
    bias_gain_velocity,
    bias_gain_mean,
    readout_params,
    readout_velocity,
    readout_mean,
):
    square, ffn, token, vector_low = (
        lax.all_gather(rounded(quadratic_params), ("dp", "head"), axis=1, tiled=True),
        lax.all_gather(rounded(perceptron_params), ("dp", "head"), axis=1, tiled=True),
        lax.all_gather(rounded(embedder_params), ("dp", "head"), axis=1, tiled=True),
        lax.all_gather(rounded(bias_gain_params), ("dp", "head"), axis=1, tiled=True),
    )
    readout_outcome = lax.all_gather(rounded(readout_params), "dp", axis=1, tiled=True)
    vectors = vector_low.astype(jnp.float32)
    tok_count = input_segments.shape[0]
    seq_rows = tok_count // SEQ
    mask_float = filler_flags.astype(jnp.float32)
    tok_input = rounded(jnp.concatenate([input_segments * (1.0 - mask_float), mask_float], axis=1))
    tok_pre = flipped_bilinear(tok_input, token[0]) + vectors[2]
    tok_act = rounded(jax.nn.silu(tok_pre))
    stream_in = (
        matrix_multiply(tok_act, square[0]) + flipped_bilinear(tok_input, token[1]) + vectors[3]
    )
    normed_one, norm_pull_one = jax.vjp(rms_gain, stream_in, vectors[0])
    normed_attn = rounded(normed_one)
    cosines, sines = rope_tables()
    query_heads = rounded(
        rotate(
            matrix_multiply(normed_attn, square[1]).reshape(seq_rows, SEQ, HEADS, HEAD_DIM),
            cosines,
            sines,
        )
    )
    key_heads = rounded(
        rotate(
            matrix_multiply(normed_attn, square[2]).reshape(seq_rows, SEQ, HEADS, HEAD_DIM),
            cosines,
            sines,
        )
    )
    value_heads = rounded(matrix_multiply(normed_attn, square[3])).reshape(
        seq_rows, SEQ, HEADS, HEAD_DIM
    )
    seg_rows = sequence_owner.reshape(seq_rows, SEQ)
    mixed, log_totals = lax.map(attend, (query_heads, key_heads, value_heads, seg_rows))
    attn_mix = mixed.reshape(tok_count, D)
    stream_mid = stream_in + matrix_multiply(attn_mix, square[4])
    normed_two, norm_pull_two = jax.vjp(rms_gain, stream_mid, vectors[1])
    normed_ffn = rounded(normed_two)
    ffn_pre = matrix_multiply(normed_ffn, ffn[0])
    ffn_act = rounded(jax.nn.silu(ffn_pre))
    stream_out = stream_mid + flipped_bilinear(ffn_act, ffn[1])
    stream_low = rounded(stream_out)
    head_pre = matrix_multiply(stream_low, square[5]) + vectors[4]
    head_act = rounded(jax.nn.silu(head_pre))
    shortcut_complete, readout_complete = (
        lax.all_gather(stream_low, "head", axis=0, tiled=True),
        lax.all_gather(head_act, "head", axis=0, tiled=True),
    )
    prediction = (
        matrix_multiply(readout_complete, readout_outcome[0])
        + matrix_multiply(shortcut_complete, readout_outcome[1])
    ).astype(jnp.bfloat16)
    gradient_of_head = jnp.stack(
        [
            bilinear_flipped(readout_complete, prediction_adjoint),
            bilinear_flipped(shortcut_complete, prediction_adjoint),
        ]
    )
    grad_head_act, grad_skip = (
        lax.psum_scatter(
            flipped_bilinear(prediction_adjoint, readout_outcome[0]).astype(jnp.bfloat16),
            "head",
            scatter_dimension=0,
            tiled=True,
        ).astype(jnp.float32),
        lax.psum_scatter(
            flipped_bilinear(prediction_adjoint, readout_outcome[1]).astype(jnp.bfloat16),
            "head",
            scatter_dimension=0,
            tiled=True,
        ).astype(jnp.float32),
    )
    grad_head_pre = rounded(grad_head_act * silu_slope(head_pre))
    grad_bias_head = jnp.sum(grad_head_pre.astype(jnp.float32), axis=0)
    grad_wh = bilinear_flipped(stream_low, grad_head_pre)
    grad_stream_out = grad_skip + flipped_bilinear(grad_head_pre, square[5])
    grad_ffn_out = rounded(grad_stream_out)
    grad_down = bilinear_flipped(grad_ffn_out, ffn_act)
    grad_ffn_pre = rounded(matrix_multiply(grad_ffn_out, ffn[1]) * silu_slope(ffn_pre))
    grad_up = bilinear_flipped(normed_ffn, grad_ffn_pre)
    grad_stream_norm, grad_gain_two = norm_pull_two(flipped_bilinear(grad_ffn_pre, ffn[0]))
    grad_stream_mid = grad_stream_out + grad_stream_norm
    grad_ffn = jnp.stack([grad_up, grad_down])
    grad_attn_out = rounded(grad_stream_mid)
    grad_wo = bilinear_flipped(attn_mix, grad_attn_out)
    grad_attn_mix = rounded(flipped_bilinear(grad_attn_out, square[4])).reshape(
        seq_rows, SEQ, HEADS, HEAD_DIM
    )
    grad_queries, grad_keys, grad_values = lax.map(
        attend_back, (query_heads, key_heads, value_heads, seg_rows, log_totals, grad_attn_mix)
    )
    grad_q_pre = rounded(rotate(grad_queries, cosines, -sines).reshape(tok_count, D))
    grad_k_pre = rounded(rotate(grad_keys, cosines, -sines).reshape(tok_count, D))
    grad_v_pre = rounded(grad_values.reshape(tok_count, D))
    grad_wq = bilinear_flipped(normed_attn, grad_q_pre)
    grad_wk = bilinear_flipped(normed_attn, grad_k_pre)
    grad_wv = bilinear_flipped(normed_attn, grad_v_pre)
    grad_normed = (
        flipped_bilinear(grad_q_pre, square[1])
        + flipped_bilinear(grad_k_pre, square[2])
        + flipped_bilinear(grad_v_pre, square[3])
    )
    grad_stream_first, grad_gain_one = norm_pull_one(grad_normed)
    grad_stream_in = grad_stream_mid + grad_stream_first
    grad_bias_out = jnp.sum(grad_stream_in, axis=0)
    grad_tok_out = rounded(grad_stream_in)
    grad_wb = bilinear_flipped(tok_act, grad_tok_out)
    grad_skip_tok = bilinear_flipped(grad_tok_out, tok_input)
    grad_tok_pre = rounded(flipped_bilinear(grad_tok_out, square[0]) * silu_slope(tok_pre))
    grad_bias_tok = jnp.sum(grad_tok_pre.astype(jnp.float32), axis=0)
    grad_hidden_tok = bilinear_flipped(grad_tok_pre, tok_input)
    grad_input = matrix_multiply(grad_tok_out, token[1]) + matrix_multiply(grad_tok_pre, token[0])
    segment_derivative = grad_input[:, :PATCH] * (1.0 - mask_float)
    grad_square = jnp.stack([grad_wb, grad_wq, grad_wk, grad_wv, grad_wo, grad_wh])
    grad_token = jnp.stack([grad_hidden_tok, grad_skip_tok])
    grad_vector = jnp.stack(
        [grad_gain_one, grad_gain_two, grad_bias_tok, grad_bias_out, grad_bias_head]
    )
    square_share, ffn_share, token_share, vector_share = (
        lax.psum_scatter(grad_square, ("dp", "head"), scatter_dimension=1, tiled=True),
        lax.psum_scatter(grad_ffn, ("dp", "head"), scatter_dimension=1, tiled=True),
        lax.psum_scatter(grad_token, ("dp", "head"), scatter_dimension=1, tiled=True),
        lax.psum_scatter(grad_vector, ("dp", "head"), scatter_dimension=1, tiled=True),
    )
    head_share = lax.psum_scatter(gradient_of_head, "dp", scatter_dimension=1, tiled=True)
    all_tokens = tok_count * lax.axis_size("dp") * lax.axis_size("head")
    matrix_rate = 0.5 / (D * all_tokens) ** 0.5
    quadratic_params_fresh, quadratic_velocity_fresh, quadratic_mean_fresh = update(
        quadratic_params, quadratic_velocity, quadratic_mean, square_share, matrix_rate
    )
    perceptron_params_fresh, perceptron_velocity_fresh, perceptron_mean_fresh = update(
        perceptron_params, perceptron_velocity, perceptron_mean, ffn_share, matrix_rate
    )
    embedder_params_fresh, embedder_velocity_fresh, embedder_mean_fresh = update(
        embedder_params,
        embedder_velocity,
        embedder_mean,
        token_share,
        0.5 / (2 * PATCH * all_tokens) ** 0.5,
    )
    bias_gain_params_fresh, bias_gain_velocity_fresh, bias_gain_mean_fresh = update(
        bias_gain_params, bias_gain_velocity, bias_gain_mean, vector_share, 0.3 / all_tokens**0.5
    )
    readout_params_fresh, readout_velocity_fresh, readout_mean_fresh = update(
        readout_params, readout_velocity, readout_mean, head_share, matrix_rate
    )
    return (
        prediction,
        segment_derivative,
        quadratic_params_fresh,
        quadratic_velocity_fresh,
        quadratic_mean_fresh,
        perceptron_params_fresh,
        perceptron_velocity_fresh,
        perceptron_mean_fresh,
        embedder_params_fresh,
        embedder_velocity_fresh,
        embedder_mean_fresh,
        bias_gain_params_fresh,
        bias_gain_velocity_fresh,
        bias_gain_mean_fresh,
        readout_params_fresh,
        readout_velocity_fresh,
        readout_mean_fresh,
    )


def solution(mesh):
    placed = (
        P(("dp", "head"), None),
        P(("dp", "head"), None),
        P(("dp", "head")),
        P("dp", "head"),
        P(None, ("dp", "head"), None),
        P(None, ("dp", "head"), None),
        P(None, ("dp", "head"), None),
        P(None, ("dp", "head"), None),
        P(None, ("dp", "head"), None),
        P(None, ("dp", "head"), None),
        P(None, ("dp", "head"), None),
        P(None, ("dp", "head"), None),
        P(None, ("dp", "head"), None),
        P(None, ("dp", "head")),
        P(None, ("dp", "head")),
        P(None, ("dp", "head")),
        P(None, "dp", "head"),
        P(None, "dp", "head"),
        P(None, "dp", "head"),
    )
    return jax.shard_map(
        on_device,
        mesh=mesh,
        in_specs=placed,
        out_specs=(
            P("dp", "head"),
            P(("dp", "head"), None),
            P(None, ("dp", "head"), None),
            P(None, ("dp", "head"), None),
            P(None, ("dp", "head"), None),
            P(None, ("dp", "head"), None),
            P(None, ("dp", "head"), None),
            P(None, ("dp", "head"), None),
            P(None, ("dp", "head"), None),
            P(None, ("dp", "head"), None),
            P(None, ("dp", "head"), None),
            P(None, ("dp", "head")),
            P(None, ("dp", "head")),
            P(None, ("dp", "head")),
            P(None, "dp", "head"),
            P(None, "dp", "head"),
            P(None, "dp", "head"),
        ),
        check_vma=False,
    )
```

profile of v0, /device:TPU:0, one launch (start us, length us, event | category | flops | bytes accessed | tf_op | source)
XLA Modules:
  0.0 1779.4 jit_solution(10228850122551237173)
XLA Ops:
  12.6 48.8 %all-gather.13.cloned.1.call-done = bf16[2,1280,320]{2,1,0:T(8,128)(2,1)} async-done(((bf16[2,160,320]{2,1,0:T(8,128)(2,1)}), bf16[2,1280,320]{2,1,0:T(8,128)(2,1)}) %all-gather.13.cloned.1.call-update) | async-done | bytes 1638416 | tf_op jit(solution)/shard_map/all_gather | solution.py:151
  61.3 5.9 convolution_convert_fusion
  68.0 40.2 %all-gather = bf16[32,40,5]{1,2,0:T(8,128)(2,1)S(1)} all-gather(bf16[1,40,5]{1,2,0:T(8,128)(2,1)S(1)} %convert_bitcast_fusion), channel_id=1, replica_groups=mesh['dp'=8,'head'=4] {'dp','head'}, dimensions={0}, use_global_device_ids=true | all-gather | bytes 13200 | tf_op jit(solution)/shard_map/all_gather | solution.py:149
  108.4 41.0 %all_gather.21 = bf16[2,1280,64]{2,1,0:T(8,128)(2,1)S(1)} all-gather(bf16[2,40,64]{2,1,0:T(8,128)(2,1)S(1)} %convert_element_type.162), channel_id=1, replica_groups=mesh['dp'=8,'head'=4] {'dp','head'}, dimensions={1}, use_global_device_ids=true | all-gather | bytes 337920 | tf_op jit(solution)/shard_map/all_gather | solution.py:148
  152.8 5.8 convolution_convert_fusion.1
  158.7 33.9 %all-gather.7.cloned.1.call-done = bf16[6,1280,1280]{2,1,0:T(8,128)(2,1)} async-done(((bf16[6,40,1280]{2,1,0:T(8,128)(2,1)}), bf16[6,1280,1280]{2,1,0:T(8,128)(2,1)}) %all-gather.7.cloned.1.call-update) | async-done | bytes 19660816 | tf_op jit(solution)/shard_map/all_gather | solution.py:146
  192.6 4.9 fusion.23
  199.6 6.2 slice_bitcast_fusion.25
  205.8 5.9 copy.104
  211.7 5.7 copy.105
  225.0 7.7 fusion.58
  232.7 4.8 convolution_convert_fusion.3
  239.2 8.8 fusion
  248.0 8.2 fusion.29
  256.2 5.9 multiply_reduce_fusion.5
  262.1 93.2 %all-gather.9.cloned.1.call-done = bf16[2,1280,5120]{2,1,0:T(8,128)(2,1)} async-done(((bf16[2,40,5120]{2,1,0:T(8,128)(2,1)}), bf16[2,1280,5120]{2,1,0:T(8,128)(2,1)}) %all-gather.9.cloned.1.call-update) | async-done | bytes 26214416 | tf_op jit(solution)/shard_map/all_gather | solution.py:147
  355.3 13.3 fusion.3
  368.5 17.6 fusion.22
  386.2 21.1 %reduce-scatter.8.cloned.1.call-done = bf16[512,1280]{1,0:T(8,128)(2,1)} async-done(((bf16[2048,1280]{1,0:T(8,128)(2,1)}), bf16[512,1280]{1,0:T(8,128)(2,1)}) %reduce-scatter.8.cloned.1.call-update) | async-done | bytes 1310736 | tf_op jit(solution)/shard_map/reduce_scatter | solution.py:209
  407.2 7.0 convert_reduce_fusion
  415.1 45.9 %reduce-scatter.6.cloned.1.call-done = bf16[512,1280]{1,0:T(8,128)(2,1)} async-done(((bf16[2048,1280]{1,0:T(8,128)(2,1)}), bf16[512,1280]{1,0:T(8,128)(2,1)}) %reduce-scatter.6.cloned.1.call-update) | async-done | bytes 1310736 | tf_op jit(solution)/shard_map/reduce_scatter | solution.py:215
  466.7 15.6 multiply_convert_fusion.1
  482.3 14.8 multiply_reduce_fusion.1
  501.8 4.9 convolution_convert_fusion.2
  508.4 13.4 multiply_reduce_fusion
  521.7 12.6 multiply_convert_fusion
  539.6 4.8 fusion.19
  548.4 8.6 fusion.30
  557.0 4.8 multiply_reduce_fusion.2
  570.9 5.5 convolution_bitcast_fusion.9
  582.9 7.5 copy.114
  590.5 6.6 fusion.11
  597.1 4.6 fusion.10
  601.8 4.7 fusion.9
  606.5 4.6 fusion.8
  611.0 4.7 fusion.7
  615.7 4.6 fusion.6
  620.6 15.1 convolution_bitcast_fusion.1
  635.7 16.4 convolution_bitcast_fusion
  652.1 35.3 %pad_maximum_fusion = f32[2,1280,5120]{2,1,0:T(8,128)} fusion(f32[1,1280,5120]{2,1,0:T(8,128)} %convolution_bitcast_fusion, f32[1,1280,5120]{2,1,0:T(8,128)} %convolution_bitcast_fusion.1), kind=kLoop, calls=%fused_computation | loop fusion | flops 13107200 | bytes 104857600 | tf_op jit(solution)/shard_map/stack | solution.py:232
  689.4 42.2 %all-reduce.1 = f32[5,1280]{1,0:T(8,128)S(1)} all-reduce(f32[5,1280]{1,0:T(8,128)S(1)} %stack.78), channel_id=7, replica_groups=mesh['dp'=8,'head'=4] {'dp','head'}, use_global_device_ids=true, to_apply=%region_17.18.clone | all-reduce | flops 6400 | bytes 51200
  737.5 4.8 fusion.36
  742.4 5.7 fusion.26
  748.2 107.0 %all-reduce.8.cloned.1.call-done = f32[2,1280,320]{2,0,1:T(2,128)} async-done(((f32[2,1280,320]{2,0,1:T(2,128)}), f32[2,1280,320]{2,0,1:T(2,128)}) %all-reduce.8.cloned.1.call-update) | async-done | bytes 3276816
  857.6 361.6 %reduce-scatter.10.cloned.1.call-done = f32[6,40,1280]{2,1,0:T(8,128)} async-done(((f32[6,1280,1280]{2,1,0:T(8,128)}), f32[6,40,1280]{2,1,0:T(8,128)}) %reduce-scatter.10.cloned.1.call-update) | async-done | bytes 1228816 | tf_op jit(solution)/shard_map/reduce_scatter | solution.py:269
  1219.2 4.6 multiply_add_fusion.4
  1223.8 543.5 %reduce-scatter.12.cloned.1.call-done = f32[2,40,5120]{2,1,0:T(8,128)} async-done(((f32[2,1280,5120]{2,1,0:T(8,128)}), f32[2,40,5120]{2,1,0:T(8,128)}) %reduce-scatter.12.cloned.1.call-update) | async-done | bytes 1638416 | tf_op jit(solution)/shard_map/reduce_scatter | solution.py:270
  1767.3 5.2 multiply_add_fusion
  (225 shorter events, 68.0 us)
Async XLA Ops:
  7.2 54.1 %copy-start = (bf16[2048,320]{0,1:T(8,128)(2,1)S(1)}, bf16[2048,320]{0,1:T(8,128)(2,1)}, u32[]{:S(2)}) copy-start(bf16[2048,320]{0,1:T(8,128)(2,1)} %param.22) | copy-start | bytes 3932164
  7.2 54.1 %all-gather.13.cloned.1.call-start = ((), (), s32[]{:S(2)}) async-start(), calls=%async_computation.7 | async-start | bytes 2211840 | tf_op jit(solution)/shard_map/all_gather | solution.py:151
  9.2 183.4 %all-gather.7.cloned.1.call-start = ((), (), s32[]{:S(2)}) async-start(), calls=%async_computation.4 | async-start | bytes 20275200 | tf_op jit(solution)/shard_map/all_gather | solution.py:146
  11.4 343.9 %all-gather.9.cloned.1.call-start = ((), (), s32[]{:S(2)}) async-start(), calls=%async_computation.5 | async-start | bytes 27033600 | tf_op jit(solution)/shard_map/all_gather | solution.py:147
  12.5 394.7 %reduce-scatter.8.cloned.1.call-start = ((), (), s32[]{:S(2)}) async-start(), calls=%async_computation.10 | async-start | bytes 6553600 | tf_op jit(solution)/shard_map/reduce_scatter | solution.py:209
  67.2 82.3 %copy-start.46 = (s32[512,32]{0,1:T(8,128)S(1)}, s32[512,32]{0,1:T(8,128)}, u32[]{:S(2)}) copy-start(s32[512,32]{0,1:T(8,128)} %param.20) | copy-start | bytes 196612
  67.2 82.3 %copy-start.55 = (f32[512,32]{0,1:T(8,128)S(1)}, f32[512,32]{0,1:T(8,128)}, u32[]{:S(2)}) copy-start(f32[512,32]{0,1:T(8,128)} %param.19) | copy-start | bytes 196612
  67.2 83.3 %copy-start.64 = (s32[512]{0:T(512)S(1)}, s32[512]{0:T(512)}, u32[]{:S(2)}) copy-start(s32[512]{0:T(512)} %param.21) | copy-start | bytes 6148
  67.2 393.7 %reduce-scatter.6.cloned.1.call-start = ((), (), s32[]{:S(2)}) async-start(), calls=%async_computation.9 | async-start | bytes 6553600 | tf_op jit(solution)/shard_map/reduce_scatter | solution.py:215
  108.4 109.0 %copy-start.53 = (f32[1280]{0:T(1024)}, f32[1280]{0:T(1024)S(1)}, u32[]{:S(2)}) copy-start(f32[1280]{0:T(1024)S(1)} %get-tuple-element.125) | copy-start | bytes 15364
  149.4 48.1 %copy-start.11 = (bf16[2,1280,64]{2,1,0:T(8,128)(2,1)}, bf16[2,1280,64]{2,1,0:T(8,128)(2,1)S(1)}, u32[]{:S(2)}) copy-start(bf16[2,1280,64]{2,1,0:T(8,128)(2,1)S(1)} %all_gather.21) | copy-start | bytes 983044
  149.5 48.1 %copy-start.40 = (bf16[512,32]{0,1:T(8,128)(2,1)}, bf16[512,32]{0,1:T(8,128)(2,1)S(1)}, u32[]{:S(2)}) copy-start(bf16[512,32]{0,1:T(8,128)(2,1)S(1)} %convert_convert_fusion) | copy-start | bytes 98308
  149.5 48.0 %copy-start.42 = (bf16[512,32]{0,1:T(8,128)(2,1)}, bf16[512,32]{0,1:T(8,128)(2,1)S(1)}, u32[]{:S(2)}) copy-start(bf16[512,32]{0,1:T(8,128)(2,1)S(1)} %multiply_convert_fusion.8) | copy-start | bytes 98308
  150.5 73.6 %copy-start.44 = (f32[512,40]{0,1:T(8,128)}, f32[512,40]{0,1:T(8,128)S(1)}, u32[]{:S(2)}) copy-start(f32[512,40]{0,1:T(8,128)S(1)} %get-tuple-element.164) | copy-start | bytes 245764
  158.7 412.2 %all-gather.11.cloned.1.call-start = ((), (), s32[]{:S(2)}) async-start(), calls=%async_computation.6 | async-start | bytes 6553600 | tf_op jit(solution)/shard_map/all_gather | solution.py:196
  199.6 17.8 copy-start.60
  219.6 13.1 copy-start.32
  224.9 7.7 copy-start.17
  224.9 7.7 copy-start.19
  224.9 7.7 copy-start.21
  225.0 7.7 copy-start.23
  239.2 8.8 copy-start.13
  248.0 8.3 copy-start.1
  386.2 28.1 %copy-start.38 = (bf16[512,1280]{1,0:T(8,128)(2,1)}, bf16[512,1280]{1,0:T(8,128)(2,1)S(1)}, u32[]{:S(2)}) copy-start(bf16[512,1280]{1,0:T(8,128)(2,1)S(1)} %fusion.22) | copy-start | bytes 3932164
  414.3 46.7 %copy-start.70 = (bf16[512,1280]{1,0:T(8,128)(2,1)S(1)}, bf16[512,1280]{1,0:T(8,128)(2,1)}, u32[]{:S(2)}) copy-start(bf16[512,1280]{1,0:T(8,128)(2,1)} %get-tuple-element.135) | copy-start | bytes 3932164
  414.3 162.1 %all-gather.15.cloned.1.call-start = ((), (), s32[]{:S(2)}) async-start(), calls=%async_computation.8 | async-start | bytes 6553600 | tf_op jit(solution)/shard_map/all_gather | solution.py:195
  415.0 321.0 %all-reduce.6.cloned.1.call-start = ((), (), s32[]{:S(2)}) async-start(), calls=%async_computation.13 | async-start | bytes 2621440
  466.7 15.6 copy-start.6
  521.7 12.6 copy-start.22
  521.7 12.6 copy-start.24
  548.3 8.6 copy-start.2
  548.3 8.6 copy-start.54
  548.3 8.6 copy-start.61
  570.9 284.3 %all-reduce.8.cloned.1.call-start = ((), (), s32[]{:S(2)}) async-start(), calls=%async_computation.14 | async-start | bytes 7864320
  590.5 628.8 %reduce-scatter.10.cloned.1.call-start = ((), (), s32[]{:S(2)}) async-start(), calls=%async_computation.11 | async-start | bytes 40550400 | tf_op jit(solution)/shard_map/reduce_scatter | solution.py:269
  620.3 1147.0 %reduce-scatter.12.cloned.1.call-start = ((), (), s32[]{:S(2)}) async-start(), calls=%async_computation.12 | async-start | bytes 54067200 | tf_op jit(solution)/shard_map/reduce_scatter | solution.py:270
  620.6 15.1 copy-start.27
  687.4 44.2 %copy-start.63 = (f32[5,40]{1,0:T(8,128)S(1)}, f32[5,40]{1,0:T(8,128)}, u32[]{:S(2)}) copy-start(f32[5,40]{1,0:T(8,128)} %param.32) | copy-start | bytes 2404
  687.4 44.2 %copy-start.67 = (f32[5,40]{1,0:T(8,128)S(1)}, f32[5,40]{1,0:T(8,128)}, u32[]{:S(2)}) copy-start(f32[5,40]{1,0:T(8,128)} %param.34) | copy-start | bytes 2404
  687.4 45.6 %copy-start.12 = (bf16[2,1280,64]{2,1,0:T(8,128)(2,1)S(1)}, bf16[2,1280,64]{2,1,0:T(8,128)(2,1)}, u32[]{:S(2)}) copy-start(bf16[2,1280,64]{2,1,0:T(8,128)(2,1)} %copy-done.11) | copy-start | bytes 983044
  687.5 48.0 %copy-start.47 = (s32[512,32]{0,1:T(8,128)S(1)}, s32[512,32]{0,1:T(8,128)}, u32[]{:S(2)}) copy-start(s32[512,32]{0,1:T(8,128)} %param.20) | copy-start | bytes 196612
  687.5 49.4 %copy-start.52 = (f32[2,40,64]{2,1,0:T(8,128)S(1)}, f32[2,40,64]{2,1,0:T(8,128)}, u32[]{:S(2)}) copy-start(f32[2,40,64]{2,1,0:T(8,128)} %param.29) | copy-start | bytes 61444
  687.5 49.4 %copy-start.56 = (f32[2,40,64]{2,1,0:T(8,128)S(1)}, f32[2,40,64]{2,1,0:T(8,128)}, u32[]{:S(2)}) copy-start(f32[2,40,64]{2,1,0:T(8,128)} %param.31) | copy-start | bytes 61444
  687.5 49.4 %copy-start.57 = (f32[2,40,64]{2,1,0:T(8,128)S(1)}, f32[2,40,64]{2,1,0:T(8,128)}, u32[]{:S(2)}) copy-start(f32[2,40,64]{2,1,0:T(8,128)} %param.30) | copy-start | bytes 61444
  742.4 113.9 %copy-start.28 = (f32[2,160,320]{2,1,0:T(8,128)S(1)}, f32[2,160,320]{2,1,0:T(8,128)}, u32[]{:S(2)}) copy-start(f32[2,160,320]{2,1,0:T(8,128)} %param.35) | copy-start | bytes 1228804
  742.4 113.9 %copy-start.48 = (f32[2,160,320]{2,1,0:T(8,128)S(1)}, f32[2,160,320]{2,1,0:T(8,128)}, u32[]{:S(2)}) copy-start(f32[2,160,320]{2,1,0:T(8,128)} %param.37) | copy-start | bytes 1228804
  742.4 113.9 %copy-start.49 = (f32[2,160,320]{2,1,0:T(8,128)S(1)}, f32[2,160,320]{2,1,0:T(8,128)}, u32[]{:S(2)}) copy-start(f32[2,160,320]{2,1,0:T(8,128)} %param.36) | copy-start | bytes 1228804
  857.6 909.7 %copy-start.8 = (f32[2,40,5120]{2,1,0:T(8,128)S(1)}, f32[2,40,5120]{2,1,0:T(8,128)}, u32[]{:S(2)}) copy-start(f32[2,40,5120]{2,1,0:T(8,128)} %param.26) | copy-start | bytes 4915204
  (35 other events, 117.2 us)
Sparse Core Ops, SparseCore 0:
  10.8 50.4 all-gather.12
  64.8 127.7 all-gather.6
  196.1 159.1 all-gather.8
  357.7 49.5 reduce-scatter.7
  409.6 51.3 reduce-scatter.5
  463.0 40.3 all-gather.10
  505.5 40.3 all-gather.14
  571.0 131.8 all-reduce.5
  706.5 148.5 all-reduce.7
  861.4 357.7 reduce-scatter.9
  1221.5 545.6 reduce-scatter.11
where the time goes:
time: 1790 us; the launch traced here: 1780 us
  waiting for transfers between devices  1260 us (70%)
  matrix products  257 us (14%)
  blocking collectives  123 us (7%)
  other arithmetic  86.9 us (5%)
  local copies, waits for them, and re-layouts  39.3 us (2%)
    reduce_scatter x1, waiting for transfers between devices, on_device(): lax.psum_scatter(grad_ffn, ('dp', 'head'), scatter_dimension=1, tiled=True)  543 us
    reduce_scatter x1, waiting for transfers between devices, on_device(): lax.psum_scatter(grad_square, ('dp', 'head'), scatter_dimension=1, tiled=...  362 us
    unnamed x13, waiting for transfers between devices  108 us
    all_gather x1, waiting for transfers between devices, on_device(): lax.all_gather(rounded(perceptron_params), ('dp', 'head'), axis=1, tiled=...  93.2 us
    dot_general x12, matrix products, flipped_bilinear(): lax.dot_general(left_mat, right_mat, (((1,), (1,)), ((), ())), preferred_...  75.2 us
    dot_general x12, matrix products, bilinear_flipped(): lax.dot_general(left_mat, right_mat, (((0,), (0,)), ((), ())), preferred_...  71.9 us
    dot_general x12, matrix products, matrix_multiply(): return jnp.dot(left_mat, right_mat, preferred_element_type=jnp.float32)  68.5 us
    all_gather x1, waiting for transfers between devices, on_device(): lax.all_gather(rounded(readout_params), 'dp', axis=1, tiled=True)  48.8 us
  transfers between devices with their start and end apart: 11, of which 8 were waited for; matrix products, arithmetic and copies ran while one was open for 21% of the time, Pallas kernels for 0%

commit v1 on v0

--- a/solution.py
+++ b/solution.py
@@ -1,7 +1,331 @@
-import jax
-import jax.numpy as jnp
+import functools
+import jax, jax.numpy as jnp
 from jax import lax
+from jax.experimental import pallas as pl
+from jax.experimental.pallas import tpu as pltpu
 from jax.sharding import PartitionSpec as P
+
+MESH = pl.DeviceIdType.MESH
+ROWS = 40
+
+def place():
+    dp, hd = lax.axis_index("dp"), lax.axis_index("head")
+    return dp // 2, dp % 2, hd // 2, hd % 2
+
+def device(z, x, y, c):
+    return (z * 2 + x, y * 2 + c)
+
+def partners(z, x, y, c):
+    found = [device((z + d) % 4, x, y, c) for d in (1, 2, 3)]
+    return found + [device(z, 1 - x, y, c), device(z, x, 1 - y, c), device(z, x, y, 1 - c)]
+
+def meet(z, x, y, c):
+    barrier = pltpu.get_barrier_semaphore()
+    for partner in partners(z, x, y, c):
+        pl.semaphore_signal(barrier, inc=1, device_id=partner, device_id_type=MESH)
+    pl.semaphore_wait(barrier, 6)
+
+def gather_kernel(pieces, count, *refs):
+    shards, full = refs[:count], refs[count:2 * count]
+    own_sem, send_z, recv_z, send_b, recv_b, send_s, recv_s = refs[2 * count:]
+    z, x, y, c = place()
+    meet(z, x, y, c)
+    n = len(pieces)
+
+    def remote(src, dst, send, recv, where):
+        return pltpu.make_async_remote_copy(
+            src_ref=src, dst_ref=dst, send_sem=send, recv_sem=recv, device_id=where, device_id_type=MESH)
+
+    own, along_z, second, third, sibling = [], [], [], [], []
+    for k, (j, start, width) in enumerate(pieces):
+        cols = pl.ds(start, width)
+        first, last = pl.ds(start, width // 2), pl.ds(start + width // 2, width // 2)
+        home, shard = full[j], shards[j]
+        own.append(pltpu.make_async_copy(shard.at[:, cols], home.at[z, x, y, c, :, cols], own_sem.at[k]))
+        along_z.append([remote(shard.at[:, cols], home.at[z, x, y, c, :, cols], send_z.at[k, d - 1],
+                               recv_z.at[k, d - 1], device((z + d) % 4, x, y, c)) for d in (1, 2, 3)])
+        a, b = home.at[:, x, y, c, :, first], home.at[:, x, y, c, :, last]
+        second.append([remote(a, a, send_b.at[k, 0], recv_b.at[k, 0], device(z, x, 1 - y, c)),
+                       remote(b, b, send_b.at[k, 1], recv_b.at[k, 1], device(z, 1 - x, y, c))])
+        a, b = home.at[:, x, :, c, :, first], home.at[:, :, y, c, :, last]
+        third.append([remote(a, a, send_b.at[k, 2], recv_b.at[k, 2], device(z, 1 - x, y, c)),
+                      remote(b, b, send_b.at[k, 3], recv_b.at[k, 3], device(z, x, 1 - y, c))])
+        a = home.at[:, :, :, c, :, cols]
+        sibling.append(remote(a, a, send_s.at[k], recv_s.at[k], device(z, x, y, 1 - c)))
+    ahead = 4
+    for t in range(-ahead, n + 2):
+        k = t + ahead
+        if k < n:
+            for copy in along_z[k]:
+                copy.start()
+            own[k].start()
+        if 0 <= t < n:
+            own[t].wait()
+            for copy in along_z[t]:
+                copy.wait_recv()
+            for copy in second[t]:
+                copy.start()
+        k = t - 1
+        if 0 <= k < n:
+            for copy in second[k]:
+                copy.wait_recv()
+            for copy in third[k]:
+                copy.start()
+        k = t - 2
+        if 0 <= k < n:
+            for copy in third[k]:
+                copy.wait_recv()
+            sibling[k].start()
+    for k in range(n):
+        sibling[k].wait_recv()
+        for copy in along_z[k] + second[k] + third[k] + [sibling[k]]:
+            copy.wait_send()
+
+def gather(shards, step=1280, cid=1):
+    count = len(shards)
+    pieces = []
+    for j, shard in enumerate(shards):
+        width = shard.shape[1]
+        s = step if width % step == 0 else width
+        pieces += [(j, start, s) for start in range(0, width, s)]
+    n = len(pieces)
+    total = sum(s.shape[1] for s in shards)
+    dma = pltpu.SemaphoreType.DMA
+    full = pl.pallas_call(
+        functools.partial(gather_kernel, tuple(pieces), count),
+        out_shape=[jax.ShapeDtypeStruct((4, 2, 2, 2, ROWS, s.shape[1]), jnp.bfloat16) for s in shards],
+        in_specs=[pl.BlockSpec(memory_space=pltpu.VMEM)] * count,
+        out_specs=[pl.BlockSpec(memory_space=pl.ANY)] * count,
+        scratch_shapes=[dma((n,)), dma((n, 3)), dma((n, 3)), dma((n, 4)), dma((n, 4)), dma((n,)), dma((n,))],
+        compiler_params=pltpu.CompilerParams(collective_id=cid, has_side_effects=True),
+        name="gather_weights",
+    )(*shards)
+    return [f.reshape(32 * ROWS, f.shape[-1]) for f in full]
+
+
+RING = 3
+
+def reduce_kernel(pieces, lefts_n, rights_n, n, width, small_width, *refs):
+    lefts, rights, small = refs[:lefts_n], refs[lefts_n:lefts_n + rights_n], refs[lefts_n + rights_n]
+    refs = refs[lefts_n + rights_n + 1:]
+    out, small_out = refs[:2]
+    left_buf, right_buf, load_sem = refs[2:5]
+    main_bufs, small_bufs = refs[5:5 + 17], refs[5 + 17:5 + 34]
+    z, x, y, c = place()
+    meet(z, x, y, c)
+    f32, low = jnp.float32, jnp.bfloat16
+
+    def lane(bufs, ring, total, columns):
+        out_s, kept, in_s, in_a, in_b, sum_a, sum_b, in_c, in_d, last, in_z, s_sem, p_sem, q_sem, z_sem, credit, credit_z = bufs
+        half = columns // 2
+        front, back = pl.ds(0, half), pl.ds(half, half)
+        to_x, to_y, to_c = device(z, 1 - x, y, c), device(z, x, 1 - y, c), device(z, x, y, 1 - c)
+
+        def remote(src, dst, sems, where):
+            return pltpu.make_async_remote_copy(
+                src_ref=src, dst_ref=dst, send_sem=sems[0], recv_sem=sems[1], device_id=where, device_id_type=MESH)
+
+        def sibling(k):
+            s = k % ring
+            return remote(out_s.at[s], in_s.at[s], (s_sem.at[s, 0], s_sem.at[s, 1]), to_c)
+
+        def first(k):
+            s = k % ring
+            return (remote(kept.at[s, :, :, 1 - y, :, front], in_a.at[s], (p_sem.at[s, 0], p_sem.at[s, 1]), to_y),
+                    remote(kept.at[s, :, 1 - x, :, :, back], in_b.at[s], (p_sem.at[s, 2], p_sem.at[s, 3]), to_x))
+
+        def second(k):
+            s = k % ring
+            return (remote(sum_a.at[s, :, 1 - x], in_c.at[s], (q_sem.at[s, 0], q_sem.at[s, 1]), to_x),
+                    remote(sum_b.at[s, :, 1 - y], in_d.at[s], (q_sem.at[s, 2], q_sem.at[s, 3]), to_y))
+
+        def third(k):
+            s = k % ring
+            return tuple(remote(last.at[s, (z + d) % 4], in_z.at[s, d - 1], (z_sem.at[s, d - 1], z_sem.at[s, d + 2]),
+                                device((z + d) % 4, x, y, c)) for d in (1, 2, 3))
+
+        def give(index, k, where):
+            @pl.when(k + ring < total)
+            def _():
+                pl.semaphore_signal(credit.at[index], inc=1, device_id=where, device_id_type=MESH)
+
+        def take(ref, k):
+            @pl.when(k >= ring)
+            def _():
+                pl.semaphore_wait(ref, 1)
+
+        def reuse(k, copies):
+            @pl.when(k >= ring)
+            def _():
+                for copy in copies(k - ring):
+                    copy.wait_send()
+
+        def add(left, right):
+            return (left.astype(f32) + right.astype(f32)).astype(low)
+
+        def send_sibling(k):
+            take(credit.at[0], k)
+            sibling(k).start()
+
+        def stage_one(k):
+            s = k % ring
+            sibling(k).wait_recv()
+
+            def body(i, carry):
+                kept[s, i] = add(kept[s, i], in_s[s, i])
+                return carry
+            lax.fori_loop(0, 4, body, 0)
+            give(0, k, to_c)
+            take(credit.at[1], k)
+            take(credit.at[2], k)
+            for copy in first(k):
+                copy.start()
+
+        def stage_two(k):
+            s = k % ring
+            reuse(k, second)
+            for copy in first(k):
+                copy.wait_recv()
+
+            def body(i, carry):
+                for j in range(2):
+                    sum_a[s, i, j] = add(kept[s, i, j, y, :, :half], in_a[s, i, j])
+                    sum_b[s, i, j] = add(kept[s, i, x, j, :, half:], in_b[s, i, j])
+                return carry
+            lax.fori_loop(0, 4, body, 0)
+            give(1, k, to_y)
+            give(2, k, to_x)
+            take(credit.at[3], k)
+            take(credit.at[4], k)
+            for copy in second(k):
+                copy.start()
+
+        def stage_three(k):
+            s = k % ring
+            reuse(k, third)
+            for copy in second(k):
+                copy.wait_recv()
+
+            def body(i, carry):
+                last[s, i, :, :half] = add(sum_a[s, i, x], in_c[s, i])
+                last[s, i, :, half:] = add(sum_b[s, i, y], in_d[s, i])
+                return carry
+            lax.fori_loop(0, 4, body, 0)
+            give(3, k, to_x)
+            give(4, k, to_y)
+            for d in (1, 2, 3):
+                take(credit_z.at[d - 1], k)
+            for copy in third(k):
+                copy.start()
+
+        def stage_four(k, target):
+            s = k % ring
+            for copy in third(k):
+                copy.wait_recv()
+            value = last[s, z].astype(f32)
+            for d in (1, 2, 3):
+                value = value + in_z[s, d - 1].astype(f32)
+            target[...] = value
+            for d in (1, 2, 3):
+                @pl.when(k + ring < total)
+                def _():
+                    pl.semaphore_signal(credit_z.at[d - 1], inc=1, device_id=device((z + 4 - d) % 4, x, y, c), device_id_type=MESH)
+
+        def drain(k):
+            for copies in ((sibling(k),), first(k), second(k), third(k)):
+                for copy in copies:
+                    copy.wait_send()
+
+        def fresh(k):
+            reuse(k, lambda j: (sibling(j),) + first(j))
+
+        return fresh, send_sibling, stage_one, stage_two, stage_three, stage_four, drain
+
+    fresh, send_sibling, one, two, three, four, drain = lane(main_bufs, RING, n, width)
+    _, small_sibling, small_one, small_two, small_three, small_four, small_drain = lane(small_bufs, 1, 1, small_width)
+    out_s, kept = main_bufs[:2]
+    small_s, small_kept = small_bufs[:2]
+
+    def load(k, start):
+        for number, (i, j, begin) in enumerate(pieces):
+            @pl.when(k == number)
+            def _():
+                s = number % 2
+                for copy in (pltpu.make_async_copy(lefts[i], left_buf.at[s], load_sem.at[s, 0]),
+                             pltpu.make_async_copy(rights[j].at[:, pl.ds(begin, width)], right_buf.at[s], load_sem.at[s, 1])):
+                    copy.start() if start else copy.wait()
+
+    def multiply(k, parity, target):
+        tile = 256
+
+        def body(j, carry):
+            cols = pl.ds(pl.multiple_of(j * tile, tile), tile)
+            value = jnp.dot(left_buf[k % 2, parity], right_buf[k % 2, :, cols], preferred_element_type=f32)
+            for i in range(16):
+                target[k % RING, i // 4, (i // 2) % 2, i % 2, :, cols] = value[i * ROWS:(i + 1) * ROWS].astype(low)
+            return carry
+        lax.fori_loop(0, width // tile, body, 0)
+
+    load(0, True)
+    small_s[0] = small[1 - c]
+    small_kept[0] = small[c]
+
+    def step(t, carry):
+        @pl.when(t < n)
+        def _():
+            load(t + 1, True)
+            load(t, False)
+            fresh(t)
+            multiply(t, 1 - c, out_s)
+            send_sibling(t)
+            multiply(t, c, kept)
+        for j, work in enumerate((lambda: small_sibling(0), lambda: small_one(0), lambda: small_two(0),
+                                  lambda: small_three(0), lambda: small_four(0, small_out))):
+            @pl.when(t == j)
+            def _():
+                work()
+        for lag, work in ((1, one), (2, two), (3, three)):
+            @pl.when((t >= lag) & (t < n + lag))
+            def _():
+                work(t - lag)
+
+        @pl.when(t >= 4)
+        def _():
+            four(t - 4, out.at[t - 4])
+        return carry
+    lax.fori_loop(0, n + 4, step, 0)
+    for k in range(n - RING, n):
+        drain(k)
+    small_drain(0)
+
+def buffers(ring, columns):
+    dma, reg = pltpu.SemaphoreType.DMA, pltpu.SemaphoreType.REGULAR
+    half, low = columns // 2, jnp.bfloat16
+    block = [pltpu.VMEM((ring, 4, 2, 2, ROWS, columns), low)] * 3
+    halves = [pltpu.VMEM((ring, 4, 2, ROWS, half), low)] * 4
+    quarters = [pltpu.VMEM((ring, 4, ROWS, half), low)] * 2
+    ends = [pltpu.VMEM((ring, 4, ROWS, columns), low), pltpu.VMEM((ring, 3, ROWS, columns), low)]
+    return block + halves + quarters + ends + [dma((ring, 2)), dma((ring, 4)), dma((ring, 4)), dma((ring, 6)), reg((5,)), reg((3,))]
+
+def turned(value):
+    tokens = value.shape[0]
+    return value.T.reshape(16, 2, ROWS, tokens).swapaxes(0, 1).reshape(2, 16 * ROWS, tokens)
+
+def reduce_products(lefts, rights, pieces, small, width=1280, cid=2):
+    n = len(pieces)
+    small_width = small.shape[-1]
+    tokens = rights[0].shape[0]
+    hbm, vmem = pl.BlockSpec(memory_space=pl.ANY), pl.BlockSpec(memory_space=pltpu.VMEM)
+    return pl.pallas_call(
+        functools.partial(reduce_kernel, tuple(pieces), len(lefts), len(rights), n, width, small_width),
+        out_shape=[jax.ShapeDtypeStruct((n, ROWS, width), jnp.float32), jax.ShapeDtypeStruct((ROWS, small_width), jnp.float32)],
+        in_specs=[hbm] * (len(lefts) + len(rights)) + [vmem],
+        out_specs=[vmem, vmem],
+        scratch_shapes=[pltpu.VMEM((2, 2, 16 * ROWS, tokens), jnp.bfloat16), pltpu.VMEM((2, tokens, width), jnp.bfloat16),
+                        pltpu.SemaphoreType.DMA((2, 2))] + buffers(RING, width) + buffers(1, small_width),
+        compiler_params=pltpu.CompilerParams(collective_id=cid, has_side_effects=True, vmem_limit_bytes=60 * 1024 * 1024),
+        name="reduce_products",
+    )(*lefts, *rights, small)
 
 D = 1280
 HEADS = 16
@@ -119,6 +443,19 @@
     master_new = master - rate * (gradient + MOMENTUM * moment_new)
     average_new = AVG_DECAY * average + (1.0 - AVG_DECAY) * master_new
     return (master_new, moment_new, average_new)
+
+
+EVERYONE = ("dp", "head")
+
+
+def summed(partial):
+    return lax.psum_scatter(rounded(partial), EVERYONE, scatter_dimension=0, tiled=True).astype(
+        jnp.float32
+    )
+
+
+def owned(values):
+    return values.reshape(16, 2, ROWS, -1).swapaxes(0, 1).reshape(2, 4, 2, 2, ROWS, -1)
 
 
 def on_device(
@@ -142,136 +479,139 @@
     readout_velocity,
     readout_mean,
 ):
-    square, ffn, token, vector_low = (
-        lax.all_gather(rounded(quadratic_params), ("dp", "head"), axis=1, tiled=True),
-        lax.all_gather(rounded(perceptron_params), ("dp", "head"), axis=1, tiled=True),
-        lax.all_gather(rounded(embedder_params), ("dp", "head"), axis=1, tiled=True),
-        lax.all_gather(rounded(bias_gain_params), ("dp", "head"), axis=1, tiled=True),
-    )
-    readout_outcome = lax.all_gather(rounded(readout_params), "dp", axis=1, tiled=True)
-    vectors = vector_low.astype(jnp.float32)
+    dp_size, head_size = lax.axis_size("dp"), lax.axis_size("head")
+    low_square, low_ffn = rounded(quadratic_params), rounded(perceptron_params)
+    low_token, low_readout = rounded(embedder_params), rounded(readout_params)
+    vector_columns = jnp.pad(rounded(bias_gain_params).T, ((0, 0), (0, 123)))
+    own_readout = lax.all_to_all(low_readout, "head", split_axis=1, concat_axis=2, tiled=True)
+    adjoint = lax.all_to_all(prediction_adjoint, "head", split_axis=0, concat_axis=1, tiled=True)
+    shards = [
+        jnp.concatenate([low_square[0], low_token[0], low_token[1], vector_columns], axis=1),
+        jnp.concatenate([low_square[1], low_square[2], low_square[3]], axis=1),
+        low_square[4],
+        low_ffn[0],
+        low_ffn[1],
+        low_square[5],
+        own_readout[0],
+        own_readout[1],
+    ]
+    fast = (dp_size, head_size) == (8, 4) and input_segments.shape[0] == SEQ
+    first, qkv_w, attn_out_w, up_w, down_w, hidden_w, readout_w, shortcut_w = (
+        gather(shards) if fast else [lax.all_gather(s, EVERYONE, axis=0, tiled=True) for s in shards]
+    )
+    tok_out_w, tok_hidden_w, tok_skip_w = first[:, :D], first[:, D : D + 64], first[:, D + 64 : D + 128]
+    vectors = first[:, D + 128 : D + 133].T.astype(jnp.float32)
+
     tok_count = input_segments.shape[0]
     seq_rows = tok_count // SEQ
     mask_float = filler_flags.astype(jnp.float32)
     tok_input = rounded(jnp.concatenate([input_segments * (1.0 - mask_float), mask_float], axis=1))
-    tok_pre = flipped_bilinear(tok_input, token[0]) + vectors[2]
+    tok_pre = flipped_bilinear(tok_input, tok_hidden_w) + vectors[2]
     tok_act = rounded(jax.nn.silu(tok_pre))
     stream_in = (
-        matrix_multiply(tok_act, square[0]) + flipped_bilinear(tok_input, token[1]) + vectors[3]
+        matrix_multiply(tok_act, tok_out_w) + flipped_bilinear(tok_input, tok_skip_w) + vectors[3]
     )
     normed_one, norm_pull_one = jax.vjp(rms_gain, stream_in, vectors[0])
     normed_attn = rounded(normed_one)
     cosines, sines = rope_tables()
+    qkv = matrix_multiply(normed_attn, qkv_w)
     query_heads = rounded(
-        rotate(
-            matrix_multiply(normed_attn, square[1]).reshape(seq_rows, SEQ, HEADS, HEAD_DIM),
-            cosines,
-            sines,
-        )
+        rotate(qkv[:, :D].reshape(seq_rows, SEQ, HEADS, HEAD_DIM), cosines, sines)
     )
     key_heads = rounded(
-        rotate(
-            matrix_multiply(normed_attn, square[2]).reshape(seq_rows, SEQ, HEADS, HEAD_DIM),
-            cosines,
-            sines,
-        )
-    )
-    value_heads = rounded(matrix_multiply(normed_attn, square[3])).reshape(
-        seq_rows, SEQ, HEADS, HEAD_DIM
-    )
+        rotate(qkv[:, D : 2 * D].reshape(seq_rows, SEQ, HEADS, HEAD_DIM), cosines, sines)
+    )
+    value_heads = rounded(qkv[:, 2 * D :]).reshape(seq_rows, SEQ, HEADS, HEAD_DIM)
     seg_rows = sequence_owner.reshape(seq_rows, SEQ)
     mixed, log_totals = lax.map(attend, (query_heads, key_heads, value_heads, seg_rows))
     attn_mix = mixed.reshape(tok_count, D)
-    stream_mid = stream_in + matrix_multiply(attn_mix, square[4])
+    stream_mid = stream_in + matrix_multiply(attn_mix, attn_out_w)
     normed_two, norm_pull_two = jax.vjp(rms_gain, stream_mid, vectors[1])
     normed_ffn = rounded(normed_two)
-    ffn_pre = matrix_multiply(normed_ffn, ffn[0])
+    ffn_pre = matrix_multiply(normed_ffn, up_w)
     ffn_act = rounded(jax.nn.silu(ffn_pre))
-    stream_out = stream_mid + flipped_bilinear(ffn_act, ffn[1])
+    stream_out = stream_mid + flipped_bilinear(ffn_act, down_w)
     stream_low = rounded(stream_out)
-    head_pre = matrix_multiply(stream_low, square[5]) + vectors[4]
+    head_pre = matrix_multiply(stream_low, hidden_w) + vectors[4]
     head_act = rounded(jax.nn.silu(head_pre))
-    shortcut_complete, readout_complete = (
-        lax.all_gather(stream_low, "head", axis=0, tiled=True),
-        lax.all_gather(head_act, "head", axis=0, tiled=True),
-    )
-    prediction = (
-        matrix_multiply(readout_complete, readout_outcome[0])
-        + matrix_multiply(shortcut_complete, readout_outcome[1])
-    ).astype(jnp.bfloat16)
-    gradient_of_head = jnp.stack(
-        [
-            bilinear_flipped(readout_complete, prediction_adjoint),
-            bilinear_flipped(shortcut_complete, prediction_adjoint),
-        ]
-    )
-    grad_head_act, grad_skip = (
-        lax.psum_scatter(
-            flipped_bilinear(prediction_adjoint, readout_outcome[0]).astype(jnp.bfloat16),
-            "head",
-            scatter_dimension=0,
-            tiled=True,
-        ).astype(jnp.float32),
-        lax.psum_scatter(
-            flipped_bilinear(prediction_adjoint, readout_outcome[1]).astype(jnp.bfloat16),
-            "head",
-            scatter_dimension=0,
-            tiled=True,
-        ).astype(jnp.float32),
-    )
+    own_prediction = rounded(
+        matrix_multiply(head_act, readout_w) + matrix_multiply(stream_low, shortcut_w)
+    )
+    prediction = lax.all_to_all(own_prediction, "head", split_axis=1, concat_axis=0, tiled=True)
+
+    grad_head_act = flipped_bilinear(adjoint, readout_w)
+    grad_skip = flipped_bilinear(adjoint, shortcut_w)
     grad_head_pre = rounded(grad_head_act * silu_slope(head_pre))
     grad_bias_head = jnp.sum(grad_head_pre.astype(jnp.float32), axis=0)
-    grad_wh = bilinear_flipped(stream_low, grad_head_pre)
-    grad_stream_out = grad_skip + flipped_bilinear(grad_head_pre, square[5])
+    grad_stream_out = grad_skip + flipped_bilinear(grad_head_pre, hidden_w)
     grad_ffn_out = rounded(grad_stream_out)
-    grad_down = bilinear_flipped(grad_ffn_out, ffn_act)
-    grad_ffn_pre = rounded(matrix_multiply(grad_ffn_out, ffn[1]) * silu_slope(ffn_pre))
-    grad_up = bilinear_flipped(normed_ffn, grad_ffn_pre)
-    grad_stream_norm, grad_gain_two = norm_pull_two(flipped_bilinear(grad_ffn_pre, ffn[0]))
+    grad_ffn_pre = rounded(matrix_multiply(grad_ffn_out, down_w) * silu_slope(ffn_pre))
+    grad_stream_norm, grad_gain_two = norm_pull_two(flipped_bilinear(grad_ffn_pre, up_w))
     grad_stream_mid = grad_stream_out + grad_stream_norm
-    grad_ffn = jnp.stack([grad_up, grad_down])
     grad_attn_out = rounded(grad_stream_mid)
-    grad_wo = bilinear_flipped(attn_mix, grad_attn_out)
-    grad_attn_mix = rounded(flipped_bilinear(grad_attn_out, square[4])).reshape(
+    grad_attn_mix = rounded(flipped_bilinear(grad_attn_out, attn_out_w)).reshape(
         seq_rows, SEQ, HEADS, HEAD_DIM
     )
     grad_queries, grad_keys, grad_values = lax.map(
         attend_back, (query_heads, key_heads, value_heads, seg_rows, log_totals, grad_attn_mix)
     )
-    grad_q_pre = rounded(rotate(grad_queries, cosines, -sines).reshape(tok_count, D))
-    grad_k_pre = rounded(rotate(grad_keys, cosines, -sines).reshape(tok_count, D))
-    grad_v_pre = rounded(grad_values.reshape(tok_count, D))
-    grad_wq = bilinear_flipped(normed_attn, grad_q_pre)
-    grad_wk = bilinear_flipped(normed_attn, grad_k_pre)
-    grad_wv = bilinear_flipped(normed_attn, grad_v_pre)
-    grad_normed = (
-        flipped_bilinear(grad_q_pre, square[1])
-        + flipped_bilinear(grad_k_pre, square[2])
-        + flipped_bilinear(grad_v_pre, square[3])
-    )
+    grad_qkv_pre = jnp.concatenate(
+        [
+            rounded(rotate(grad_queries, cosines, -sines).reshape(tok_count, D)),
+            rounded(rotate(grad_keys, cosines, -sines).reshape(tok_count, D)),
+            rounded(grad_values.reshape(tok_count, D)),
+        ],
+        axis=1,
+    )
+    grad_normed = flipped_bilinear(grad_qkv_pre, qkv_w)
     grad_stream_first, grad_gain_one = norm_pull_one(grad_normed)
     grad_stream_in = grad_stream_mid + grad_stream_first
     grad_bias_out = jnp.sum(grad_stream_in, axis=0)
     grad_tok_out = rounded(grad_stream_in)
-    grad_wb = bilinear_flipped(tok_act, grad_tok_out)
     grad_skip_tok = bilinear_flipped(grad_tok_out, tok_input)
-    grad_tok_pre = rounded(flipped_bilinear(grad_tok_out, square[0]) * silu_slope(tok_pre))
+    grad_tok_pre = rounded(flipped_bilinear(grad_tok_out, tok_out_w) * silu_slope(tok_pre))
     grad_bias_tok = jnp.sum(grad_tok_pre.astype(jnp.float32), axis=0)
     grad_hidden_tok = bilinear_flipped(grad_tok_pre, tok_input)
-    grad_input = matrix_multiply(grad_tok_out, token[1]) + matrix_multiply(grad_tok_pre, token[0])
+    grad_input = matrix_multiply(grad_tok_out, tok_skip_w) + matrix_multiply(
+        grad_tok_pre, tok_hidden_w
+    )
     segment_derivative = grad_input[:, :PATCH] * (1.0 - mask_float)
-    grad_square = jnp.stack([grad_wb, grad_wq, grad_wk, grad_wv, grad_wo, grad_wh])
-    grad_token = jnp.stack([grad_hidden_tok, grad_skip_tok])
     grad_vector = jnp.stack(
-        [grad_gain_one, grad_gain_two, grad_bias_tok, grad_bias_out, grad_bias_head]
-    )
-    square_share, ffn_share, token_share, vector_share = (
-        lax.psum_scatter(grad_square, ("dp", "head"), scatter_dimension=1, tiled=True),
-        lax.psum_scatter(grad_ffn, ("dp", "head"), scatter_dimension=1, tiled=True),
-        lax.psum_scatter(grad_token, ("dp", "head"), scatter_dimension=1, tiled=True),
-        lax.psum_scatter(grad_vector, ("dp", "head"), scatter_dimension=1, tiled=True),
-    )
-    head_share = lax.psum_scatter(gradient_of_head, "dp", scatter_dimension=1, tiled=True)
+        [grad_gain_one, grad_gain_two, grad_bias_tok, grad_bias_out, grad_bias_head], axis=1
+    )
+    small = rounded(
+        jnp.concatenate([grad_hidden_tok, grad_skip_tok, jnp.pad(grad_vector, ((0, 0), (0, 123)))], axis=1)
+    )
+    wide = ffn_act.shape[1] // D
+    pieces = [(0, 0, 0), (1, 0, 0), (1, 1, 0)]
+    pieces += [(2, 2, D * j) for j in range(wide)] + [(3, 3, D * j) for j in range(wide)]
+    pieces += [(4, 4, 0)] + [(5, 5, D * j) for j in range(3)] + [(6, 6, 0)]
+    lefts = [head_act, stream_low, grad_ffn_out, normed_ffn, attn_mix, normed_attn, tok_act]
+    rights = [adjoint, grad_head_pre, ffn_act, grad_ffn_pre, grad_attn_out, grad_qkv_pre, grad_tok_out]
+    if fast:
+        shares, small_share = reduce_products([turned(v) for v in lefts], rights, pieces, owned(small))
+    else:
+        shares = [
+            summed(bilinear_flipped(lefts[i], rights[j][:, start : start + D])) for i, j, start in pieces
+        ]
+        small_share = summed(small)
+    head_share = lax.all_to_all(
+        jnp.stack([shares[0], shares[1]]), "head", split_axis=2, concat_axis=1, tiled=True
+    )
+    down_at = 3
+    up_at = down_at + wide
+    wo_at = up_at + wide
+    square_share = jnp.stack(
+        [shares[wo_at + 4], shares[wo_at + 1], shares[wo_at + 2], shares[wo_at + 3], shares[wo_at], shares[2]]
+    )
+    ffn_share = jnp.stack(
+        [
+            jnp.concatenate([shares[up_at + j] for j in range(wide)], axis=1),
+            jnp.concatenate([shares[down_at + j] for j in range(wide)], axis=1),
+        ]
+    )
+    token_share = jnp.stack([small_share[:, :64], small_share[:, 64:128]])
+    vector_share = small_share[:, 128:133].T
     all_tokens = tok_count * lax.axis_size("dp") * lax.axis_size("head")
     matrix_rate = 0.5 / (D * all_tokens) ** 0.5
     quadratic_params_fresh, quadratic_velocity_fresh, quadratic_mean_fresh = update(

time: 1790 us -> 828 us (0.46)
  waiting for transfers between devices: 1260 us -> 2.28 us
  Pallas kernels: 0 us -> 493 us
  blocking collectives: 123 us -> 0 us
  matrix products: 257 us -> 156 us
  local copies, waits for them, and re-layouts: 39.3 us -> 86 us
  other arithmetic: 86.9 us -> 57.7 us
  starting transfers between devices: 0.67 us -> 20 us
    reduce_scatter x4 -> x0, waiting for transfers between devices: 972 us -> none  [the longest x1 543 us: on_device(): lax.psum_scatter(grad_ffn, ('dp', 'head'), scatter_dimension=1, tiled=True)]
    pallas_call x0 -> x2, Pallas kernels: none -> 493 us  [the longest x1 248 us: reduce_products(): pl.pallas_call(functools.partial(reduce_kernel, tuple(pieces), len(lefts)...]
    all_gather x5 -> x0, waiting for transfers between devices: 176 us -> none  [the longest x1 93.2 us: on_device(): lax.all_gather(rounded(perceptron_params), ('dp', 'head'), axis=1, tiled=...]
    unnamed x13 -> x0, waiting for transfers between devices: 108 us -> none
    all_gather x2 -> x0, blocking collectives: 81.2 us -> none  [the longest x1 41 us: on_device(): lax.all_gather(rounded(embedder_params), ('dp', 'head'), axis=1, tiled=True)]
    dot_general x12 -> x2, matrix products: 71.9 us -> 0.7 us  [bilinear_flipped(): lax.dot_general(left_mat, right_mat, (((0,), (0,)), ((), ())), preferred_...]
    unnamed x1 -> x0, blocking collectives: 42.2 us -> none
    another operation x5, other arithmetic: 37.3 us -> 2.65 us  [the longest x1 35.3 us: on_device(): grad_ffn = jnp.stack([grad_up, grad_down])]
  transfers between devices with their start and end apart: 11 -> 4, of which waited for: 8 -> 1; matrix products, arithmetic and copies ran while one was open for 21% -> 35% of each run, Pallas kernels for 0% -> 60%
where the time goes in v1:
time: 828 us; the launch traced here: 817 us
  Pallas kernels  493 us (60%)
  matrix products  156 us (19%)
  local copies, waits for them, and re-layouts  86 us (10%)
  other arithmetic  57.7 us (7%)
  starting transfers between devices  20 us (2%)
    pallas_call x1, Pallas kernels, reduce_products(): pl.pallas_call(functools.partial(reduce_kernel, tuple(pieces), len(lefts)...  248 us
    pallas_call x1, Pallas kernels, gather(): pl.pallas_call(functools.partial(gather_kernel, tuple(pieces), count), ou...  245 us
    dot_general x10, matrix products, flipped_bilinear(): lax.dot_general(left_mat, right_mat, (((1,), (1,)), ((), ())), preferred_...  60.4 us
    dot_general x10, matrix products, matrix_multiply(): return jnp.dot(left_mat, right_mat, preferred_element_type=jnp.float32)  54 us
    convert_element_type x6, other arithmetic, rounded(): return values_in.astype(jnp.bfloat16)  20.9 us
    unnamed x173, local copies, waits for them, and re-layouts  20.3 us
  transfers between devices with their start and end apart: 4, of which 1 were waited for; matrix products, arithmetic and copies ran while one was open for 35% of the time, Pallas kernels for 60%

profile of v1, /device:TPU:0, one launch (start us, length us, event | category | flops | bytes accessed | tf_op | source)
XLA Modules:
  0.0 817.2 jit_solution(7394138047920429256)
XLA Ops:
  0.7 2.2 copy.260
  2.9 4.3 all-to-all-start
  18.7 4.3 all-to-all-start.2
  24.8 244.7 %gather_weights.1 = (bf16[4,2,2,2,40,1536]{5,4,3,2,1,0:T(8,128)(2,1)}, bf16[4,2,2,2,40,3840]{5,4,3,2,1,0:T(8,128)(2,1)}, bf16[4,2,2,2,40,1280]{5,4,3,2,1,0:T(8,1...) custom-call(bf16[40,1536]{1,0:T(8,128)(2,1)} %concatenate.61.refs_0_, ...), custom_call_target="tpu_custom_call" | custom-call | tf_op jit(solution)/shard_map/gather_weights/pallas_call | solution.py:94
  270.7 3.1 fusion.25
  273.8 2.2 fusion.13
  277.5 5.4 fusion.61
  284.1 2.6 fusion.71
  286.8 2.4 copy.205
  289.2 3.2 copy.206
  292.4 3.4 copy.207
  295.9 3.4 fusion.35
  299.3 7.5 fusion.73
  306.8 8.4 %fusion = f32[16,512]{1,0:T(8,128)S(1)} fusion(f32[16,512,512]{1,2,0:T(8,128)} %get-tuple-element.248, f32[16,512]{1,0:T(8,128)S(1)} %get-tuple-element.247), kind=kLoop, calls=%fused_computation.6 | loop fusion | flops 8380416 | bytes 16842752 | tf_op jit(solution)/shard_map/while/body/eval_jaxpr/reduce_sum | solution.py:412
  315.2 7.7 fusion.26
  325.1 16.5 %multiply_convert_fusion.2 = (bf16[512,5120]{1,0:T(8,128)(2,1)}, f32[512,5120]{1,0:T(8,128)}) fusion(bf16[1280,5120]{1,0:T(8,128)(2,1)} %bitcast.286, f32[512,1280]{1,0:T(8,128)S(1)} %get-tuple-element.250, f32[1280]{0:T(1024)S(1)} %get-tuple-element.178, f32[512]{0:T(512)S(1)} %fusion.54), kind=kOutput, calls=%fused_computation.9 | convolution fusion | flops 6725959680 | bytes 31464448 | tf_op jit(solution)/shard_map/dot_general | solution.py:343
  341.6 12.9 %fusion.11 = bf16[512,1280]{1,0:T(8,128)(2,1)S(1)} fusion(f32[512,1280]{1,0:T(8,128)S(1)} %get-tuple-element.250, bf16[512,5120]{1,0:T(8,128)(2,1)} %get-tuple-element.251.refs_9_, bf16[1280,5120]{1,0:T(8,128)(2,1)} %bitcast.288), kind=kOutput, calls=%fused_computation.31 | convolution fusion | flops 6712197120 | bytes 22282240 | tf_op jit(solution)/shard_map/dot_general | solution.py:347
  354.5 5.6 fusion.24
  375.2 7.9 all-to-all-start.1
  383.2 5.6 fusion.75
  393.8 6.9 fusion.20
  400.7 3.2 copy.212
  404.0 15.1 %multiply_convert_fusion.1.refs_10_ = bf16[512,5120]{1,0:T(8,128)(2,1)} fusion(f32[512,5120]{1,0:T(8,128)} %get-tuple-element.252, bf16[1280,5120]{1,0:T(8,128)(2,1)} %bitcast.289, f32[512,1280]{1,0:T(8,128)S(1)} %fusion.76, f32[1280,512]{0,1:T(8,128)} %copy.212), kind=kOutput, calls=%fused_computation.8 | convolution fusion | flops 6735790080 | bytes 34078720 | tf_op jit(solution)/shard_map/dot_general | solution.py:343
  419.1 14.7 %multiply_reduce_fusion.1 = (bf16[1280]{0:T(1024)(128)(2,1)S(1)}, f32[512]{0:T(512)S(1)}, f32[512,1280]{1,0:T(8,128)}) fusion(f32[512,1280]{1,0:T(8,128)} %copy-done.5, f32[512]{0:T(512)S(1)} %fusion.54, f32[1280]{0:T(1024)S(1)} %get-tuple-element.178, bf16[512,5120]{1,0:T(8,128)(2,1)} %multiply_convert_fusion.1.refs_10_, bf16[1280,5120]{1,0:T(8,128)(2,1)} %bitcast.287), kind=kOutput, calls=%fused_computation.51 | convolution fusion | flops 6714817024 | bytes 23604736 | tf_op jit(solution)/shard_map/dot_general | solution.py:347
  433.8 6.5 fusion.69
  443.9 9.6 %fusion.27 = bf16[16,80,512]{2,1,0:T(8,128)(2,1)} fusion(bf16[512,16,80]{0,2,1:T(8,128)(2,1)S(1)} %bitcast.241, f32[16,512,512]{1,2,0:T(8,128)} %get-tuple-element.248, f32[16,512]{1,0:T(8,128)S(1)} %log_add_fusion), kind=kOutput, calls=%fused_computation.74 | convolution fusion | flops 680132608 | bytes 19431424 | tf_op jit(solution)/shard_map/while/body/eval_jaxpr/hqk,qhd->khd/dot_general | solution.py:427
  453.5 11.1 %multiply_reduce_fusion = (f32[16,512]{1,0:T(8,128)S(1)}, f32[16,512,512]{1,2,0:T(8,128)}) fusion(f32[16,512,512]{1,2,0:T(8,128)} %get-tuple-element.248, f32[16,512]{1,0:T(8,128)S(1)} %log_add_fusion, bf16[512,16,80]{0,2,1:T(8,128)(2,1)S(1)} %bitcast.242, bf16[512,16,80]{0,2,1:T(8,128)(2,1)S(1)} %bitcast.250), kind=kOutput, calls=%fused_computation.1 | convolution fusion | flops 683663360 | bytes 36241408 | tf_op jit(solution)/shard_map/while/body/eval_jaxpr/qhd,khd->hqk/dot_general | solution.py:424
  464.7 12.3 %multiply_convert_fusion = bf16[16,512,512]{1,2,0:T(8,128)(2,1)S(1)} fusion(f32[16,512,512]{1,2,0:T(8,128)} %get-tuple-element.259, f32[16,512,512]{1,2,0:T(8,128)} %get-tuple-element.248, f32[16,512]{1,0:T(8,128)S(1)} %get-tuple-element.258, f32[16,512]{1,0:T(8,128)S(1)} %log_add_fusion), kind=kLoop, calls=%fused_computation | loop fusion | flops 16777216 | bytes 42008576 | tf_op jit(solution)/shard_map/while/body/eval_jaxpr/convert_element_type | solution.py:359
  478.3 4.3 multiply_bitcast_fusion
  482.6 2.5 copy.219
  485.0 2.5 subtract_convert_fusion.1
  489.4 2.6 copy.218
  492.0 2.4 copy.217
  494.5 10.3 %multiply_reduce_fusion.2 = (bf16[1280]{0:T(1024)(128)(2,1)S(1)}, f32[512]{0:T(512)S(1)}, f32[512,1280]{1,0:T(8,128)S(1)}) fusion(f32[512,1280]{1,0:T(8,128)S(1)} %copy-done.1, f32[512]{0:T(512)S(1)} %copy-done.67, f32[1280]{0:T(1024)S(1)} %copy-done.62, bf16[1280,3840]{1,0:T(8,128)(2,1)} %bitcast.290, bf16[512,1280]{1,0:T(8,128)(2,1)} %copy.219, ...), kind=kOutput, calls=%fused_computation.52 | convolution fusion | flops 5048891904 | bytes 19017216 | tf_op jit(solution)/shard_map/dot_general | solution.py:347
  508.7 2.4 fusion.74
  511.7 2.5 copy.237.refs_7_
  514.2 3.4 pad_maximum_fusion.refs_12_
  518.0 2.3 fusion.44
  523.3 2.5 copy.227
  529.9 247.9 %reduce_products.1 = (f32[16,40,1280]{2,1,0:T(8,128)}, f32[40,256]{1,0:T(8,128)}) custom-call(bf16[2,640,512]{2,1,0:T(8,128)(2,1)} %bitcast.245, bf16[2,640,512]{2,1,0:T(8,128)(2,1)} %bitcast.246, bf16[2,640,512]{2,1,0:T(8,128)(2,1)} %bitcast.251, bf16[2,640,512]{2,1,0:T(8,128)(2,1)} %bitcast.252, bf16[2,640,512]{2,1,0:T(8,128)(2,1)} %bitcast.247, ...), custom_call_target="tpu_custom_call" | custom-call | tf_op jit(solution)/shard_map/reduce_products/pallas_call | solution.py:319
  777.8 2.7 slice_bitcast_fusion.9
  782.4 2.7 multiply_add_fusion
  790.3 3.3 reshape.369
  795.2 4.1 multiply_add_fusion.2
  799.3 3.5 all-to-all-start.3
  805.5 2.6 copy.256
  808.0 2.3 all-to-all-done.3
  812.6 2.3 reshape.370
  (254 shorter events, 73.5 us)
Async XLA Ops:
  0.7 10.7 %copy-start.53 = (f32[2,40,64]{2,1,0:T(8,128)S(1)}, f32[2,40,64]{2,1,0:T(8,128)}, u32[]{:S(2)}) copy-start(f32[2,40,64]{2,1,0:T(8,128)} %param.29) | copy-start | bytes 61444
  0.7 10.8 %copy-start.6 = (f32[2,40,5120]{2,1,0:T(8,128)S(1)}, f32[2,40,5120]{2,1,0:T(8,128)}, u32[]{:S(2)}) copy-start(f32[2,40,5120]{2,1,0:T(8,128)} %param.26) | copy-start | bytes 4915204
  2.9 15.8 %all-to-all-start = ((bf16[2,160,320]{2,0,1:T(2,128)(2,1)}), bf16[2,160,320]{2,0,1:T(2,128)(2,1)S(1)}, u32[]{:S(2)}, u32[]{:S(2)}) async-start(bf16[2,160,320]{2,0,1:T(2,128)(2,1)} %copy.260), calls=%async_computation | async-start | bytes 491520 | tf_op jit(solution)/shard_map/all_to_all | solution.py:486
  11.6 5.5 copy-start.37
  11.6 5.5 copy-start.60
  11.6 5.5 copy-start.47
  11.6 6.3 copy-start.48
  13.6 282.2 %copy-start.35 = (f32[512,40]{0,1:T(8,128)}, f32[512,40]{0,1:T(8,128)S(1)}, u32[]{:S(2)}) copy-start(f32[512,40]{0,1:T(8,128)S(1)} %get-tuple-element.244) | copy-start | bytes 245764
  17.2 258.9 %copy-start.39 = (bf16[512,32]{0,1:T(8,128)(2,1)}, bf16[512,32]{0,1:T(8,128)(2,1)S(1)}, u32[]{:S(2)}) copy-start(bf16[512,32]{0,1:T(8,128)(2,1)S(1)} %multiply_convert_fusion.9) | copy-start | bytes 98308
  18.7 257.4 %copy-start.41 = (bf16[512,32]{0,1:T(8,128)(2,1)}, bf16[512,32]{0,1:T(8,128)(2,1)S(1)}, u32[]{:S(2)}) copy-start(bf16[512,32]{0,1:T(8,128)(2,1)S(1)} %convert_convert_fusion) | copy-start | bytes 98308
  18.7 356.5 %all-to-all-start.2 = ((bf16[4,512,320]{1,2,0:T(8,128)(2,1)}), bf16[4,512,320]{1,2,0:T(8,128)(2,1)}, u32[]{:S(2)}, u32[]{:S(2)}) async-start(bf16[4,512,320]{1,2,0:T(8,128)(2,1)} %bitcast.239), calls=%async_computation.2 | async-start | bytes 2621440 | tf_op jit(solution)/shard_map/all_to_all | solution.py:487
  270.7 6.2 copy-start.61
  270.7 6.2 slice-start
  276.8 6.1 copy-start.63
  276.8 46.1 %copy-start = (f32[512,1280]{1,0:T(8,128)}, f32[512,1280]{1,0:T(8,128)S(1)}, u32[]{:S(2)}) copy-start(f32[512,1280]{1,0:T(8,128)S(1)} %get-tuple-element.246) | copy-start | bytes 7864324
  276.9 6.1 copy-start.66
  299.2 7.5 copy-start.19
  299.2 7.5 copy-start.21
  299.3 7.5 copy-start.23
  299.3 7.5 copy-start.25
  306.8 8.4 %copy-start.9 = (bf16[512,1280]{0,1:T(8,128)(2,1)S(1)}, bf16[512,1280]{0,1:T(8,128)(2,1)}, u32[]{:S(2)}) copy-start(bf16[512,1280]{0,1:T(8,128)(2,1)} %copy.205) | copy-start | bytes 3932164
  315.2 7.7 copy-start.17
  325.1 16.5 %copy-start.5 = (f32[512,1280]{1,0:T(8,128)}, f32[512,1280]{1,0:T(8,128)S(1)}, u32[]{:S(2)}) copy-start(f32[512,1280]{1,0:T(8,128)S(1)} %get-tuple-element.250) | copy-start | bytes 7864324
  354.5 7.9 copy-start.33
  354.5 5.6 copy-start.73
  375.2 8.0 copy-start.77
  375.2 424.1 %all-to-all-start.1 = ((bf16[512,4,320]{0,2,1:T(8,128)(2,1)}), bf16[512,4,320]{0,2,1:T(8,128)(2,1)}, u32[]{:S(2)}, u32[]{:S(2)}) async-start(bf16[512,4,320]{0,2,1:T(8,128)(2,1)} %bitcast.31), calls=%async_computation.1 | async-start | bytes 2621440 | tf_op jit(solution)/shard_map/all_to_all | solution.py:540
  383.2 6.6 copy-start.72
  433.8 7.6 copy-start.18
  443.9 9.6 %copy-start.10 = (bf16[512,1280]{0,1:T(8,128)(2,1)S(1)}, bf16[512,1280]{0,1:T(8,128)(2,1)}, u32[]{:S(2)}) copy-start(bf16[512,1280]{0,1:T(8,128)(2,1)} %copy.205) | copy-start | bytes 3932164
  464.7 12.3 %copy-start.24 = (bf16[512,16,40]{0,2,1:T(8,128)(2,1)S(1)}, bf16[512,16,40]{0,2,1:T(8,128)(2,1)}, u32[]{:S(2)}) copy-start(bf16[512,16,40]{0,2,1:T(8,128)(2,1)} %copy-done.23) | copy-start | bytes 1966084
  464.7 12.3 %copy-start.26 = (bf16[512,16,40]{0,2,1:T(8,128)(2,1)S(1)}, bf16[512,16,40]{0,2,1:T(8,128)(2,1)}, u32[]{:S(2)}) copy-start(bf16[512,16,40]{0,2,1:T(8,128)(2,1)} %copy-done.25) | copy-start | bytes 1966084
  489.4 5.0 copy-start.62
  489.4 5.0 copy-start.67
  494.5 10.3 %copy-start.64 = (f32[512]{0:T(512)S(1)}, f32[512]{0:T(512)}, u32[]{:S(2)}) copy-start(f32[512]{0:T(512)} %copy-done.63) | copy-start | bytes 6148
  494.5 10.3 %copy-start.4 = (f32[512,1280]{1,0:T(8,128)S(1)}, f32[512,1280]{1,0:T(8,128)}, u32[]{:S(2)}) copy-start(f32[512,1280]{1,0:T(8,128)} %get-tuple-element.200) | copy-start | bytes 7864324
  785.8 7.9 copy-start.54
  785.8 9.3 %copy-start.16 = (f32[6,40,1280]{2,1,0:T(8,128)S(1)}, f32[6,40,1280]{2,1,0:T(8,128)}, u32[]{:S(2)}) copy-start(f32[6,40,1280]{2,1,0:T(8,128)} %param.23) | copy-start | bytes 3686404
  795.2 7.6 copy-start.56
  795.2 7.6 copy-start.57
  795.2 7.6 copy-start.58
  795.2 7.6 copy-start.59
  795.2 9.6 %copy-start.38 = (s32[512,32]{0,1:T(8,128)S(1)}, s32[512,32]{0,1:T(8,128)}, u32[]{:S(2)}) copy-start(s32[512,32]{0,1:T(8,128)} %param.20) | copy-start | bytes 196612
  795.2 9.6 %copy-start.51 = (f32[512,64]{0,1:T(8,128)S(1)}, f32[512,64]{0,1:T(8,128)}, u32[]{:S(2)}) copy-start(f32[512,64]{0,1:T(8,128)} %fusion.44) | copy-start | bytes 393220
  799.3 11.0 %all-to-all-start.3 = ((f32[4,1,25600]{2,1,0:T(1,128)}), f32[4,1,25600]{2,1,0:T(1,128)S(1)}, u32[]{:S(2)}, u32[]{:S(2)}) async-start(f32[4,1,25600]{2,1,0:T(1,128)} %reshape.369), calls=%async_computation.3 | async-start | bytes 819200 | tf_op jit(solution)/shard_map/all_to_all | solution.py:598
  808.0 7.5 copy-start.27
  808.0 7.5 copy-start.43
  808.0 7.5 copy-start.44
  (37 other events, 106.2 us)

commit v2 on v1

--- a/solution.py
+++ b/solution.py
@@ -376,66 +376,201 @@
     half_dim = HEAD_DIM // 2
     position = jnp.arange(SEQ, dtype=jnp.float32)[:, None]
     spacing = 10000.0 ** (-jnp.arange(half_dim, dtype=jnp.float32) / half_dim)
-    angles = position * spacing[None, :]
+    angles = (position * spacing[None, :]).T
     return (jnp.cos(angles), jnp.sin(angles))
 
 
-def rotate(heads_in, cosines, sines):
-    half_dim = heads_in.shape[-1] // 2
-    lower_half = heads_in[..., :half_dim]
-    upper_half = heads_in[..., half_dim:]
-    cos_rows = cosines[:, None, :]
-    sin_rows = sines[:, None, :]
-    return jnp.concatenate(
+def contract_rows(left_mat, right_mat):
+    return lax.dot_general(
+        left_mat, right_mat, (((0,), (0,)), ((), ())), preferred_element_type=jnp.float32
+    )
+
+
+def contract_columns(left_mat, right_mat):
+    return lax.dot_general(
+        left_mat, right_mat, (((1,), (1,)), ((), ())), preferred_element_type=jnp.float32
+    )
+
+
+def turned_head(head, cosines, sines):
+    lower, upper = head[: HEAD_DIM // 2], head[HEAD_DIM // 2 :]
+    return jnp.concatenate([lower * cosines - upper * sines, upper * cosines + lower * sines], axis=0)
+
+
+def fill_bias(bias, owner_column, owner_row):
+    @pl.when(pl.program_id(0) == 0)
+    def _():
+        keys = lax.broadcasted_iota(jnp.int32, (SEQ, SEQ), 0)
+        queries = lax.broadcasted_iota(jnp.int32, (SEQ, SEQ), 1)
+        allowed = (keys <= queries) & (owner_column[...] == owner_row[...])
+        bias[...] = jnp.where(allowed, 0.0, -1e30)
+
+
+def spread(target, block):
+    target[...] = block.astype(jnp.float32).T.reshape(target.shape)
+
+
+def gathered_heads(source):
+    return source[...].reshape(STEP_HEADS * HEAD_DIM, SEQ).T.astype(jnp.bfloat16)
+
+
+def attend_kernel(
+    query_in, key_in, value_in, cosines, sines, owner_column, owner_row, mixed, log_totals, bias, heads, outcome
+):
+    fill_bias(bias, owner_column, owner_row)
+    cos, sin = cosines[...], sines[...]
+    for i, block in enumerate((query_in, key_in, value_in)):
+        spread(heads.at[i], block[...])
+
+    def one(i):
+        query = rounded(turned_head(heads[0, i], cos, sin))
+        key = rounded(turned_head(heads[1, i], cos, sin))
+        value = rounded(heads[2, i])
+        for j in range(SEQ // TILE):
+            cols, rows = slice(j * TILE, (j + 1) * TILE), (j + 1) * TILE
+            scores = contract_rows(key[:, :rows], query[:, cols]) * HEAD_DIM ** (-0.5) + bias[:rows, cols]
+            top = jnp.max(scores, axis=0, keepdims=True)
+            expo = jnp.exp(scores - top)
+            total = jnp.sum(expo, axis=0, keepdims=True)
+            probability = rounded(expo * (1.0 / total))
+            outcome[i, :, cols] = matrix_multiply(value[:, :rows], probability)
+            log_totals[i, :, cols] = top + jnp.log(total)
+
+    def pair(i, carry):
+        one(2 * i)
+        one(2 * i + 1)
+        return carry
+
+    lax.fori_loop(0, STEP_HEADS // 2, pair, 0)
+    mixed[...] = gathered_heads(outcome)
+
+
+def attend_back_kernel(
+    query_in,
+    key_in,
+    value_in,
+    cosines,
+    sines,
+    owner_column,
+    owner_row,
+    log_totals,
+    grad_mixed,
+    grad_query_out,
+    grad_key_out,
+    grad_value_out,
+    bias,
+    heads,
+    outcome,
+):
+    fill_bias(bias, owner_column, owner_row)
+    cos, sin = cosines[...], sines[...]
+    scale = HEAD_DIM ** (-0.5)
+    for i, block in enumerate((query_in, key_in, value_in, grad_mixed)):
+        spread(heads.at[i], block[...])
+
+    def one(i):
+        query = rounded(turned_head(heads[0, i], cos, sin))
+        key = rounded(turned_head(heads[1, i], cos, sin))
+        value, grad_mix = rounded(heads[2, i]), rounded(heads[3, i])
+        grad_key, grad_value = [], []
+        for j in range(SEQ // TILE):
+            cols, rows = slice(j * TILE, (j + 1) * TILE), (j + 1) * TILE
+            scores = contract_rows(key[:, :rows], query[:, cols]) * scale + bias[:rows, cols]
+            probability = jnp.exp(scores - log_totals[i, :, cols])
+            grad_probs = contract_rows(value[:, :rows], grad_mix[:, cols])
+            inner_sum = jnp.sum(probability * grad_probs, axis=0, keepdims=True)
+            grad_scores = rounded(probability * (grad_probs - inner_sum))
+            grad_query = matrix_multiply(key[:, :rows], grad_scores) * scale
+            outcome[0, i, :, cols] = turned_head(grad_query, cos[:, cols], -sin[:, cols])
+            grad_key.append(contract_columns(query[:, cols], grad_scores))
+            grad_value.append(contract_columns(grad_mix[:, cols], rounded(probability)))
+        for j in range(SEQ // TILE):
+            cols = slice(j * TILE, (j + 1) * TILE)
+            key_part = sum(g[:, cols] for g in grad_key[j:]) * scale
+            outcome[1, i, :, cols] = turned_head(key_part, cos[:, cols], -sin[:, cols])
+            outcome[2, i, :, cols] = sum(g[:, cols] for g in grad_value[j:])
+
+    def pair(i, carry):
+        one(2 * i)
+        one(2 * i + 1)
+        return carry
+
+    lax.fori_loop(0, STEP_HEADS // 2, pair, 0)
+    for i, block in enumerate((grad_query_out, grad_key_out, grad_value_out)):
+        block[...] = gathered_heads(outcome.at[i])
+
+
+STEP_HEADS = 8
+TILE = 256
+
+
+def token_block(third=0):
+    steps = HEADS // STEP_HEADS
+    return pl.BlockSpec((SEQ, STEP_HEADS * HEAD_DIM), lambda h: (0, third * steps + h))
+
+
+def attention_specs():
+    half = pl.BlockSpec((HEAD_DIM // 2, SEQ), lambda h: (0, 0))
+    return [
+        token_block(0),
+        token_block(1),
+        token_block(2),
+        half,
+        half,
+        pl.BlockSpec((SEQ, 1), lambda h: (0, 0)),
+        pl.BlockSpec((1, SEQ), lambda h: (0, 0)),
+    ]
+
+
+def attention_call(kernel, in_specs, out_shape, out_specs, name, held, operands):
+    return pl.pallas_call(
+        kernel,
+        grid=(HEADS // STEP_HEADS,),
+        out_shape=out_shape,
+        in_specs=in_specs,
+        out_specs=out_specs,
+        scratch_shapes=[pltpu.VMEM((SEQ, SEQ), jnp.float32)]
+        + [pltpu.VMEM((*lead, STEP_HEADS, HEAD_DIM, SEQ), jnp.float32) for lead in held],
+        cost_estimate=pl.CostEstimate(
+            flops=8 * HEADS * SEQ * SEQ * HEAD_DIM,
+            bytes_accessed=20 * HEADS * HEAD_DIM * SEQ,
+            transcendentals=HEADS * SEQ * SEQ,
+        ),
+        compiler_params=pltpu.CompilerParams(vmem_limit_bytes=30 * 1024 * 1024),
+        name=name,
+    )(*operands)
+
+
+TOTALS = pl.BlockSpec((STEP_HEADS, 1, SEQ), lambda h: (h, 0, 0))
+
+
+def attend(qkv, cosines, sines, owners):
+    operands = (qkv, qkv, qkv, cosines, sines, owners[:, None], owners[None, :])
+    return attention_call(
+        attend_kernel,
+        attention_specs(),
         [
-            lower_half * cos_rows - upper_half * sin_rows,
-            upper_half * cos_rows + lower_half * sin_rows,
+            jax.ShapeDtypeStruct((SEQ, HEADS * HEAD_DIM), jnp.bfloat16),
+            jax.ShapeDtypeStruct((HEADS, 1, SEQ), jnp.float32),
         ],
-        axis=-1,
-    )
-
-
-def masked_scores(query_heads, key_heads, segments):
-    scores = jnp.einsum(
-        "qhd,khd->hqk", query_heads, key_heads, preferred_element_type=jnp.float32
-    ) * HEAD_DIM ** (-0.5)
-    places = jnp.arange(SEQ)
-    allowed = (places[:, None] >= places[None, :]) & (segments[:, None] == segments[None, :])
-    return jnp.where(allowed[None], scores, -1e30)
-
-
-def attend(bundle):
-    query_heads, key_heads, value_heads, segments = bundle
-    scores = masked_scores(query_heads, key_heads, segments)
-    row_max = jnp.max(scores, axis=-1, keepdims=True)
-    expo = jnp.exp(scores - row_max)
-    row_total = jnp.sum(expo, axis=-1, keepdims=True)
-    probability = expo / row_total
-    mixed = jnp.einsum(
-        "hqk,khd->qhd", rounded(probability), value_heads, preferred_element_type=jnp.float32
-    )
-    return (rounded(mixed), (row_max + jnp.log(row_total))[..., 0])
-
-
-def attend_back(bundle):
-    query_heads, key_heads, value_heads, segments, log_totals, grad_mixed = bundle
-    scores = masked_scores(query_heads, key_heads, segments)
-    probability = jnp.exp(scores - log_totals[..., None])
-    grad_probs = jnp.einsum(
-        "qhd,khd->hqk", grad_mixed, value_heads, preferred_element_type=jnp.float32
-    )
-    grad_values = jnp.einsum(
-        "hqk,qhd->khd", rounded(probability), grad_mixed, preferred_element_type=jnp.float32
-    )
-    inner_sum = jnp.sum(probability * grad_probs, axis=-1, keepdims=True)
-    grad_scores = rounded(probability * (grad_probs - inner_sum))
-    grad_queries = jnp.einsum(
-        "hqk,khd->qhd", grad_scores, key_heads, preferred_element_type=jnp.float32
-    ) * HEAD_DIM ** (-0.5)
-    grad_keys = jnp.einsum(
-        "hqk,qhd->khd", grad_scores, query_heads, preferred_element_type=jnp.float32
-    ) * HEAD_DIM ** (-0.5)
-    return (grad_queries, grad_keys, grad_values)
+        [token_block(), TOTALS],
+        "attend",
+        [(3,), ()],
+        operands,
+    )
+
+
+def attend_back(qkv, cosines, sines, owners, log_totals, grad_mixed):
+    operands = (qkv, qkv, qkv, cosines, sines, owners[:, None], owners[None, :], log_totals, grad_mixed)
+    return attention_call(
+        attend_back_kernel,
+        attention_specs() + [TOTALS, token_block()],
+        [jax.ShapeDtypeStruct((SEQ, HEADS * HEAD_DIM), jnp.bfloat16)] * 3,
+        [token_block()] * 3,
+        "attend_back",
+        [(4,), (3,)],
+        operands,
+    )
 
 
 def update(master, moment, average, gradient, rate):
@@ -452,6 +587,13 @@
     return lax.psum_scatter(rounded(partial), EVERYONE, scatter_dimension=0, tiled=True).astype(
         jnp.float32
     )
+
+
+def gather_in_parts(shards):
+    early = gather(shards[:6])
+    late, _ = lax.optimization_barrier((jnp.concatenate(shards[6:], axis=1), early[0]))
+    late = lax.all_gather(late, EVERYONE, axis=0, tiled=True)
+    return early + [late[:, :D], late[:, D:]]
 
 
 def owned(values):
@@ -497,7 +639,9 @@
     ]
     fast = (dp_size, head_size) == (8, 4) and input_segments.shape[0] == SEQ
     first, qkv_w, attn_out_w, up_w, down_w, hidden_w, readout_w, shortcut_w = (
-        gather(shards) if fast else [lax.all_gather(s, EVERYONE, axis=0, tiled=True) for s in shards]
+        gather_in_parts(shards)
+        if fast
+        else [lax.all_gather(s, EVERYONE, axis=0, tiled=True) for s in shards]
     )
     tok_out_w, tok_hidden_w, tok_skip_w = first[:, :D], first[:, D : D + 64], first[:, D + 64 : D + 128]
     vectors = first[:, D + 128 : D + 133].T.astype(jnp.float32)
@@ -514,17 +658,13 @@
     normed_one, norm_pull_one = jax.vjp(rms_gain, stream_in, vectors[0])
     normed_attn = rounded(normed_one)
     cosines, sines = rope_tables()
+    row_tokens = [slice(r * SEQ, (r + 1) * SEQ) for r in range(seq_rows)]
     qkv = matrix_multiply(normed_attn, qkv_w)
-    query_heads = rounded(
-        rotate(qkv[:, :D].reshape(seq_rows, SEQ, HEADS, HEAD_DIM), cosines, sines)
-    )
-    key_heads = rounded(
-        rotate(qkv[:, D : 2 * D].reshape(seq_rows, SEQ, HEADS, HEAD_DIM), cosines, sines)
-    )
-    value_heads = rounded(qkv[:, 2 * D :]).reshape(seq_rows, SEQ, HEADS, HEAD_DIM)
-    seg_rows = sequence_owner.reshape(seq_rows, SEQ)
-    mixed, log_totals = lax.map(attend, (query_heads, key_heads, value_heads, seg_rows))
-    attn_mix = mixed.reshape(tok_count, D)
+    qkv = [qkv[part] for part in row_tokens]
+    attended = [
+        attend(heads, cosines, sines, sequence_owner[part]) for heads, part in zip(qkv, row_tokens)
+    ]
+    attn_mix = jnp.concatenate([mixed for mixed, _ in attended], axis=0)
     stream_mid = stream_in + matrix_multiply(attn_mix, attn_out_w)
     normed_two, norm_pull_two = jax.vjp(rms_gain, stream_mid, vectors[1])
     normed_ffn = rounded(normed_two)
@@ -539,6 +679,13 @@
     )
     prediction = lax.all_to_all(own_prediction, "head", split_axis=1, concat_axis=0, tiled=True)
 
+    head_share = summed(
+        jnp.concatenate(
+            [rounded(bilinear_flipped(head_act, adjoint)), rounded(bilinear_flipped(stream_low, adjoint))],
+            axis=1,
+        )
+    )
+    head_share = jnp.stack([head_share[:, :D], head_share[:, D:]])
     grad_head_act = flipped_bilinear(adjoint, readout_w)
     grad_skip = flipped_bilinear(adjoint, shortcut_w)
     grad_head_pre = rounded(grad_head_act * silu_slope(head_pre))
@@ -549,21 +696,15 @@
     grad_stream_norm, grad_gain_two = norm_pull_two(flipped_bilinear(grad_ffn_pre, up_w))
     grad_stream_mid = grad_stream_out + grad_stream_norm
     grad_attn_out = rounded(grad_stream_mid)
-    grad_attn_mix = rounded(flipped_bilinear(grad_attn_out, attn_out_w)).reshape(
-        seq_rows, SEQ, HEADS, HEAD_DIM
-    )
-    grad_queries, grad_keys, grad_values = lax.map(
-        attend_back, (query_heads, key_heads, value_heads, seg_rows, log_totals, grad_attn_mix)
-    )
-    grad_qkv_pre = jnp.concatenate(
-        [
-            rounded(rotate(grad_queries, cosines, -sines).reshape(tok_count, D)),
-            rounded(rotate(grad_keys, cosines, -sines).reshape(tok_count, D)),
-            rounded(grad_values.reshape(tok_count, D)),
-        ],
-        axis=1,
-    )
-    grad_normed = flipped_bilinear(grad_qkv_pre, qkv_w)
+    grad_attn_mix = rounded(flipped_bilinear(grad_attn_out, attn_out_w))
+    grad_heads = [
+        attend_back(heads, cosines, sines, sequence_owner[part], log_totals, grad_attn_mix[part])
+        for heads, part, (_, log_totals) in zip(qkv, row_tokens, attended)
+    ]
+    grad_qkv_pre = [jnp.concatenate([heads[i] for heads in grad_heads], axis=0) for i in range(3)]
+    grad_normed = sum(
+        flipped_bilinear(grad, qkv_w[:, D * i : D * (i + 1)]) for i, grad in enumerate(grad_qkv_pre)
+    )
     grad_stream_first, grad_gain_one = norm_pull_one(grad_normed)
     grad_stream_in = grad_stream_mid + grad_stream_first
     grad_bias_out = jnp.sum(grad_stream_in, axis=0)
@@ -583,11 +724,11 @@
         jnp.concatenate([grad_hidden_tok, grad_skip_tok, jnp.pad(grad_vector, ((0, 0), (0, 123)))], axis=1)
     )
     wide = ffn_act.shape[1] // D
-    pieces = [(0, 0, 0), (1, 0, 0), (1, 1, 0)]
-    pieces += [(2, 2, D * j) for j in range(wide)] + [(3, 3, D * j) for j in range(wide)]
-    pieces += [(4, 4, 0)] + [(5, 5, D * j) for j in range(3)] + [(6, 6, 0)]
-    lefts = [head_act, stream_low, grad_ffn_out, normed_ffn, attn_mix, normed_attn, tok_act]
-    rights = [adjoint, grad_head_pre, ffn_act, grad_ffn_pre, grad_attn_out, grad_qkv_pre, grad_tok_out]
+    pieces = [(0, 0, 0)]
+    pieces += [(1, 1, D * j) for j in range(wide)] + [(2, 2, D * j) for j in range(wide)]
+    pieces += [(3, 3, 0)] + [(4, 4 + j, 0) for j in range(3)] + [(5, 7, 0)]
+    lefts = [stream_low, grad_ffn_out, normed_ffn, attn_mix, normed_attn, tok_act]
+    rights = [grad_head_pre, ffn_act, grad_ffn_pre, grad_attn_out, *grad_qkv_pre, grad_tok_out]
     if fast:
         shares, small_share = reduce_products([turned(v) for v in lefts], rights, pieces, owned(small))
     else:
@@ -596,13 +737,13 @@
         ]
         small_share = summed(small)
     head_share = lax.all_to_all(
-        jnp.stack([shares[0], shares[1]]), "head", split_axis=2, concat_axis=1, tiled=True
-    )
-    down_at = 3
+        head_share, "head", split_axis=2, concat_axis=1, tiled=True
+    )
+    down_at = 1
     up_at = down_at + wide
     wo_at = up_at + wide
     square_share = jnp.stack(
-        [shares[wo_at + 4], shares[wo_at + 1], shares[wo_at + 2], shares[wo_at + 3], shares[wo_at], shares[2]]
+        [shares[wo_at + 4], shares[wo_at + 1], shares[wo_at + 2], shares[wo_at + 3], shares[wo_at], shares[0]]
     )
     ffn_share = jnp.stack(
         [

time: 828 us -> 738 us (0.89)
  matrix products: 156 us -> 122 us
  other arithmetic: 57.7 us -> 24.3 us
  Pallas kernels: 493 us -> 477 us
  local copies, waits for them, and re-layouts: 86 us -> 71.7 us
  between operations: 2.21 us -> 15.6 us
    dot_general x6 -> x0, matrix products: 41.5 us -> none  [the longest x1 11.1 us: attend_back(): jnp.einsum('qhd,khd->hqk', grad_mixed, value_heads, preferred_element_typ...]
    pallas_call x0 -> x2, Pallas kernels: none -> 36.5 us  [attention_call(): pl.pallas_call(kernel, grid=(HEADS // STEP_HEADS,), out_shape=out_shape,...]
    pallas_call x1, Pallas kernels: 245 us -> 218 us  [gather(): pl.pallas_call(functools.partial(gather_kernel, tuple(pieces), count), ou...]
    pallas_call x1, Pallas kernels: 248 us -> 223 us  [reduce_products(): pl.pallas_call(functools.partial(reduce_kernel, tuple(pieces), len(lefts)...]
    slice x6 -> x1, local copies, waits for them, and re-layouts: 13 us -> 0.09 us  [on_device(): own_readout[0]]
    convert_element_type x6 -> x5, other arithmetic: 20.9 us -> 8.23 us  [rounded(): return values_in.astype(jnp.bfloat16)]
    unnamed x173 -> x165, local copies, waits for them, and re-layouts: 20.3 us -> 31.2 us
    reduce_sum x1 -> x0, other arithmetic: 8.37 us -> none  [attend(): row_total = jnp.sum(expo, axis=-1, keepdims=True)]
  transfers between devices with their start and end apart: 4 -> 6, of which waited for: 1 -> 1; matrix products, arithmetic and copies ran while one was open for 35% -> 27% of each run, Pallas kernels for 60% -> 65%
where the time goes in v2:
time: 738 us; the launch traced here: 734 us
  Pallas kernels  477 us (65%)
  matrix products  122 us (17%)
  local copies, waits for them, and re-layouts  71.7 us (10%)
  other arithmetic  24.3 us (3%)
  starting transfers between devices  20.8 us (3%)
  between operations  15.6 us (2%)
    pallas_call x1, Pallas kernels, reduce_products(): pl.pallas_call(functools.partial(reduce_kernel, tuple(pieces), len(lefts)...  223 us
    pallas_call x1, Pallas kernels, gather(): pl.pallas_call(functools.partial(gather_kernel, tuple(pieces), count), ou...  218 us
    dot_general x12, matrix products, flipped_bilinear(): lax.dot_general(left_mat, right_mat, (((1,), (1,)), ((), ())), preferred_...  60.4 us
    dot_general x10, matrix products, matrix_multiply(): return jnp.dot(left_mat, right_mat, preferred_element_type=jnp.float32)  53.8 us
    pallas_call x2, Pallas kernels, attention_call(): pl.pallas_call(kernel, grid=(HEADS // STEP_HEADS,), out_shape=out_shape,...  36.5 us
    unnamed x165, local copies, waits for them, and re-layouts  31.2 us
  transfers between devices with their start and end apart: 6, of which 1 were waited for; matrix products, arithmetic and copies ran while one was open for 27% of the time, Pallas kernels for 65%

profile of v2, /device:TPU:0, one launch (start us, length us, event | category | flops | bytes accessed | tf_op | source)
XLA Modules:
  0.0 733.6 jit_solution(3223165608255115714)
XLA Ops:
  7.2 2.2 copy.233
  9.5 4.3 all-to-all-start
  18.5 218.0 %gather_weights.1 = (bf16[4,2,2,2,40,1536]{5,4,3,2,1,0:T(8,128)(2,1)}, bf16[4,2,2,2,40,3840]{5,4,3,2,1,0:T(8,128)(2,1)}, bf16[4,2,2,2,40,1280]{5,4,3,2,1,0:T(8,1...) custom-call(bf16[40,1536]{1,0:T(8,128)(2,1)} %concatenate.34.refs_0_, ...), custom_call_target="tpu_custom_call" | custom-call | tf_op jit(solution)/shard_map/gather_weights/pallas_call | solution.py:94
  239.1 7.4 %all-to-all-start.2 = ((bf16[4,512,320]{1,2,0:T(8,128)(2,1)}), bf16[4,512,320]{1,2,0:T(8,128)(2,1)}, u32[]{:S(2)}, u32[]{:S(2)}) async-start(bf16[4,512,320]{1,2,0:T(8,128)(2,1)} %bitcast.193), calls=%async_computation.2 | async-start | bytes 2621440 | tf_op jit(solution)/shard_map/all_to_all | solution.py:629
  248.4 3.1 fusion.25
  251.5 2.2 fusion.17
  255.2 5.4 fusion.45.query_in.key_in.value_in
  260.6 15.5 %attend.1 = (bf16[512,1280]{1,0:T(8,128)(2,1)S(1)}, f32[16,1,512]{2,1,0:T(1,128)S(1)}) custom-call(f32[512,3840]{1,0:T(8,128)S(1)} %fusion.45.query_in.key_in.value_in, f32[512,3840]{1,0:T(8,128)S(1)} %fusion.45.query_in.key_in.value_in, f32[512,3840]{1,0:T(8,128)S(1)} %fusion.45.query_in.key_in.value_in, f32[40,512]{1,0:T(8,128)S(1)} %get-tuple-element.205.cosines, ...), custom_call_target="tpu_custom_call" | custom-call | flops 2684354560 | bytes 13107200 | tf_op jit(solution)/shard_map/attend/pallas_call | solution.py:526
  276.1 4.0 multiply_reduce_fusion.4
  280.2 11.6 %multiply_convert_fusion.1 = (bf16[512,5120]{1,0:T(8,128)(2,1)}, f32[512,5120]{1,0:T(8,128)}) fusion(bf16[1280,5120]{1,0:T(8,128)(2,1)S(1)} %bitcast.234, f32[512,1280]{1,0:T(8,128)S(1)} %get-tuple-element.209, f32[1280]{0:T(1024)S(1)} %get-tuple-element.152, f32[512]{0:T(512)S(1)} %fusion.42), kind=kOutput, calls=%fused_computation.1 | convolution fusion | flops 6725959680 | bytes 31464448 | tf_op jit(solution)/shard_map/dot_general | solution.py:343
  291.8 13.6 %fusion.9 = bf16[512,1280]{1,0:T(8,128)(2,1)} fusion(f32[512,1280]{1,0:T(8,128)S(1)} %get-tuple-element.209, bf16[512,5120]{1,0:T(8,128)(2,1)} %get-tuple-element.210.refs_7_, bf16[1280,5120]{1,0:T(8,128)(2,1)} %bitcast.235), kind=kOutput, calls=%fused_computation.28 | convolution fusion | flops 6712197120 | bytes 22282240 | tf_op jit(solution)/shard_map/dot_general | solution.py:347
  306.1 1.6 copy.197
  310.6 1.9 copy.207
  315.1 5.3 convolution_add_fusion.6
  320.4 3.4 convolution_convert_fusion
  323.9 3.3 convolution_convert_fusion.1
  327.2 3.1 pad_maximum_fusion
  330.3 9.5 %copy.224 = bf16[1280,2560]{1,0:T(8,128)(2,1)} copy(bf16[1280,2560]{0,1:T(8,128)(2,1)} %pad_maximum_fusion) | data formatting | bytes 13107200
  339.9 5.1 fusion.14
  345.0 1.9 fusion.7
  348.3 5.1 all-to-all-start.1
  353.4 5.0 fusion.56
  359.5 1.9 fusion.57
  361.4 2.1 copy.199
  363.5 6.9 fusion.24
  370.4 3.2 copy.195
  373.6 15.3 %multiply_convert_fusion.refs_8_ = bf16[512,5120]{1,0:T(8,128)(2,1)} fusion(f32[512,5120]{1,0:T(8,128)} %get-tuple-element.211, bf16[1280,5120]{1,0:T(8,128)(2,1)} %bitcast.236, f32[512,1280]{1,0:T(8,128)S(1)} %fusion.57, f32[1280,512]{0,1:T(8,128)} %copy.195), kind=kOutput, calls=%fused_computation | convolution fusion | flops 6735790080 | bytes 34078720 | tf_op jit(solution)/shard_map/dot_general | solution.py:343
  390.1 14.8 %multiply_reduce_fusion = (bf16[1280]{0:T(1024)(128)(2,1)S(1)}, f32[512]{0:T(512)S(1)}, f32[512,1280]{1,0:T(8,128)}) fusion(f32[512,1280]{1,0:T(8,128)} %copy-done.21, f32[512]{0:T(512)S(1)} %fusion.42, f32[1280]{0:T(1024)S(1)} %get-tuple-element.152, bf16[512,5120]{1,0:T(8,128)(2,1)} %multiply_convert_fusion.refs_8_, bf16[1280,5120]{1,0:T(8,128)(2,1)} %bitcast.231), kind=kOutput, calls=%fused_computation.48 | convolution fusion | flops 6714817024 | bytes 23604736 | tf_op jit(solution)/shard_map/dot_general | solution.py:347
  405.0 6.8 fusion.52
  411.8 1.7 copy.201
  414.8 4.0 convolution_convert_fusion.2.grad_mixed
  418.8 3.3 copy-done.1
  422.1 21.1 %attend_back.1 = (bf16[512,1280]{1,0:T(8,128)(2,1)S(1)}, bf16[512,1280]{1,0:T(8,128)(2,1)S(1)}, bf16[512,1280]{1,0:T(8,128)(2,1)S(1)}) custom-call(f32[512,3840]{1,0:T(8,128)S(1)} %copy-done.1, f32[512,3840]{1,0:T(8,128)S(1)} %copy-done.1, f32[512,3840]{1,0:T(8,128)S(1)} %copy-done.1, f32[40,512]{1,0:T(8,128)S(1)} %copy-done.8, f32[40,512]{1,0:T(8,128)S(1)} %copy-done.6, ...), custom_call_target="tpu_custom_call" | custom-call | flops 2684354560 | bytes 13107200 | tf_op jit(solution)/shard_map/attend_back/pallas_call | solution.py:526
  443.2 1.9 fusion.3
  445.2 1.9 convolution_add_fusion.4
  447.2 2.4 multiply_reduce_fusion.1
  452.2 2.6 copy.206
  454.9 4.3 fusion.55
  462.0 222.7 %reduce_products.1 = (f32[14,40,1280]{2,1,0:T(8,128)}, f32[40,256]{1,0:T(8,128)}) custom-call(bf16[2,640,512]{2,1,0:T(8,128)(2,1)} %bitcast.200, bf16[2,640,512]{2,1,0:T(8,128)(2,1)} %bitcast.203, bf16[2,640,512]{2,1,0:T(8,128)(2,1)} %bitcast.204, bf16[2,640,512]{2,1,0:T(8,128)(2,1)} %bitcast.201, bf16[2,640,512]{2,1,0:T(8,128)(2,1)} %bitcast.205, ...), custom_call_target="tpu_custom_call" | custom-call | tf_op jit(solution)/shard_map/reduce_products/pallas_call | solution.py:319
  692.1 2.3 multiply_add_fusion.2
  695.9 2.7 multiply_add_fusion
  700.9 4.8 copy.237
  705.7 3.3 reshape.180
  709.0 3.5 all-to-all-start.3
  715.2 2.6 copy.229
  717.7 2.3 all-to-all-done.3
  720.5 1.8 reduce.14
  722.3 2.3 reshape.181
  (239 shorter events, 43.2 us)
Async XLA Ops:
  7.2 8.6 %copy-start.40 = (f32[2,40,64]{2,1,0:T(8,128)S(1)}, f32[2,40,64]{2,1,0:T(8,128)}, u32[]{:S(2)}) copy-start(f32[2,40,64]{2,1,0:T(8,128)} %param.29) | copy-start | bytes 61444
  7.2 8.6 %copy-start.53 = (f32[5,40]{1,0:T(8,128)S(1)}, f32[5,40]{1,0:T(8,128)}, u32[]{:S(2)}) copy-start(f32[5,40]{1,0:T(8,128)} %param.32) | copy-start | bytes 2404
  7.2 8.7 %copy-start.16 = (f32[2,40,5120]{2,1,0:T(8,128)S(1)}, f32[2,40,5120]{2,1,0:T(8,128)}, u32[]{:S(2)}) copy-start(f32[2,40,5120]{2,1,0:T(8,128)} %param.26) | copy-start | bytes 4915204
  9.5 229.7 %all-to-all-start = ((bf16[2,160,320]{2,0,1:T(2,128)(2,1)}), bf16[2,160,320]{2,0,1:T(2,128)(2,1)S(1)}, u32[]{:S(2)}, u32[]{:S(2)}) async-start(bf16[2,160,320]{2,0,1:T(2,128)(2,1)} %copy.233), calls=%async_computation | async-start | bytes 491520 | tf_op jit(solution)/shard_map/all_to_all | solution.py:628
  16.0 221.7 %copy-start.9 = (s32[512]{0:T(512)S(1)}, s32[512]{0:T(512)}, u32[]{:S(2)}) copy-start(s32[512]{0:T(512)} %param.21) | copy-start | bytes 6148
  16.0 221.8 %copy-start.26 = (bf16[2048,320]{0,1:T(8,128)(2,1)S(1)}, bf16[2048,320]{0,1:T(8,128)(2,1)}, u32[]{:S(2)}) copy-start(bf16[2048,320]{0,1:T(8,128)(2,1)} %param.22) | copy-start | bytes 3932164
  239.0 9.3 %copy-start.31 = (s32[512,32]{0,1:T(8,128)S(1)}, s32[512,32]{0,1:T(8,128)}, u32[]{:S(2)}) copy-start(s32[512,32]{0,1:T(8,128)} %param.20) | copy-start | bytes 196612
  239.0 9.3 %copy-start.46 = (f32[512,32]{0,1:T(8,128)S(1)}, f32[512,32]{0,1:T(8,128)}, u32[]{:S(2)}) copy-start(f32[512,32]{0,1:T(8,128)} %param.19) | copy-start | bytes 196612
  239.1 15.8 %copy-start.49 = (f32[1280]{0:T(1024)}, f32[1280]{0:T(1024)S(1)}, u32[]{:S(2)}) copy-start(f32[1280]{0:T(1024)S(1)} %get-tuple-element.153) | copy-start | bytes 15364
  239.1 81.3 %all-to-all-start.2 = ((bf16[4,512,320]{1,2,0:T(8,128)(2,1)}), bf16[4,512,320]{1,2,0:T(8,128)(2,1)}, u32[]{:S(2)}, u32[]{:S(2)}) async-start(bf16[4,512,320]{1,2,0:T(8,128)(2,1)} %bitcast.193), calls=%async_computation.2 | async-start | bytes 2621440 | tf_op jit(solution)/shard_map/all_to_all | solution.py:629
  246.5 93.4 %all-gather.2.cloned.1.call-start = ((), (), s32[]{:S(2)}) async-start(), calls=%async_computation.5 | async-start | bytes 6758400 | tf_op jit(solution)/shard_map/all_gather | solution.py:595
  247.7 451.6 %reduce-scatter.4.cloned.1.call-start = ((), (), s32[]{:S(2)}) async-start(), calls=%async_computation.6 | async-start | bytes 6758400
  248.3 5.4 copy-start.33
  248.3 5.4 copy-start.35
  248.4 6.6 slice-start.4
  254.5 6.1 copy-start.51
  254.5 21.6 %copy-start.13 = (f32[512,1280]{1,0:T(8,128)}, f32[512,1280]{1,0:T(8,128)S(1)}, u32[]{:S(2)}) copy-start(f32[512,1280]{1,0:T(8,128)S(1)} %get-tuple-element.207) | copy-start | bytes 7864324
  254.5 6.1 copy-start.54
  254.9 5.7 copy-start.5
  254.9 5.7 copy-start.7
  260.6 15.5 %copy-start = (f32[512,3840]{1,0:T(8,128)}, f32[512,3840]{1,0:T(8,128)S(1)}, u32[]{:S(2)}) copy-start(f32[512,3840]{1,0:T(8,128)S(1)} %fusion.45.query_in.key_in.value_in) | copy-start | bytes 23592964
  260.6 19.6 %slice-start = ((s8[13107200]{0:T(1024)(128)(4,1)}), s8[4194304]{0:T(1024)(128)(4,1)S(1)}, s32[]{:S(2)}) async-start(s8[13107200]{0:T(1024)(128)(4,1)} %bitcast.232), calls=%async_computation.7 | async-start | bytes 8388608
  260.6 19.6 %slice-start.1 = ((s8[13107200]{0:T(1024)(128)(4,1)}), s8[4194304]{0:T(1024)(128)(4,1)S(1)}, s32[]{:S(2)}) async-start(s8[13107200]{0:T(1024)(128)(4,1)} %bitcast.232), calls=%async_computation.8 | async-start | bytes 8388608
  260.6 19.6 %slice-start.2 = ((s8[13107200]{0:T(1024)(128)(4,1)}), s8[4194304]{0:T(1024)(128)(4,1)S(1)}, s32[]{:S(2)}) async-start(s8[13107200]{0:T(1024)(128)(4,1)} %bitcast.232), calls=%async_computation.9 | async-start | bytes 8388608
  280.1 11.7 %copy-start.56 = (f32[512]{0:T(512)}, f32[512]{0:T(512)S(1)}, u32[]{:S(2)}) copy-start(f32[512]{0:T(512)S(1)} %get-tuple-element.208) | copy-start | bytes 6148
  280.1 11.7 %copy-start.21 = (f32[512,1280]{1,0:T(8,128)}, f32[512,1280]{1,0:T(8,128)S(1)}, u32[]{:S(2)}) copy-start(f32[512,1280]{1,0:T(8,128)S(1)} %get-tuple-element.209) | copy-start | bytes 7864324
  339.9 5.1 copy-start.60
  348.3 5.1 copy-start.63
  348.3 360.7 %all-to-all-start.1 = ((bf16[512,4,320]{0,2,1:T(8,128)(2,1)}), bf16[512,4,320]{0,2,1:T(8,128)(2,1)}, u32[]{:S(2)}, u32[]{:S(2)}) async-start(bf16[512,4,320]{0,2,1:T(8,128)(2,1)} %bitcast.22), calls=%async_computation.1 | async-start | bytes 2621440 | tf_op jit(solution)/shard_map/all_to_all | solution.py:680
  353.4 6.1 copy-start.61
  373.6 15.3 %copy-start.28 = (bf16[1280,512]{1,0:T(8,128)(2,1)S(1)}, bf16[1280,512]{1,0:T(8,128)(2,1)}, u32[]{:S(2)}) copy-start(bf16[1280,512]{1,0:T(8,128)(2,1)} %get-tuple-element.212) | copy-start | bytes 3932164
  390.1 14.8 %copy-start.57 = (f32[512]{0:T(512)S(1)}, f32[512]{0:T(512)}, u32[]{:S(2)}) copy-start(f32[512]{0:T(512)} %copy-done.56) | copy-start | bytes 6148
  414.8 28.4 %slice-start.7 = ((s8[9830400]{0:T(1024)(128)(4,1)}), s8[4194304]{0:T(1024)(128)(4,1)S(1)}, s32[]{:S(2)}) async-start(s8[9830400]{0:T(1024)(128)(4,1)} %bitcast.240), calls=%async_computation.14 | async-start | bytes 8388608
  422.1 21.1 %slice-start.8 = ((s8[9830400]{0:T(1024)(128)(4,1)}), s8[4194304]{0:T(1024)(128)(4,1)S(1)}, s32[]{:S(2)}) async-start(s8[9830400]{0:T(1024)(128)(4,1)} %bitcast.240), calls=%async_computation.15 | async-start | bytes 8388608
  422.1 21.1 %slice-start.9 = ((s8[9830400]{0:T(1024)(128)(4,1)}), s8[1441792]{0:T(1024)(128)(4,1)S(1)}, s32[]{:S(2)}) async-start(s8[9830400]{0:T(1024)(128)(4,1)} %bitcast.240), calls=%async_computation.16 | async-start | bytes 2883584
  450.7 8.9 %copy-start.11 = (bf16[512,1280]{1,0:T(8,128)(2,1)}, bf16[512,1280]{1,0:T(8,128)(2,1)S(1)}, u32[]{:S(2)}) copy-start(bf16[512,1280]{1,0:T(8,128)(2,1)S(1)} %get-tuple-element.172.refs_13_) | copy-start | bytes 3932164
  454.9 4.7 copy-start.34
  454.9 4.7 copy-start.36
  684.7 5.4 copy-start.20
  700.8 11.6 %copy-start.42 = (f32[40,256]{1,0:T(8,128)S(1)}, f32[40,256]{1,0:T(8,128)}, u32[]{:S(2)}) copy-start(f32[40,256]{1,0:T(8,128)} %get-tuple-element.44) | copy-start | bytes 122884
  700.8 11.6 %copy-start.43 = (f32[5,40]{0,1:T(8,128)S(1)}, f32[5,40]{0,1:T(8,128)}, u32[]{:S(2)}) copy-start(f32[5,40]{0,1:T(8,128)} %copy.216) | copy-start | bytes 2404
  700.8 11.6 %copy-start.44 = (f32[5,40]{0,1:T(8,128)S(1)}, f32[5,40]{0,1:T(8,128)}, u32[]{:S(2)}) copy-start(f32[5,40]{0,1:T(8,128)} %copy.217) | copy-start | bytes 2404
  700.9 11.6 %copy-start.45 = (f32[5,40]{0,1:T(8,128)S(1)}, f32[5,40]{0,1:T(8,128)}, u32[]{:S(2)}) copy-start(f32[5,40]{0,1:T(8,128)} %copy.213) | copy-start | bytes 2404
  700.9 13.7 %copy-start.32 = (s32[512,32]{0,1:T(8,128)S(1)}, s32[512,32]{0,1:T(8,128)}, u32[]{:S(2)}) copy-start(s32[512,32]{0,1:T(8,128)} %param.20) | copy-start | bytes 196612
  709.0 11.0 %all-to-all-start.3 = ((f32[4,1,25600]{2,1,0:T(1,128)}), f32[4,1,25600]{2,1,0:T(1,128)S(1)}, u32[]{:S(2)}, u32[]{:S(2)}) async-start(f32[4,1,25600]{2,1,0:T(1,128)} %reshape.180), calls=%async_computation.3 | async-start | bytes 819200 | tf_op jit(solution)/shard_map/all_to_all | solution.py:739
  717.7 7.5 %copy-start.22 = (f32[2,160,320]{2,1,0:T(8,128)S(1)}, f32[2,160,320]{2,1,0:T(8,128)}, u32[]{:S(2)}) copy-start(f32[2,160,320]{2,1,0:T(8,128)} %param.35) | copy-start | bytes 1228804
  717.7 7.5 %copy-start.37 = (f32[2,160,320]{2,1,0:T(8,128)S(1)}, f32[2,160,320]{2,1,0:T(8,128)}, u32[]{:S(2)}) copy-start(f32[2,160,320]{2,1,0:T(8,128)} %param.37) | copy-start | bytes 1228804
  717.7 7.5 %copy-start.38 = (f32[2,160,320]{2,1,0:T(8,128)S(1)}, f32[2,160,320]{2,1,0:T(8,128)}, u32[]{:S(2)}) copy-start(f32[2,160,320]{2,1,0:T(8,128)} %param.36) | copy-start | bytes 1228804
  (34 other events, 98.1 us)
Sparse Core Ops, SparseCore 0:
  250.8 74.0 all-gather.1
  340.0 152.2 reduce-scatter.3

commit v3 on v2

--- a/solution.py
+++ b/solution.py
@@ -25,41 +25,117 @@
         pl.semaphore_signal(barrier, inc=1, device_id=partner, device_id_type=MESH)
     pl.semaphore_wait(barrier, 6)
 
-def gather_kernel(pieces, count, *refs):
-    shards, full = refs[:count], refs[count:2 * count]
-    own_sem, send_z, recv_z, send_b, recv_b, send_s, recv_s = refs[2 * count:]
+def gather_kernel(early, late, count, *refs):
+    shards, full = refs[:count], refs[count : 2 * count]
+    own_sem, z_sem, b_sem, s_sem, own_late, b_late, hop_sem, s_late = refs[2 * count :]
     z, x, y, c = place()
     meet(z, x, y, c)
-    n = len(pieces)
-
-    def remote(src, dst, send, recv, where):
+    n, m = len(early), len(late)
+    to_x, to_y, to_c = device(z, 1 - x, y, c), device(z, x, 1 - y, c), device(z, x, y, 1 - c)
+
+    def remote(src, dst, sems, where):
         return pltpu.make_async_remote_copy(
-            src_ref=src, dst_ref=dst, send_sem=send, recv_sem=recv, device_id=where, device_id_type=MESH)
+            src_ref=src, dst_ref=dst, send_sem=sems[0], recv_sem=sems[1], device_id=where, device_id_type=MESH
+        )
+
+    def pair(sems, k, i):
+        return sems.at[k, 2 * i], sems.at[k, 2 * i + 1]
+
+    def halves(piece):
+        _, start, width = piece
+        return pl.ds(start, width), pl.ds(start, width // 2), pl.ds(start + width // 2, width // 2)
 
     own, along_z, second, third, sibling = [], [], [], [], []
-    for k, (j, start, width) in enumerate(pieces):
-        cols = pl.ds(start, width)
-        first, last = pl.ds(start, width // 2), pl.ds(start + width // 2, width // 2)
-        home, shard = full[j], shards[j]
+    for k, piece in enumerate(early):
+        cols, front, back = halves(piece)
+        home, shard = full[piece[0]], shards[piece[0]]
         own.append(pltpu.make_async_copy(shard.at[:, cols], home.at[z, x, y, c, :, cols], own_sem.at[k]))
-        along_z.append([remote(shard.at[:, cols], home.at[z, x, y, c, :, cols], send_z.at[k, d - 1],
-                               recv_z.at[k, d - 1], device((z + d) % 4, x, y, c)) for d in (1, 2, 3)])
-        a, b = home.at[:, x, y, c, :, first], home.at[:, x, y, c, :, last]
-        second.append([remote(a, a, send_b.at[k, 0], recv_b.at[k, 0], device(z, x, 1 - y, c)),
-                       remote(b, b, send_b.at[k, 1], recv_b.at[k, 1], device(z, 1 - x, y, c))])
-        a, b = home.at[:, x, :, c, :, first], home.at[:, :, y, c, :, last]
-        third.append([remote(a, a, send_b.at[k, 2], recv_b.at[k, 2], device(z, 1 - x, y, c)),
-                      remote(b, b, send_b.at[k, 3], recv_b.at[k, 3], device(z, x, 1 - y, c))])
+        along_z.append(
+            [
+                remote(
+                    shard.at[:, cols],
+                    home.at[z, x, y, c, :, cols],
+                    pair(z_sem, k, d - 1),
+                    device((z + d) % 4, x, y, c),
+                )
+                for d in (1, 2, 3)
+            ]
+        )
+        a, b = home.at[:, x, y, c, :, front], home.at[:, x, y, c, :, back]
+        second.append([remote(a, a, pair(b_sem, k, 0), to_y), remote(b, b, pair(b_sem, k, 1), to_x)])
+        a, b = home.at[:, x, :, c, :, front], home.at[:, :, y, c, :, back]
+        third.append([remote(a, a, pair(b_sem, k, 2), to_x), remote(b, b, pair(b_sem, k, 3), to_y)])
         a = home.at[:, :, :, c, :, cols]
-        sibling.append(remote(a, a, send_s.at[k], recv_s.at[k], device(z, x, y, 1 - c)))
-    ahead = 4
-    for t in range(-ahead, n + 2):
-        k = t + ahead
+        sibling.append(remote(a, a, pair(s_sem, k, 0), to_c))
+
+    own_q, first_q, second_q, sibling_q = [], [], [], []
+    for k, piece in enumerate(late):
+        cols, front, back = halves(piece)
+        home, shard = full[piece[0]], shards[piece[0]]
+        own_q.append(pltpu.make_async_copy(shard.at[:, cols], home.at[z, x, y, c, :, cols], own_late.at[k]))
+        first_q.append(
+            [
+                remote(shard.at[:, front], home.at[z, x, y, c, :, front], pair(b_late, k, 0), to_x),
+                remote(shard.at[:, back], home.at[z, x, y, c, :, back], pair(b_late, k, 1), to_y),
+            ]
+        )
+        a, b = home.at[z, :, y, c, :, front], home.at[z, x, :, c, :, back]
+        second_q.append([remote(a, a, pair(b_late, k, 2), to_y), remote(b, b, pair(b_late, k, 3), to_x)])
+        a = home.at[:, :, :, c, :, cols]
+        sibling_q.append(remote(a, a, pair(s_late, k, 0), to_c))
+
+    def hop(k, h, work):
+        cols = halves(late[k])[0]
+        home = full[late[k][0]]
+
+        def copy(plane, direction, where):
+            a = home.at[plane, :, :, c, :, cols]
+            return remote(a, a, pair(hop_sem, k, 2 * h + direction), where)
+
+        if work == "recv":
+            cases = [(z >= h + 1, z - 1 - h, 0, (z + 3) % 4), (z <= 2 - h, z + 1 + h, 1, (z + 1) % 4)]
+        else:
+            cases = [((z <= 2) & (z >= h), z - h, 0, (z + 1) % 4), ((z >= 1) & (z <= 3 - h), z + h, 1, (z + 3) % 4)]
+        for taken, plane, direction, other in cases:
+
+            @pl.when(taken)
+            def _():
+                made = copy(plane, direction, device(other, x, y, c))
+                if work == "recv":
+                    made.wait_recv()
+                elif work == "start":
+                    made.start()
+                else:
+                    made.wait_send()
+
+    ahead = 2
+
+    def start_z(k):
         if k < n:
             for copy in along_z[k]:
                 copy.start()
             own[k].start()
-        if 0 <= t < n:
+
+    for k in range(ahead):
+        start_z(k)
+    for k in range(m):
+        own_q[k].start()
+        for copy in first_q[k]:
+            copy.start()
+    for k in range(m):
+        own_q[k].wait()
+        for copy in first_q[k]:
+            copy.wait_recv()
+        for copy in second_q[k]:
+            copy.start()
+    hops = {}
+    for k in range(m):
+        begin = (3 * k) // 2
+        for h in range(4):
+            hops.setdefault(begin + 2 * h, []).append((k, h))
+    for t in range(max(n + 2, max(hops) + 1)):
+        start_z(t + ahead)
+        if t < n:
             own[t].wait()
             for copy in along_z[t]:
                 copy.wait_recv()
@@ -71,36 +147,57 @@
                 copy.wait_recv()
             for copy in third[k]:
                 copy.start()
+        for k, h in hops.get(t, []):
+            if h == 0:
+                for copy in second_q[k]:
+                    copy.wait_recv()
+            else:
+                hop(k, h - 1, "recv")
+            if h < 3:
+                hop(k, h, "start")
+            else:
+                sibling_q[k].start()
         k = t - 2
         if 0 <= k < n:
             for copy in third[k]:
                 copy.wait_recv()
             sibling[k].start()
+    for k in range(m):
+        sibling_q[k].wait_recv()
+        for copy in first_q[k] + second_q[k] + [sibling_q[k]]:
+            copy.wait_send()
+        for h in range(3):
+            hop(k, h, "sent")
     for k in range(n):
         sibling[k].wait_recv()
         for copy in along_z[k] + second[k] + third[k] + [sibling[k]]:
             copy.wait_send()
 
-def gather(shards, step=1280, cid=1):
-    count = len(shards)
-    pieces = []
-    for j, shard in enumerate(shards):
-        width = shard.shape[1]
-        s = step if width % step == 0 else width
-        pieces += [(j, start, s) for start in range(0, width, s)]
-    n = len(pieces)
-    total = sum(s.shape[1] for s in shards)
+
+def gather(shards, early, late, cid=1):
+    count, n, m = len(shards), len(early), len(late)
     dma = pltpu.SemaphoreType.DMA
     full = pl.pallas_call(
-        functools.partial(gather_kernel, tuple(pieces), count),
+        functools.partial(gather_kernel, tuple(early), tuple(late), count),
         out_shape=[jax.ShapeDtypeStruct((4, 2, 2, 2, ROWS, s.shape[1]), jnp.bfloat16) for s in shards],
         in_specs=[pl.BlockSpec(memory_space=pltpu.VMEM)] * count,
         out_specs=[pl.BlockSpec(memory_space=pl.ANY)] * count,
-        scratch_shapes=[dma((n,)), dma((n, 3)), dma((n, 3)), dma((n, 4)), dma((n, 4)), dma((n,)), dma((n,))],
+        scratch_shapes=[dma((n,)), dma((n, 6)), dma((n, 8)), dma((n, 2))]
+        + [dma((m,)), dma((m, 8)), dma((m, 12)), dma((m, 2))],
         compiler_params=pltpu.CompilerParams(collective_id=cid, has_side_effects=True),
         name="gather_weights",
     )(*shards)
     return [f.reshape(32 * ROWS, f.shape[-1]) for f in full]
+
+
+EARLY = (
+    [(0, 1280, 256), (0, 0, 1280)]
+    + [(1, 1280 * j, 1280) for j in range(3)]
+    + [(2, 0, 1280)]
+    + [(4, 1280 * j, 1280) for j in range(4)]
+    + [(3, 3072, 768), (3, 3840, 1280), (5, 0, 768), (5, 768, 512)]
+)
+LATE = [(3, 512 * j, 512) for j in range(6)]
 
 
 RING = 3
@@ -590,7 +687,7 @@
 
 
 def gather_in_parts(shards):
-    early = gather(shards[:6])
+    early = gather(shards[:6], EARLY, LATE)
     late, _ = lax.optimization_barrier((jnp.concatenate(shards[6:], axis=1), early[0]))
     late = lax.all_gather(late, EVERYONE, axis=0, tiled=True)
     return early + [late[:, :D], late[:, D:]]
@@ -637,7 +734,7 @@
         own_readout[0],
         own_readout[1],
     ]
-    fast = (dp_size, head_size) == (8, 4) and input_segments.shape[0] == SEQ
+    fast = (dp_size, head_size) == (8, 4) and perceptron_params.shape[2] == 4 * D
     first, qkv_w, attn_out_w, up_w, down_w, hidden_w, readout_w, shortcut_w = (
         gather_in_parts(shards)
         if fast
@@ -679,13 +776,10 @@
     )
     prediction = lax.all_to_all(own_prediction, "head", split_axis=1, concat_axis=0, tiled=True)
 
-    head_share = summed(
-        jnp.concatenate(
-            [rounded(bilinear_flipped(head_act, adjoint)), rounded(bilinear_flipped(stream_low, adjoint))],
-            axis=1,
-        )
-    )
-    head_share = jnp.stack([head_share[:, :D], head_share[:, D:]])
+    shard_rows = D // (dp_size * head_size)
+    head_left = jnp.stack([v.T.reshape(-1, shard_rows, tok_count) for v in (head_act, stream_low)], axis=1)
+    head_share = summed(matrix_multiply(head_left.reshape(2 * D, tok_count), adjoint))
+    head_share = head_share.reshape(2, shard_rows, head_size, -1).transpose(2, 0, 1, 3)
     grad_head_act = flipped_bilinear(adjoint, readout_w)
     grad_skip = flipped_bilinear(adjoint, shortcut_w)
     grad_head_pre = rounded(grad_head_act * silu_slope(head_pre))
@@ -736,9 +830,8 @@
             summed(bilinear_flipped(lefts[i], rights[j][:, start : start + D])) for i, j, start in pieces
         ]
         small_share = summed(small)
-    head_share = lax.all_to_all(
-        head_share, "head", split_axis=2, concat_axis=1, tiled=True
-    )
+    head_share = lax.all_to_all(head_share, "head", split_axis=0, concat_axis=0)
+    head_share = head_share.transpose(1, 0, 2, 3).reshape(readout_params.shape)
     down_at = 1
     up_at = down_at + wide
     wo_at = up_at + wide

time: 738 us -> 683 us (0.925)
  Pallas kernels: 477 us -> 445 us
  local copies, waits for them, and re-layouts: 71.7 us -> 54.4 us
    pallas_call x1, Pallas kernels: 218 us -> 189 us  [gather(): pl.pallas_call(functools.partial(gather_kernel, tuple(early), tuple(late)...]
    unnamed x165 -> x161, local copies, waits for them, and re-layouts: 31.2 us -> 15.5 us
    dot_general x10 -> x11, matrix products: 53.8 us -> 61.2 us  [matrix_multiply(): return jnp.dot(left_mat, right_mat, preferred_element_type=jnp.float32)]
  transfers between devices with their start and end apart: 6 -> 6, of which waited for: 1 -> 1; matrix products, arithmetic and copies ran while one was open for 27% -> 27% of each run, Pallas kernels for 65% -> 66%
where the time goes in v3:
time: 683 us; the launch traced here: 678 us
  Pallas kernels  445 us (65%)
  matrix products  123 us (18%)
  local copies, waits for them, and re-layouts  54.4 us (8%)
  other arithmetic  19.5 us (3%)
  starting transfers between devices  17.3 us (3%)
  between operations  15.8 us (2%)
    pallas_call x1, Pallas kernels, reduce_products(): pl.pallas_call(functools.partial(reduce_kernel, tuple(pieces), len(lefts)...  219 us
    pallas_call x1, Pallas kernels, gather(): pl.pallas_call(functools.partial(gather_kernel, tuple(early), tuple(late)...  189 us
    dot_general x11, matrix products, matrix_multiply(): return jnp.dot(left_mat, right_mat, preferred_element_type=jnp.float32)  61.2 us
    dot_general x12, matrix products, flipped_bilinear(): lax.dot_general(left_mat, right_mat, (((1,), (1,)), ((), ())), preferred_...  60.7 us
    pallas_call x2, Pallas kernels, attention_call(): pl.pallas_call(kernel, grid=(HEADS // STEP_HEADS,), out_shape=out_shape,...  36.7 us
    unnamed x161, local copies, waits for them, and re-layouts  15.5 us
  transfers between devices with their start and end apart: 6, of which 1 were waited for; matrix products, arithmetic and copies ran while one was open for 27% of the time, Pallas kernels for 66%

profile of v3, /device:TPU:0, one launch (start us, length us, event | category | flops | bytes accessed | tf_op | source)
XLA Modules:
  0.0 677.9 jit_solution(4542250811812668852)
XLA Ops:
  7.2 2.2 copy.244
  9.5 4.3 all-to-all-start
  18.5 189.0 %gather_weights.1 = (bf16[4,2,2,2,40,1536]{5,4,3,2,1,0:T(8,128)(2,1)}, bf16[4,2,2,2,40,3840]{5,4,3,2,1,0:T(8,128)(2,1)}, bf16[4,2,2,2,40,1280]{5,4,3,2,1,0:T(8,1...) custom-call(bf16[40,1536]{1,0:T(8,128)(2,1)} %concatenate.31.refs_0_, ...), custom_call_target="tpu_custom_call" | custom-call | tf_op jit(solution)/shard_map/gather_weights/pallas_call | solution.py:180
  209.8 4.4 all-to-all-start.2
  216.1 3.1 fusion.28
  219.2 2.2 fusion.17
  222.9 5.4 fusion.51.query_in.key_in.value_in
  228.4 15.5 %attend.1 = (bf16[512,1280]{1,0:T(8,128)(2,1)S(1)}, f32[16,1,512]{2,1,0:T(1,128)S(1)}) custom-call(f32[512,3840]{1,0:T(8,128)S(1)} %fusion.51.query_in.key_in.value_in, f32[512,3840]{1,0:T(8,128)S(1)} %fusion.51.query_in.key_in.value_in, f32[512,3840]{1,0:T(8,128)S(1)} %fusion.51.query_in.key_in.value_in, f32[40,512]{1,0:T(8,128)S(1)} %get-tuple-element.203.cosines, ...), custom_call_target="tpu_custom_call" | custom-call | flops 2684354560 | bytes 13107200 | tf_op jit(solution)/shard_map/attend/pallas_call | solution.py:623
  244.0 4.0 multiply_reduce_fusion.4
  248.1 11.8 %multiply_convert_fusion.1 = (bf16[512,5120]{1,0:T(8,128)(2,1)}, f32[512,5120]{1,0:T(8,128)}) fusion(bf16[1280,5120]{1,0:T(8,128)(2,1)S(1)} %bitcast.243, f32[512,1280]{1,0:T(8,128)S(1)} %get-tuple-element.207, f32[1280]{0:T(1024)S(1)} %get-tuple-element.152, f32[512]{0:T(512)S(1)} %fusion.47), kind=kOutput, calls=%fused_computation.2 | convolution fusion | flops 6725959680 | bytes 31464448 | tf_op jit(solution)/shard_map/dot_general | solution.py:440
  259.9 13.7 %fusion.9 = bf16[512,1280]{1,0:T(8,128)(2,1)} fusion(f32[512,1280]{1,0:T(8,128)S(1)} %get-tuple-element.207, bf16[512,5120]{1,0:T(8,128)(2,1)} %get-tuple-element.208.refs_7_, bf16[1280,5120]{1,0:T(8,128)(2,1)} %bitcast.244), kind=kOutput, calls=%fused_computation.26 | convolution fusion | flops 6712197120 | bytes 22282240 | tf_op jit(solution)/shard_map/dot_general | solution.py:444
  274.3 1.6 copy.206
  277.0 1.5 copy.212
  278.5 2.6 copy.213
  281.1 2.1 copy.216
  285.8 6.3 fusion.29
  292.1 1.6 copy.228
  294.3 6.8 %convolution_convert_fusion = bf16[2560,1280]{1,0:T(8,128)(2,1)} fusion(bf16[2560,512]{1,0:T(8,128)(2,1)S(1)} %bitcast.222, bf16[512,1280]{0,1:T(8,128)(2,1)} %bitcast.25), kind=kOutput, calls=%fused_computation | convolution fusion | flops 3358720000 | bytes 10485760 | tf_op jit(solution)/shard_map/dot_general | solution.py:440
  301.1 1.7 copy-done.64
  302.8 4.3 fusion.14
  307.1 1.9 fusion.7
  310.5 4.7 all-to-all-start.1
  315.2 5.0 fusion.62
  321.3 1.9 fusion.63
  323.2 2.1 copy.208
  325.3 7.0 %fusion.27 = (bf16[1280,512]{1,0:T(8,128)(2,1)}, f32[1280,512]{1,0:T(8,128)}) fusion(f32[512,1280]{0,1:T(8,128)} %copy.208, bf16[512,1280]{0,1:T(8,128)(2,1)} %bitcast.25, bf16[1280,2560]{1,0:T(8,128)(2,1)} %all-gather.2.cloned.1.call-done), kind=kOutput, calls=%fused_computation.50 | convolution fusion | flops 1679032320 | bytes 11141120 | tf_op jit(solution)/shard_map/dot_general | solution.py:444
  332.3 3.2 copy.204
  335.5 15.3 %multiply_convert_fusion.refs_8_ = bf16[512,5120]{1,0:T(8,128)(2,1)} fusion(f32[512,5120]{1,0:T(8,128)} %get-tuple-element.209, bf16[1280,5120]{1,0:T(8,128)(2,1)} %bitcast.245, f32[512,1280]{1,0:T(8,128)S(1)} %fusion.63, f32[1280,512]{0,1:T(8,128)} %copy.204), kind=kOutput, calls=%fused_computation.1 | convolution fusion | flops 6735790080 | bytes 34078720 | tf_op jit(solution)/shard_map/dot_general | solution.py:440
  352.0 14.8 %multiply_reduce_fusion = (bf16[1280]{0:T(1024)(128)(2,1)S(1)}, f32[512]{0:T(512)S(1)}, f32[512,1280]{1,0:T(8,128)}) fusion(f32[512,1280]{1,0:T(8,128)} %copy-done.21, f32[512]{0:T(512)S(1)} %fusion.47, f32[1280]{0:T(1024)S(1)} %get-tuple-element.152, bf16[512,5120]{1,0:T(8,128)(2,1)} %multiply_convert_fusion.refs_8_, bf16[1280,5120]{1,0:T(8,128)(2,1)} %bitcast.240), kind=kOutput, calls=%fused_computation.52 | convolution fusion | flops 6714817024 | bytes 23604736 | tf_op jit(solution)/shard_map/dot_general | solution.py:444
  366.9 6.8 fusion.58
  373.7 1.7 copy.210
  376.6 4.0 convolution_convert_fusion.1.grad_mixed
  380.6 3.3 copy-done.1
  383.9 21.1 %attend_back.1 = (bf16[512,1280]{1,0:T(8,128)(2,1)S(1)}, bf16[512,1280]{1,0:T(8,128)(2,1)S(1)}, bf16[512,1280]{1,0:T(8,128)(2,1)S(1)}) custom-call(f32[512,3840]{1,0:T(8,128)S(1)} %copy-done.1, f32[512,3840]{1,0:T(8,128)S(1)} %copy-done.1, f32[512,3840]{1,0:T(8,128)S(1)} %copy-done.1, f32[40,512]{1,0:T(8,128)S(1)} %copy-done.8, f32[40,512]{1,0:T(8,128)S(1)} %copy-done.6, ...), custom_call_target="tpu_custom_call" | custom-call | flops 2684354560 | bytes 13107200 | tf_op jit(solution)/shard_map/attend_back/pallas_call | solution.py:623
  405.1 1.9 fusion.3
  407.1 1.9 convolution_add_fusion.4
  409.0 2.4 multiply_reduce_fusion.1
  412.6 1.5 copy.214
  414.1 2.6 copy.215
  416.8 4.3 fusion.61
  423.9 219.5 %reduce_products.1 = (f32[14,40,1280]{2,1,0:T(8,128)}, f32[40,256]{1,0:T(8,128)}) custom-call(bf16[2,640,512]{2,1,0:T(8,128)(2,1)} %bitcast.210, bf16[2,640,512]{2,1,0:T(8,128)(2,1)} %bitcast.213, bf16[2,640,512]{2,1,0:T(8,128)(2,1)} %bitcast.214, bf16[2,640,512]{2,1,0:T(8,128)(2,1)} %bitcast.211, bf16[2,640,512]{2,1,0:T(8,128)(2,1)} %bitcast.215, ...), custom_call_target="tpu_custom_call" | custom-call | tf_op jit(solution)/shard_map/reduce_products/pallas_call | solution.py:416
  643.4 1.6 fusion.38
  645.0 1.6 fusion.35
  649.1 2.9 multiply_add_fusion
  652.9 2.2 multiply_add_fusion.2
  657.2 3.6 all-to-all-start.3
  663.6 2.6 copy.239
  666.1 3.2 all-to-all-done.3
  (232 shorter events, 33.5 us)
Async XLA Ops:
  7.2 8.6 %copy-start.40 = (f32[2,40,64]{2,1,0:T(8,128)S(1)}, f32[2,40,64]{2,1,0:T(8,128)}, u32[]{:S(2)}) copy-start(f32[2,40,64]{2,1,0:T(8,128)} %param.29) | copy-start | bytes 61444
  7.2 8.6 %copy-start.53 = (f32[5,40]{1,0:T(8,128)S(1)}, f32[5,40]{1,0:T(8,128)}, u32[]{:S(2)}) copy-start(f32[5,40]{1,0:T(8,128)} %param.32) | copy-start | bytes 2404
  7.2 8.7 %copy-start.16 = (f32[2,40,5120]{2,1,0:T(8,128)S(1)}, f32[2,40,5120]{2,1,0:T(8,128)}, u32[]{:S(2)}) copy-start(f32[2,40,5120]{2,1,0:T(8,128)} %param.26) | copy-start | bytes 4915204
  9.5 198.0 %all-to-all-start = ((bf16[2,160,320]{2,0,1:T(2,128)(2,1)}), bf16[2,160,320]{2,0,1:T(2,128)(2,1)S(1)}, u32[]{:S(2)}, u32[]{:S(2)}) async-start(bf16[2,160,320]{2,0,1:T(2,128)(2,1)} %copy.244), calls=%async_computation | async-start | bytes 491520 | tf_op jit(solution)/shard_map/all_to_all | solution.py:725
  13.7 287.4 %all-gather.2.cloned.1.call-start = ((), (), s32[]{:S(2)}) async-start(), calls=%async_computation.5 | async-start | bytes 6758400 | tf_op jit(solution)/shard_map/all_gather | solution.py:692
  17.0 191.7 %copy-start.26 = (bf16[2048,320]{0,1:T(8,128)(2,1)S(1)}, bf16[2048,320]{0,1:T(8,128)(2,1)}, u32[]{:S(2)}) copy-start(bf16[2048,320]{0,1:T(8,128)(2,1)} %param.22) | copy-start | bytes 3932164
  208.7 7.0 %copy-start.9 = (s32[512]{0:T(512)S(1)}, s32[512]{0:T(512)}, u32[]{:S(2)}) copy-start(s32[512]{0:T(512)} %param.21) | copy-start | bytes 6148
  209.8 6.2 copy-start.31
  209.8 6.2 copy-start.46
  209.8 84.4 %all-to-all-start.2 = ((bf16[4,512,320]{1,2,0:T(8,128)(2,1)}), bf16[4,512,320]{1,2,0:T(8,128)(2,1)}, u32[]{:S(2)}, u32[]{:S(2)}) async-start(bf16[4,512,320]{1,2,0:T(8,128)(2,1)} %bitcast.201), calls=%async_computation.2 | async-start | bytes 2621440 | tf_op jit(solution)/shard_map/all_to_all | solution.py:726
  214.3 440.8 %reduce-scatter.2.cloned.1.call-start = ((), (), s32[]{:S(2)}) async-start(), calls=%async_computation.6 | async-start | bytes 6758400 | tf_op jit(solution)/shard_map/reduce_scatter | solution.py:684
  216.0 6.7 copy-start.49
  216.0 5.4 copy-start.33
  216.1 5.4 copy-start.35
  216.1 6.6 slice-start.4
  222.2 6.1 copy-start.51
  222.2 21.7 %copy-start.13 = (f32[512,1280]{1,0:T(8,128)}, f32[512,1280]{1,0:T(8,128)S(1)}, u32[]{:S(2)}) copy-start(f32[512,1280]{1,0:T(8,128)S(1)} %get-tuple-element.205) | copy-start | bytes 7864324
  222.2 6.1 copy-start.54
  222.6 5.7 copy-start.5
  222.6 5.7 copy-start.7
  228.3 15.6 %copy-start = (f32[512,3840]{1,0:T(8,128)}, f32[512,3840]{1,0:T(8,128)S(1)}, u32[]{:S(2)}) copy-start(f32[512,3840]{1,0:T(8,128)S(1)} %fusion.51.query_in.key_in.value_in) | copy-start | bytes 23592964
  228.4 19.7 %slice-start = ((s8[13107200]{0:T(1024)(128)(4,1)}), s8[4194304]{0:T(1024)(128)(4,1)S(1)}, s32[]{:S(2)}) async-start(s8[13107200]{0:T(1024)(128)(4,1)} %bitcast.241), calls=%async_computation.7 | async-start | bytes 8388608
  228.4 19.7 %slice-start.1 = ((s8[13107200]{0:T(1024)(128)(4,1)}), s8[4194304]{0:T(1024)(128)(4,1)S(1)}, s32[]{:S(2)}) async-start(s8[13107200]{0:T(1024)(128)(4,1)} %bitcast.241), calls=%async_computation.8 | async-start | bytes 8388608
  228.4 19.7 %slice-start.2 = ((s8[13107200]{0:T(1024)(128)(4,1)}), s8[4194304]{0:T(1024)(128)(4,1)S(1)}, s32[]{:S(2)}) async-start(s8[13107200]{0:T(1024)(128)(4,1)} %bitcast.241), calls=%async_computation.9 | async-start | bytes 8388608
  248.0 11.9 %copy-start.56 = (f32[512]{0:T(512)}, f32[512]{0:T(512)S(1)}, u32[]{:S(2)}) copy-start(f32[512]{0:T(512)S(1)} %get-tuple-element.206) | copy-start | bytes 6148
  248.0 11.9 %copy-start.21 = (f32[512,1280]{1,0:T(8,128)}, f32[512,1280]{1,0:T(8,128)S(1)}, u32[]{:S(2)}) copy-start(f32[512,1280]{1,0:T(8,128)S(1)} %get-tuple-element.207) | copy-start | bytes 7864324
  302.8 4.3 copy-start.27
  302.8 4.3 copy-start.60
  310.5 4.7 copy-start.65
  310.5 346.8 %all-to-all-start.1 = ((bf16[512,4,320]{0,2,1:T(8,128)(2,1)}), bf16[512,4,320]{0,2,1:T(8,128)(2,1)}, u32[]{:S(2)}, u32[]{:S(2)}) async-start(bf16[512,4,320]{0,2,1:T(8,128)(2,1)} %bitcast.22), calls=%async_computation.1 | async-start | bytes 2621440 | tf_op jit(solution)/shard_map/all_to_all | solution.py:777
  315.2 6.1 copy-start.61
  335.5 15.3 %copy-start.28 = (bf16[1280,512]{1,0:T(8,128)(2,1)S(1)}, bf16[1280,512]{1,0:T(8,128)(2,1)}, u32[]{:S(2)}) copy-start(bf16[1280,512]{1,0:T(8,128)(2,1)} %get-tuple-element.210) | copy-start | bytes 3932164
  352.0 14.8 %copy-start.57 = (f32[512]{0:T(512)S(1)}, f32[512]{0:T(512)}, u32[]{:S(2)}) copy-start(f32[512]{0:T(512)} %copy-done.56) | copy-start | bytes 6148
  376.6 28.5 %slice-start.7 = ((s8[9830400]{0:T(1024)(128)(4,1)}), s8[4194304]{0:T(1024)(128)(4,1)S(1)}, s32[]{:S(2)}) async-start(s8[9830400]{0:T(1024)(128)(4,1)} %bitcast.249), calls=%async_computation.14 | async-start | bytes 8388608
  383.9 21.2 %slice-start.8 = ((s8[9830400]{0:T(1024)(128)(4,1)}), s8[4194304]{0:T(1024)(128)(4,1)S(1)}, s32[]{:S(2)}) async-start(s8[9830400]{0:T(1024)(128)(4,1)} %bitcast.249), calls=%async_computation.15 | async-start | bytes 8388608
  383.9 21.2 %slice-start.9 = ((s8[9830400]{0:T(1024)(128)(4,1)}), s8[1441792]{0:T(1024)(128)(4,1)S(1)}, s32[]{:S(2)}) async-start(s8[9830400]{0:T(1024)(128)(4,1)} %bitcast.249), calls=%async_computation.16 | async-start | bytes 2883584
  412.6 8.9 %copy-start.11 = (bf16[512,1280]{1,0:T(8,128)(2,1)}, bf16[512,1280]{1,0:T(8,128)(2,1)S(1)}, u32[]{:S(2)}) copy-start(bf16[512,1280]{1,0:T(8,128)(2,1)S(1)} %get-tuple-element.172.refs_13_) | copy-start | bytes 3932164
  416.8 4.7 copy-start.34
  416.8 4.7 copy-start.36
  423.8 221.2 %copy-start.12 = (bf16[512,1280]{1,0:T(8,128)(2,1)S(1)}, bf16[512,1280]{1,0:T(8,128)(2,1)}, u32[]{:S(2)}) copy-start(bf16[512,1280]{1,0:T(8,128)(2,1)} %copy-done.11) | copy-start | bytes 3932164
  655.1 5.8 copy-start.43
  655.1 5.8 copy-start.44
  655.1 5.8 copy-start.45
  655.1 7.9 %copy-start.32 = (s32[512,32]{0,1:T(8,128)S(1)}, s32[512,32]{0,1:T(8,128)}, u32[]{:S(2)}) copy-start(s32[512,32]{0,1:T(8,128)} %param.20) | copy-start | bytes 196612
  657.2 12.1 %copy-start.22 = (f32[2,160,320]{2,1,0:T(8,128)S(1)}, f32[2,160,320]{2,1,0:T(8,128)}, u32[]{:S(2)}) copy-start(f32[2,160,320]{2,1,0:T(8,128)} %param.35) | copy-start | bytes 1228804
  657.2 12.1 %copy-start.37 = (f32[2,160,320]{2,1,0:T(8,128)S(1)}, f32[2,160,320]{2,1,0:T(8,128)}, u32[]{:S(2)}) copy-start(f32[2,160,320]{2,1,0:T(8,128)} %param.37) | copy-start | bytes 1228804
  657.2 12.1 %copy-start.38 = (f32[2,160,320]{2,1,0:T(8,128)S(1)}, f32[2,160,320]{2,1,0:T(8,128)}, u32[]{:S(2)}) copy-start(f32[2,160,320]{2,1,0:T(8,128)} %param.36) | copy-start | bytes 1228804
  657.2 12.0 %all-to-all-start.3 = ((f32[4,2,40,320]{3,2,1,0:T(8,128)}), f32[4,2,40,320]{3,2,1,0:T(8,128)S(1)}, u32[]{:S(2)}, u32[]{:S(2)}) async-start(f32[4,2,40,320]{3,2,1,0:T(8,128)} %bitcast.202), calls=%async_computation.4 | async-start | bytes 983040 | tf_op jit(solution)/shard_map/all_to_all | solution.py:833
  (34 other events, 98.4 us)
Sparse Core Ops, SparseCore 0:
  208.8 73.3 all-gather.1
  301.2 149.9 reduce-scatter.1

commit v4 on v3

--- a/solution.py
+++ b/solution.py
@@ -206,14 +206,14 @@
     lefts, rights, small = refs[:lefts_n], refs[lefts_n:lefts_n + rights_n], refs[lefts_n + rights_n]
     refs = refs[lefts_n + rights_n + 1:]
     out, small_out = refs[:2]
-    left_buf, right_buf, load_sem = refs[2:5]
-    main_bufs, small_bufs = refs[5:5 + 17], refs[5 + 17:5 + 34]
+    left_buf, right_buf, flipped, load_sem = refs[2:6]
+    main_bufs, small_bufs = refs[6 : 6 + 16], refs[6 + 16 : 6 + 32]
     z, x, y, c = place()
     meet(z, x, y, c)
     f32, low = jnp.float32, jnp.bfloat16
 
     def lane(bufs, ring, total, columns):
-        out_s, kept, in_s, in_a, in_b, sum_a, sum_b, in_c, in_d, last, in_z, s_sem, p_sem, q_sem, z_sem, credit, credit_z = bufs
+        both, in_s, in_a, in_b, sum_a, sum_b, in_c, in_d, last, in_z, s_sem, p_sem, q_sem, z_sem, credit, credit_z = bufs
         half = columns // 2
         front, back = pl.ds(0, half), pl.ds(half, half)
         to_x, to_y, to_c = device(z, 1 - x, y, c), device(z, x, 1 - y, c), device(z, x, y, 1 - c)
@@ -224,12 +224,12 @@
 
         def sibling(k):
             s = k % ring
-            return remote(out_s.at[s], in_s.at[s], (s_sem.at[s, 0], s_sem.at[s, 1]), to_c)
+            return remote(both.at[1 - c, s], in_s.at[s], (s_sem.at[s, 0], s_sem.at[s, 1]), to_c)
 
         def first(k):
             s = k % ring
-            return (remote(kept.at[s, :, :, 1 - y, :, front], in_a.at[s], (p_sem.at[s, 0], p_sem.at[s, 1]), to_y),
-                    remote(kept.at[s, :, 1 - x, :, :, back], in_b.at[s], (p_sem.at[s, 2], p_sem.at[s, 3]), to_x))
+            return (remote(both.at[c, s, :, :, 1 - y, :, front], in_a.at[s], (p_sem.at[s, 0], p_sem.at[s, 1]), to_y),
+                    remote(both.at[c, s, :, 1 - x, :, :, back], in_b.at[s], (p_sem.at[s, 2], p_sem.at[s, 3]), to_x))
 
         def second(k):
             s = k % ring
@@ -269,7 +269,7 @@
             sibling(k).wait_recv()
 
             def body(i, carry):
-                kept[s, i] = add(kept[s, i], in_s[s, i])
+                both[c, s, i] = add(both[c, s, i], in_s[s, i])
                 return carry
             lax.fori_loop(0, 4, body, 0)
             give(0, k, to_c)
@@ -286,8 +286,8 @@
 
             def body(i, carry):
                 for j in range(2):
-                    sum_a[s, i, j] = add(kept[s, i, j, y, :, :half], in_a[s, i, j])
-                    sum_b[s, i, j] = add(kept[s, i, x, j, :, half:], in_b[s, i, j])
+                    sum_a[s, i, j] = add(both[c, s, i, j, y, :, :half], in_a[s, i, j])
+                    sum_b[s, i, j] = add(both[c, s, i, x, j, :, half:], in_b[s, i, j])
                 return carry
             lax.fori_loop(0, 4, body, 0)
             give(1, k, to_y)
@@ -340,8 +340,7 @@
 
     fresh, send_sibling, one, two, three, four, drain = lane(main_bufs, RING, n, width)
     _, small_sibling, small_one, small_two, small_three, small_four, small_drain = lane(small_bufs, 1, 1, small_width)
-    out_s, kept = main_bufs[:2]
-    small_s, small_kept = small_bufs[:2]
+    both, small_both = main_bufs[0], small_bufs[0]
 
     def load(k, start):
         for number, (i, j, begin) in enumerate(pieces):
@@ -352,20 +351,27 @@
                              pltpu.make_async_copy(rights[j].at[:, pl.ds(begin, width)], right_buf.at[s], load_sem.at[s, 1])):
                     copy.start() if start else copy.wait()
 
-    def multiply(k, parity, target):
-        tile = 256
+    def multiply(k):
+        flipped[...] = left_buf[k % 2].T
+        tile, rows = 256, 16 * ROWS
 
         def body(j, carry):
             cols = pl.ds(pl.multiple_of(j * tile, tile), tile)
-            value = jnp.dot(left_buf[k % 2, parity], right_buf[k % 2, :, cols], preferred_element_type=f32)
-            for i in range(16):
-                target[k % RING, i // 4, (i // 2) % 2, i % 2, :, cols] = value[i * ROWS:(i + 1) * ROWS].astype(low)
+            for part in range(2):
+                value = jnp.dot(
+                    flipped[part * rows : (part + 1) * rows], right_buf[k % 2, :, cols], preferred_element_type=f32
+                )
+                for r in range(16):
+                    i = part * 16 + r
+                    both[i % 2, k % RING, i // 8, (i // 4) % 2, (i // 2) % 2, :, cols] = value[
+                        r * ROWS : (r + 1) * ROWS
+                    ].astype(low)
             return carry
+
         lax.fori_loop(0, width // tile, body, 0)
 
     load(0, True)
-    small_s[0] = small[1 - c]
-    small_kept[0] = small[c]
+    small_both[:, 0] = small[...]
 
     def step(t, carry):
         @pl.when(t < n)
@@ -373,9 +379,8 @@
             load(t + 1, True)
             load(t, False)
             fresh(t)
-            multiply(t, 1 - c, out_s)
+            multiply(t)
             send_sibling(t)
-            multiply(t, c, kept)
         for j, work in enumerate((lambda: small_sibling(0), lambda: small_one(0), lambda: small_two(0),
                                   lambda: small_three(0), lambda: small_four(0, small_out))):
             @pl.when(t == j)
@@ -398,15 +403,11 @@
 def buffers(ring, columns):
     dma, reg = pltpu.SemaphoreType.DMA, pltpu.SemaphoreType.REGULAR
     half, low = columns // 2, jnp.bfloat16
-    block = [pltpu.VMEM((ring, 4, 2, 2, ROWS, columns), low)] * 3
+    block = [pltpu.VMEM((2, ring, 4, 2, 2, ROWS, columns), low), pltpu.VMEM((ring, 4, 2, 2, ROWS, columns), low)]
     halves = [pltpu.VMEM((ring, 4, 2, ROWS, half), low)] * 4
     quarters = [pltpu.VMEM((ring, 4, ROWS, half), low)] * 2
     ends = [pltpu.VMEM((ring, 4, ROWS, columns), low), pltpu.VMEM((ring, 3, ROWS, columns), low)]
     return block + halves + quarters + ends + [dma((ring, 2)), dma((ring, 4)), dma((ring, 4)), dma((ring, 6)), reg((5,)), reg((3,))]
-
-def turned(value):
-    tokens = value.shape[0]
-    return value.T.reshape(16, 2, ROWS, tokens).swapaxes(0, 1).reshape(2, 16 * ROWS, tokens)
 
 def reduce_products(lefts, rights, pieces, small, width=1280, cid=2):
     n = len(pieces)
@@ -418,7 +419,8 @@
         out_shape=[jax.ShapeDtypeStruct((n, ROWS, width), jnp.float32), jax.ShapeDtypeStruct((ROWS, small_width), jnp.float32)],
         in_specs=[hbm] * (len(lefts) + len(rights)) + [vmem],
         out_specs=[vmem, vmem],
-        scratch_shapes=[pltpu.VMEM((2, 2, 16 * ROWS, tokens), jnp.bfloat16), pltpu.VMEM((2, tokens, width), jnp.bfloat16),
+        scratch_shapes=[pltpu.VMEM((2, tokens, 32 * ROWS), jnp.bfloat16), pltpu.VMEM((2, tokens, width), jnp.bfloat16),
+                        pltpu.VMEM((32 * ROWS, tokens), jnp.bfloat16),
                         pltpu.SemaphoreType.DMA((2, 2))] + buffers(RING, width) + buffers(1, small_width),
         compiler_params=pltpu.CompilerParams(collective_id=cid, has_side_effects=True, vmem_limit_bytes=60 * 1024 * 1024),
         name="reduce_products",
@@ -824,7 +826,7 @@
     lefts = [stream_low, grad_ffn_out, normed_ffn, attn_mix, normed_attn, tok_act]
     rights = [grad_head_pre, ffn_act, grad_ffn_pre, grad_attn_out, *grad_qkv_pre, grad_tok_out]
     if fast:
-        shares, small_share = reduce_products([turned(v) for v in lefts], rights, pieces, owned(small))
+        shares, small_share = reduce_products(lefts, rights, pieces, owned(small))
     else:
         shares = [
             summed(bilinear_flipped(lefts[i], rights[j][:, start : start + D])) for i, j, start in pieces

time: 683 us -> 670 us (0.981)
  local copies, waits for them, and re-layouts: 54.4 us -> 37.6 us
  Pallas kernels: 445 us -> 456 us
    pallas_call x1, Pallas kernels: 219 us -> 231 us  [reduce_products(): pl.pallas_call(functools.partial(reduce_kernel, tuple(pieces), len(lefts)...]
    transpose x6 -> x0, local copies, waits for them, and re-layouts: 10.3 us -> none  [turned(): value.T.reshape(16, 2, ROWS, tokens).swapaxes(0, 1)]
    unnamed x161 -> x173, local copies, waits for them, and re-layouts: 15.5 us -> 19.1 us
  transfers between devices with their start and end apart: 6 -> 6, of which waited for: 1 -> 1; matrix products, arithmetic and copies ran while one was open for 27% -> 24% of each run, Pallas kernels for 66% -> 69%
where the time goes in v4:
time: 670 us; the launch traced here: 665 us
  Pallas kernels  456 us (68%)
  matrix products  117 us (17%)
  local copies, waits for them, and re-layouts  37.6 us (6%)
  starting transfers between devices  17.6 us (3%)
  other arithmetic  17.6 us (3%)
  between operations  15.7 us (2%)
    pallas_call x1, Pallas kernels, reduce_products(): pl.pallas_call(functools.partial(reduce_kernel, tuple(pieces), len(lefts)...  231 us
    pallas_call x1, Pallas kernels, gather(): pl.pallas_call(functools.partial(gather_kernel, tuple(early), tuple(late)...  189 us
    dot_general x11, matrix products, matrix_multiply(): return jnp.dot(left_mat, right_mat, preferred_element_type=jnp.float32)  60.3 us
    dot_general x12, matrix products, flipped_bilinear(): lax.dot_general(left_mat, right_mat, (((1,), (1,)), ((), ())), preferred_...  55.8 us
    pallas_call x2, Pallas kernels, attention_call(): pl.pallas_call(kernel, grid=(HEADS // STEP_HEADS,), out_shape=out_shape,...  36.5 us
    unnamed x173, local copies, waits for them, and re-layouts  19.1 us
  transfers between devices with their start and end apart: 6, of which 1 were waited for; matrix products, arithmetic and copies ran while one was open for 24% of the time, Pallas kernels for 69%

profile of v4, /device:TPU:0, one launch (start us, length us, event | category | flops | bytes accessed | tf_op | source)
XLA Modules:
  0.0 665.0 jit_solution(16536140933153969787)
XLA Ops:
  7.2 2.2 copy.171
  9.5 4.3 all-to-all-start
  13.7 1.3 convert_element_type.87
  18.5 189.0 %gather_weights.1 = (bf16[4,2,2,2,40,1536]{5,4,3,2,1,0:T(8,128)(2,1)}, bf16[4,2,2,2,40,3840]{5,4,3,2,1,0:T(8,128)(2,1)}, bf16[4,2,2,2,40,1280]{5,4,3,2,1,0:T(8,1...) custom-call(bf16[40,1536]{1,0:T(8,128)(2,1)} %concatenate.31.refs_0_, ...), custom_call_target="tpu_custom_call" | custom-call | tf_op jit(solution)/shard_map/gather_weights/pallas_call | solution.py:180
  208.8 1.2 copy.172
  210.1 4.3 all-to-all-start.2
  216.4 3.5 multiply_convert_fusion.5
  219.9 1.9 fusion.16
  223.3 1.2 slice-done.9
  224.4 1.4 slice-done.10
  225.9 5.2 fusion.51.query_in.key_in.value_in
  231.2 15.5 %attend.1 = (bf16[512,1280]{1,0:T(8,128)(2,1)S(1)}, f32[16,1,512]{2,1,0:T(1,128)S(1)}) custom-call(f32[512,3840]{1,0:T(8,128)S(1)} %fusion.51.query_in.key_in.value_in, f32[512,3840]{1,0:T(8,128)S(1)} %fusion.51.query_in.key_in.value_in, f32[512,3840]{1,0:T(8,128)S(1)} %fusion.51.query_in.key_in.value_in, f32[40,512]{1,0:T(8,128)S(1)} %get-tuple-element.201.cosines, ...), custom_call_target="tpu_custom_call" | custom-call | flops 2684354560 | bytes 13107200 | tf_op jit(solution)/shard_map/attend/pallas_call | solution.py:625
  246.7 4.4 multiply_reduce_fusion.4
  251.5 11.4 %multiply_convert_fusion.1 = (bf16[512,5120]{1,0:T(8,128)(2,1)}, f32[512,5120]{1,0:T(8,128)}) fusion(bf16[512,1280]{1,0:T(8,128)(2,1)S(1)} %multiply_convert_fusion.3.refs_2_, bf16[1280,5120]{1,0:T(8,128)(2,1)S(1)} %bitcast.182), kind=kOutput, calls=%fused_computation.2 | convolution fusion | flops 6723993600 | bytes 30146560 | tf_op jit(solution)/shard_map/dot_general | solution.py:442
  263.0 13.7 %fusion.9.refs_0_ = bf16[512,1280]{1,0:T(8,128)(2,1)S(1)} fusion(f32[512,1280]{1,0:T(8,128)S(1)} %get-tuple-element.207, bf16[512,5120]{1,0:T(8,128)(2,1)} %get-tuple-element.208.refs_7_, bf16[1280,5120]{1,0:T(8,128)(2,1)} %bitcast.183), kind=kOutput, calls=%fused_computation.28 | convolution fusion | flops 6712197120 | bytes 22282240 | tf_op jit(solution)/shard_map/dot_general | solution.py:446
  279.8 5.9 fusion.23
  285.7 2.4 copy.155
  288.1 1.6 pad_maximum_fusion
  289.7 2.0 copy.157
  291.6 8.4 %convolution_convert_fusion = bf16[2560,1280]{1,0:T(8,128)(2,1)} fusion(bf16[2560,512]{1,0:T(8,128)(2,1)} %bitcast.163, bf16[512,1280]{0,1:T(8,128)(2,1)} %bitcast.25), kind=kOutput, calls=%fused_computation | convolution fusion | flops 3358720000 | bytes 10485760 | tf_op jit(solution)/shard_map/dot_general | solution.py:442
  300.1 5.1 fusion.13
  305.1 1.9 fusion.7
  307.0 1.5 copy.141
  308.5 4.7 all-to-all-start.1
  313.2 4.5 convolution_bitcast_fusion.1
  317.7 5.1 fusion.50
  322.9 3.4 fusion.48
  327.4 13.0 %multiply_convert_fusion.refs_8_ = bf16[512,5120]{1,0:T(8,128)(2,1)} fusion(f32[512,5120]{1,0:T(8,128)} %get-tuple-element.209, bf16[512,1280]{1,0:T(8,128)(2,1)S(1)} %get-tuple-element.210.refs_1_, bf16[1280,5120]{1,0:T(8,128)(2,1)S(1)} %bitcast.186), kind=kOutput, calls=%fused_computation.1 | convolution fusion | flops 6734479360 | bytes 30146560 | tf_op jit(solution)/shard_map/dot_general | solution.py:442
  340.3 14.5 %multiply_reduce_fusion = (bf16[1280]{0:T(1024)(128)(2,1)S(1)}, f32[512]{0:T(512)S(1)}, f32[512,1280]{1,0:T(8,128)}) fusion(f32[512,1280]{1,0:T(8,128)S(1)} %copy-done.17, f32[512]{0:T(512)S(1)} %fusion.39, f32[1280]{0:T(1024)S(1)} %get-tuple-element.152, bf16[512,5120]{1,0:T(8,128)(2,1)} %multiply_convert_fusion.refs_8_, bf16[1280,5120]{1,0:T(8,128)(2,1)} %bitcast.179), kind=kOutput, calls=%fused_computation.45 | convolution fusion | flops 6714817024 | bytes 23604736 | tf_op jit(solution)/shard_map/dot_general | solution.py:446
  354.9 3.4 fusion.45
  358.4 1.9 convolution_convert_fusion.1.grad_mixed
  360.3 3.3 copy-done.1
  363.7 21.1 %attend_back.1 = (bf16[512,1280]{1,0:T(8,128)(2,1)S(1)}, bf16[512,1280]{1,0:T(8,128)(2,1)S(1)}, bf16[512,1280]{1,0:T(8,128)(2,1)S(1)}) custom-call(f32[512,3840]{1,0:T(8,128)S(1)} %copy-done.1, f32[512,3840]{1,0:T(8,128)S(1)} %copy-done.1, f32[512,3840]{1,0:T(8,128)S(1)} %copy-done.1, f32[40,512]{1,0:T(8,128)S(1)} %copy-done.9, f32[40,512]{1,0:T(8,128)S(1)} %copy-done.7, ...), custom_call_target="tpu_custom_call" | custom-call | flops 2684354560 | bytes 13107200 | tf_op jit(solution)/shard_map/attend_back/pallas_call | solution.py:625
  384.8 1.9 fusion.3
  386.8 1.9 convolution_add_fusion.4
  388.8 2.3 multiply_reduce_fusion.1
  391.9 1.8 copy-done.44
  394.6 2.3 fusion.49
  399.7 230.9 %reduce_products.1 = (f32[14,40,1280]{2,1,0:T(8,128)}, f32[40,256]{1,0:T(8,128)}) custom-call(bf16[512,1280]{1,0:T(8,128)(2,1)} %copy-done.23, bf16[512,1280]{1,0:T(8,128)(2,1)} %copy-done.31, bf16[512,1280]{1,0:T(8,128)(2,1)} %copy-done.21, bf16[512,1280]{1,0:T(8,128)(2,1)} %copy-done.2, bf16[512,1280]{1,0:T(8,128)(2,1)} %copy-done.20, ...), custom_call_target="tpu_custom_call" | custom-call | tf_op jit(solution)/shard_map/reduce_products/pallas_call | solution.py:417
  630.6 1.6 fusion.30
  632.2 1.6 fusion.27
  636.4 2.9 multiply_add_fusion
  640.1 2.2 multiply_add_fusion.2
  642.3 1.3 reshape.138
  644.5 3.6 all-to-all-start.3
  650.8 2.6 copy.166
  653.4 3.2 all-to-all-done.3
  656.6 1.2 multiply_add_fusion.4
  (235 shorter events, 24.0 us)
Async XLA Ops:
  7.2 8.6 %copy-start.45 = (f32[2,40,64]{2,1,0:T(8,128)S(1)}, f32[2,40,64]{2,1,0:T(8,128)}, u32[]{:S(2)}) copy-start(f32[2,40,64]{2,1,0:T(8,128)} %param.29) | copy-start | bytes 61444
  7.2 8.6 %copy-start.60 = (f32[5,40]{1,0:T(8,128)S(1)}, f32[5,40]{1,0:T(8,128)}, u32[]{:S(2)}) copy-start(f32[5,40]{1,0:T(8,128)} %param.32) | copy-start | bytes 2404
  7.2 8.7 %copy-start.18 = (f32[2,40,5120]{2,1,0:T(8,128)S(1)}, f32[2,40,5120]{2,1,0:T(8,128)}, u32[]{:S(2)}) copy-start(f32[2,40,5120]{2,1,0:T(8,128)} %param.26) | copy-start | bytes 4915204
  9.5 200.6 %all-to-all-start = ((bf16[2,160,320]{2,0,1:T(2,128)(2,1)}), bf16[2,160,320]{2,0,1:T(2,128)(2,1)S(1)}, u32[]{:S(2)}, u32[]{:S(2)}) async-start(bf16[2,160,320]{2,0,1:T(2,128)(2,1)} %copy.171), calls=%async_computation | async-start | bytes 491520 | tf_op jit(solution)/shard_map/all_to_all | solution.py:727
  16.0 192.6 %copy-start.10 = (s32[512]{0:T(512)S(1)}, s32[512]{0:T(512)}, u32[]{:S(2)}) copy-start(s32[512]{0:T(512)} %param.21) | copy-start | bytes 6148
  16.0 192.8 %copy-start.32 = (bf16[2048,320]{0,1:T(8,128)(2,1)S(1)}, bf16[2048,320]{0,1:T(8,128)(2,1)}, u32[]{:S(2)}) copy-start(bf16[2048,320]{0,1:T(8,128)(2,1)} %param.22) | copy-start | bytes 3932164
  210.0 6.3 copy-start.35
  210.0 6.3 copy-start.53
  210.1 12.9 %copy-start.51 = (f32[1280]{0:T(1024)}, f32[1280]{0:T(1024)S(1)}, u32[]{:S(2)}) copy-start(f32[1280]{0:T(1024)S(1)} %get-tuple-element.153) | copy-start | bytes 15364
  210.1 81.5 %all-to-all-start.2 = ((bf16[4,512,320]{1,2,0:T(8,128)(2,1)}), bf16[4,512,320]{1,2,0:T(8,128)(2,1)}, u32[]{:S(2)}, u32[]{:S(2)}) async-start(bf16[4,512,320]{1,2,0:T(8,128)(2,1)} %bitcast.153), calls=%async_computation.2 | async-start | bytes 2621440 | tf_op jit(solution)/shard_map/all_to_all | solution.py:728
  214.4 85.6 %all-gather.2.cloned.1.call-start = ((), (), s32[]{:S(2)}) async-start(), calls=%async_computation.5 | async-start | bytes 6758400 | tf_op jit(solution)/shard_map/all_gather | solution.py:694
  215.7 426.7 %reduce-scatter.2.cloned.1.call-start = ((), (), s32[]{:S(2)}) async-start(), calls=%async_computation.6 | async-start | bytes 6758400 | tf_op jit(solution)/shard_map/reduce_scatter | solution.py:686
  216.3 5.4 copy-start.37
  216.4 5.4 copy-start.39
  222.5 8.6 %copy-start.58 = (f32[512]{0:T(512)}, f32[512]{0:T(512)S(1)}, u32[]{:S(2)}) copy-start(f32[512]{0:T(512)S(1)} %get-tuple-element.204) | copy-start | bytes 6148
  222.5 24.2 %copy-start.12 = (f32[512,1280]{1,0:T(8,128)}, f32[512,1280]{1,0:T(8,128)S(1)}, u32[]{:S(2)}) copy-start(f32[512,1280]{1,0:T(8,128)S(1)} %get-tuple-element.205) | copy-start | bytes 7864324
  222.5 8.6 %copy-start.56 = (f32[512]{0:T(512)}, f32[512]{0:T(512)S(1)}, u32[]{:S(2)}) copy-start(f32[512]{0:T(512)S(1)} %fusion.38) | copy-start | bytes 6148
  222.9 8.2 %copy-start.6 = (f32[40,512]{1,0:T(8,128)}, f32[40,512]{1,0:T(8,128)S(1)}, u32[]{:S(2)}) copy-start(f32[40,512]{1,0:T(8,128)S(1)} %get-tuple-element.200.sines) | copy-start | bytes 245764
  222.9 8.2 %copy-start.8 = (f32[40,512]{1,0:T(8,128)}, f32[40,512]{1,0:T(8,128)S(1)}, u32[]{:S(2)}) copy-start(f32[40,512]{1,0:T(8,128)S(1)} %get-tuple-element.201.cosines) | copy-start | bytes 245764
  223.2 7.9 %copy-start.20 = (bf16[512,1280]{1,0:T(8,128)(2,1)}, bf16[512,1280]{1,0:T(8,128)(2,1)S(1)}, u32[]{:S(2)}) copy-start(bf16[512,1280]{1,0:T(8,128)(2,1)S(1)} %multiply_convert_fusion.4.refs_4_) | copy-start | bytes 3932164
  231.1 15.5 %copy-start = (f32[512,3840]{1,0:T(8,128)}, f32[512,3840]{1,0:T(8,128)S(1)}, u32[]{:S(2)}) copy-start(f32[512,3840]{1,0:T(8,128)S(1)} %fusion.51.query_in.key_in.value_in) | copy-start | bytes 23592964
  231.2 20.3 %slice-start = ((s8[13107200]{0:T(1024)(128)(4,1)}), s8[4194304]{0:T(1024)(128)(4,1)S(1)}, s32[]{:S(2)}) async-start(s8[13107200]{0:T(1024)(128)(4,1)} %bitcast.180), calls=%async_computation.7 | async-start | bytes 8388608
  231.2 20.3 %slice-start.1 = ((s8[13107200]{0:T(1024)(128)(4,1)}), s8[4194304]{0:T(1024)(128)(4,1)S(1)}, s32[]{:S(2)}) async-start(s8[13107200]{0:T(1024)(128)(4,1)} %bitcast.180), calls=%async_computation.8 | async-start | bytes 8388608
  231.2 20.3 %slice-start.2 = ((s8[13107200]{0:T(1024)(128)(4,1)}), s8[4194304]{0:T(1024)(128)(4,1)S(1)}, s32[]{:S(2)}) async-start(s8[13107200]{0:T(1024)(128)(4,1)} %bitcast.180), calls=%async_computation.9 | async-start | bytes 8388608
  251.1 11.8 %copy-start.16 = (f32[512,1280]{1,0:T(8,128)}, f32[512,1280]{1,0:T(8,128)S(1)}, u32[]{:S(2)}) copy-start(f32[512,1280]{1,0:T(8,128)S(1)} %get-tuple-element.207) | copy-start | bytes 7864324
  251.5 11.5 %copy-start.21 = (bf16[512,1280]{1,0:T(8,128)(2,1)}, bf16[512,1280]{1,0:T(8,128)(2,1)S(1)}, u32[]{:S(2)}) copy-start(bf16[512,1280]{1,0:T(8,128)(2,1)S(1)} %multiply_convert_fusion.3.refs_2_) | copy-start | bytes 3932164
  262.9 14.6 %copy-start.61 = (f32[5,40]{1,0:T(8,128)S(1)}, f32[5,40]{1,0:T(8,128)}, u32[]{:S(2)}) copy-start(f32[5,40]{1,0:T(8,128)} %param.34) | copy-start | bytes 2404
  263.0 15.3 %copy-start.62 = (f32[5,40]{1,0:T(8,128)S(1)}, f32[5,40]{1,0:T(8,128)}, u32[]{:S(2)}) copy-start(f32[5,40]{1,0:T(8,128)} %param.33) | copy-start | bytes 2404
  276.6 28.5 %copy-start.23 = (bf16[512,1280]{1,0:T(8,128)(2,1)}, bf16[512,1280]{1,0:T(8,128)(2,1)S(1)}, u32[]{:S(2)}) copy-start(bf16[512,1280]{1,0:T(8,128)(2,1)S(1)} %fusion.9.refs_0_) | copy-start | bytes 3932164
  308.5 336.0 %all-to-all-start.1 = ((bf16[512,4,320]{0,2,1:T(8,128)(2,1)}), bf16[512,4,320]{0,2,1:T(8,128)(2,1)}, u32[]{:S(2)}, u32[]{:S(2)}) async-start(bf16[512,4,320]{0,2,1:T(8,128)(2,1)} %bitcast.22), calls=%async_computation.1 | async-start | bytes 2621440 | tf_op jit(solution)/shard_map/all_to_all | solution.py:779
  317.7 5.1 copy-start.65
  317.7 9.6 %slice-start.4 = ((s8[13107200]{0:T(1024)(128)(4,1)}), s8[4194304]{0:T(1024)(128)(4,1)S(1)}, s32[]{:S(2)}) async-start(s8[13107200]{0:T(1024)(128)(4,1)} %bitcast.184), calls=%async_computation.11 | async-start | bytes 8388608
  317.7 9.6 %slice-start.5 = ((s8[13107200]{0:T(1024)(128)(4,1)}), s8[4194304]{0:T(1024)(128)(4,1)S(1)}, s32[]{:S(2)}) async-start(s8[13107200]{0:T(1024)(128)(4,1)} %bitcast.184), calls=%async_computation.12 | async-start | bytes 8388608
  317.7 9.6 %slice-start.6 = ((s8[13107200]{0:T(1024)(128)(4,1)}), s8[4194304]{0:T(1024)(128)(4,1)S(1)}, s32[]{:S(2)}) async-start(s8[13107200]{0:T(1024)(128)(4,1)} %bitcast.184), calls=%async_computation.13 | async-start | bytes 8388608
  327.3 13.0 %copy-start.17 = (f32[512,1280]{1,0:T(8,128)S(1)}, f32[512,1280]{1,0:T(8,128)}, u32[]{:S(2)}) copy-start(f32[512,1280]{1,0:T(8,128)} %copy-done.16) | copy-start | bytes 7864324
  358.4 26.4 %slice-start.11 = ((s8[9830400]{0:T(1024)(128)(4,1)}), s8[4194304]{0:T(1024)(128)(4,1)S(1)}, s32[]{:S(2)}) async-start(s8[9830400]{0:T(1024)(128)(4,1)} %bitcast.190), calls=%async_computation.18 | async-start | bytes 8388608
  363.7 21.1 %slice-start.12 = ((s8[9830400]{0:T(1024)(128)(4,1)}), s8[4194304]{0:T(1024)(128)(4,1)S(1)}, s32[]{:S(2)}) async-start(s8[9830400]{0:T(1024)(128)(4,1)} %bitcast.190), calls=%async_computation.19 | async-start | bytes 8388608
  363.7 21.1 %slice-start.13 = ((s8[9830400]{0:T(1024)(128)(4,1)}), s8[1441792]{0:T(1024)(128)(4,1)S(1)}, s32[]{:S(2)}) async-start(s8[9830400]{0:T(1024)(128)(4,1)} %bitcast.190), calls=%async_computation.20 | async-start | bytes 2883584
  391.9 5.4 copy-start.14
  399.7 232.5 %copy-start.15 = (bf16[512,1280]{1,0:T(8,128)(2,1)S(1)}, bf16[512,1280]{1,0:T(8,128)(2,1)}, u32[]{:S(2)}) copy-start(bf16[512,1280]{1,0:T(8,128)(2,1)} %copy-done.14) | copy-start | bytes 3932164
  642.3 5.8 copy-start.48
  642.3 5.8 copy-start.49
  642.3 5.8 copy-start.50
  642.3 7.9 %copy-start.36 = (s32[512,32]{0,1:T(8,128)S(1)}, s32[512,32]{0,1:T(8,128)}, u32[]{:S(2)}) copy-start(s32[512,32]{0,1:T(8,128)} %param.20) | copy-start | bytes 196612
  644.5 12.1 %copy-start.26 = (f32[2,160,320]{2,1,0:T(8,128)S(1)}, f32[2,160,320]{2,1,0:T(8,128)}, u32[]{:S(2)}) copy-start(f32[2,160,320]{2,1,0:T(8,128)} %param.35) | copy-start | bytes 1228804
  644.5 12.1 %copy-start.41 = (f32[2,160,320]{2,1,0:T(8,128)S(1)}, f32[2,160,320]{2,1,0:T(8,128)}, u32[]{:S(2)}) copy-start(f32[2,160,320]{2,1,0:T(8,128)} %param.37) | copy-start | bytes 1228804
  644.5 12.1 %copy-start.42 = (f32[2,160,320]{2,1,0:T(8,128)S(1)}, f32[2,160,320]{2,1,0:T(8,128)}, u32[]{:S(2)}) copy-start(f32[2,160,320]{2,1,0:T(8,128)} %param.36) | copy-start | bytes 1228804
  644.5 12.0 %all-to-all-start.3 = ((f32[4,2,40,320]{3,2,1,0:T(8,128)}), f32[4,2,40,320]{3,2,1,0:T(8,128)S(1)}, u32[]{:S(2)}, u32[]{:S(2)}) async-start(f32[4,2,40,320]{3,2,1,0:T(8,128)} %bitcast.154), calls=%async_computation.4 | async-start | bytes 983040 | tf_op jit(solution)/shard_map/all_to_all | solution.py:835
  (40 other events, 119.9 us)
Sparse Core Ops, SparseCore 0:
  218.7 73.1 all-gather.1
  300.1 150.9 reduce-scatter.1

commit v5 on v4

--- a/solution.py
+++ b/solution.py
@@ -201,13 +201,16 @@
 
 
 RING = 3
-
-def reduce_kernel(pieces, lefts_n, rights_n, n, width, small_width, *refs):
+SLOW_EVERY = 3
+SLOW_STEPS = (1, 4, 7, 9, 10, 11)
+LAST_LAG = 5
+
+def reduce_kernel(pieces, lefts_n, rights_n, n, m, width, small_width, *refs):
     lefts, rights, small = refs[:lefts_n], refs[lefts_n:lefts_n + rights_n], refs[lefts_n + rights_n]
     refs = refs[lefts_n + rights_n + 1:]
     out, small_out = refs[:2]
     left_buf, right_buf, flipped, load_sem = refs[2:6]
-    main_bufs, small_bufs = refs[6 : 6 + 16], refs[6 + 16 : 6 + 32]
+    main_bufs, small_bufs, slow_bufs = refs[6 : 6 + 16], refs[6 + 16 : 6 + 32], refs[6 + 32 :]
     z, x, y, c = place()
     meet(z, x, y, c)
     f32, low = jnp.float32, jnp.bfloat16
@@ -342,28 +345,184 @@
     _, small_sibling, small_one, small_two, small_three, small_four, small_drain = lane(small_bufs, 1, 1, small_width)
     both, small_both = main_bufs[0], small_bufs[0]
 
+    def slow_lane(k):
+        whole, in_s, up_in, down_in, total, in_a, in_b, sum_a, sum_b, in_c, in_d, s_sem, up_sem, down_sem, p_sem = slow_bufs
+        half = width // 2
+        front, back = pl.ds(0, half), pl.ds(half, half)
+        to_x, to_y, to_c = device(z, 1 - x, y, c), device(z, x, 1 - y, c), device(z, x, y, 1 - c)
+
+        def remote(src, dst, sems, i, where):
+            return pltpu.make_async_remote_copy(
+                src_ref=src,
+                dst_ref=dst,
+                send_sem=sems.at[k, 2 * i],
+                recv_sem=sems.at[k, 2 * i + 1],
+                device_id=where,
+                device_id_type=MESH,
+            )
+
+        def add(left, right):
+            return (left.astype(f32) + right.astype(f32)).astype(low)
+
+        def sibling():
+            return remote(whole.at[1 - c, k], in_s.at[k], s_sem, 0, to_c)
+
+        def up(b):
+            return remote(whole.at[c, k, b], up_in.at[k, b - 1], up_sem, b - 1, device((z + 1) % 4, x, y, c))
+
+        def down(b):
+            return remote(whole.at[c, k, b], down_in.at[k, b], down_sem, b, device((z + 3) % 4, x, y, c))
+
+        def first():
+            return (
+                remote(total.at[k, :, 1 - y, :, front], in_a.at[k], p_sem, 0, to_y),
+                remote(total.at[k, 1 - x, :, :, back], in_b.at[k], p_sem, 1, to_x),
+            )
+
+        def second():
+            return (
+                remote(sum_a.at[k, 1 - x], in_c.at[k], p_sem, 2, to_x),
+                remote(sum_b.at[k, 1 - y], in_d.at[k], p_sem, 3, to_y),
+            )
+
+        def take(copy, planes):
+            for b in planes:
+                copy(b).wait_recv()
+
+        def pass_on(copy, source, planes):
+            for b in planes:
+                whole[c, k, b] = add(whole[c, k, b], source(b))
+            for b in planes:
+                copy(b).start()
+
+        def from_below(b):
+            return up_in[k, b - 1]
+
+        def from_above(b):
+            return down_in[k, b]
+
+        def stage_one():
+            sibling().wait_recv()
+
+            def body(i, carry):
+                whole[c, k, i] = add(whole[c, k, i], in_s[k, i])
+                return carry
+
+            lax.fori_loop(0, 4, body, 0)
+
+            @pl.when(z == 0)
+            def _():
+                for b in (3, 2, 1):
+                    up(b).start()
+
+            @pl.when(z == 3)
+            def _():
+                for b in (0, 1, 2):
+                    down(b).start()
+
+        def stage_two():
+            @pl.when(z == 1)
+            def _():
+                take(up, (3, 2, 1))
+                pass_on(up, from_below, (3, 2))
+
+            @pl.when(z == 2)
+            def _():
+                take(down, (0, 1, 2))
+                pass_on(down, from_above, (0, 1))
+
+        def stage_three():
+            @pl.when(z == 2)
+            def _():
+                take(up, (3, 2))
+                pass_on(up, from_below, (3,))
+
+            @pl.when(z == 1)
+            def _():
+                take(down, (0, 1))
+                pass_on(down, from_above, (0,))
+
+        def stage_four():
+            for b in range(4):
+
+                @pl.when(z == b)
+                def _():
+                    if b == 3:
+                        take(up, (3,))
+                    if b == 0:
+                        take(down, (0,))
+                    value = whole[c, k, b].astype(f32)
+                    if b > 0:
+                        value = value + from_below(b).astype(f32)
+                    if b < 3:
+                        value = value + from_above(b).astype(f32)
+                    total[k] = value.astype(low)
+
+            for copy in first():
+                copy.start()
+
+        def stage_five():
+            for copy in first():
+                copy.wait_recv()
+            for j in range(2):
+                sum_a[k, j] = add(total[k, j, y, :, :half], in_a[k, j])
+                sum_b[k, j] = add(total[k, x, j, :, half:], in_b[k, j])
+            for copy in second():
+                copy.start()
+
+        def stage_six():
+            for copy in second():
+                copy.wait_recv()
+            out[n + k, :, :half] = sum_a[k, x].astype(f32) + in_c[k].astype(f32)
+            out[n + k, :, half:] = sum_b[k, y].astype(f32) + in_d[k].astype(f32)
+
+        def drain():
+            for copy in (sibling(), *first(), *second()):
+                copy.wait_send()
+            for copy, chip, planes in (
+                (up, 0, (3, 2, 1)),
+                (up, 1, (3, 2)),
+                (up, 2, (3,)),
+                (down, 3, (0, 1, 2)),
+                (down, 2, (0, 1)),
+                (down, 1, (0,)),
+            ):
+
+                @pl.when(z == chip)
+                def _():
+                    for b in planes:
+                        copy(b).wait_send()
+
+        return lambda: sibling().start(), stage_one, stage_two, stage_three, stage_four, stage_five, stage_six, drain
+
+    def load_piece(number, s, start):
+        i, j, begin = pieces[number]
+        for copy in (
+            pltpu.make_async_copy(lefts[i], left_buf.at[s], load_sem.at[s, 0]),
+            pltpu.make_async_copy(rights[j].at[:, pl.ds(begin, width)], right_buf.at[s], load_sem.at[s, 1]),
+        ):
+            copy.start() if start else copy.wait()
+
     def load(k, start):
-        for number, (i, j, begin) in enumerate(pieces):
+        for number in range(n):
+
             @pl.when(k == number)
             def _():
-                s = number % 2
-                for copy in (pltpu.make_async_copy(lefts[i], left_buf.at[s], load_sem.at[s, 0]),
-                             pltpu.make_async_copy(rights[j].at[:, pl.ds(begin, width)], right_buf.at[s], load_sem.at[s, 1])):
-                    copy.start() if start else copy.wait()
-
-    def multiply(k):
-        flipped[...] = left_buf[k % 2].T
+                load_piece(number, number % 2, start)
+
+    def multiply(slot, target, place_in):
+        flipped[...] = left_buf[slot].T
         tile, rows = 256, 16 * ROWS
 
         def body(j, carry):
             cols = pl.ds(pl.multiple_of(j * tile, tile), tile)
             for part in range(2):
                 value = jnp.dot(
-                    flipped[part * rows : (part + 1) * rows], right_buf[k % 2, :, cols], preferred_element_type=f32
+                    flipped[part * rows : (part + 1) * rows], right_buf[slot, :, cols], preferred_element_type=f32
                 )
                 for r in range(16):
                     i = part * 16 + r
-                    both[i % 2, k % RING, i // 8, (i // 4) % 2, (i // 2) % 2, :, cols] = value[
+                    target[i % 2, place_in, i // 8, (i // 4) % 2, (i // 2) % 2, :, cols] = value[
                         r * ROWS : (r + 1) * ROWS
                     ].astype(low)
             return carry
@@ -371,6 +530,9 @@
         lax.fori_loop(0, width // tile, body, 0)
 
     load(0, True)
+    slow = [slow_lane(k) for k in range(m)]
+    if m:
+        load_piece(n, 2, True)
     small_both[:, 0] = small[...]
 
     def step(t, carry):
@@ -379,8 +541,25 @@
             load(t + 1, True)
             load(t, False)
             fresh(t)
-            multiply(t)
+            multiply(t % 2, both, t % RING)
             send_sibling(t)
+        for k in range(m):
+
+            @pl.when(t == SLOW_EVERY * k)
+            def _():
+                load_piece(n + k, 2, False)
+                multiply(2, slow_bufs[0], k)
+                slow[k][0]()
+                if k + 1 < m:
+                    load_piece(n + k + 1, 2, True)
+
+        for k in range(m):
+            for stage, at in enumerate(SLOW_STEPS):
+
+                @pl.when(t == SLOW_EVERY * k + at)
+                def _():
+                    slow[k][stage + 1]()
+
         for j, work in enumerate((lambda: small_sibling(0), lambda: small_one(0), lambda: small_two(0),
                                   lambda: small_three(0), lambda: small_four(0, small_out))):
             @pl.when(t == j)
@@ -391,14 +570,16 @@
             def _():
                 work(t - lag)
 
-        @pl.when(t >= 4)
+        @pl.when(t >= LAST_LAG)
         def _():
-            four(t - 4, out.at[t - 4])
+            four(t - LAST_LAG, out.at[t - LAST_LAG])
         return carry
-    lax.fori_loop(0, n + 4, step, 0)
+    lax.fori_loop(0, n + LAST_LAG, step, 0)
     for k in range(n - RING, n):
         drain(k)
     small_drain(0)
+    for k in range(m):
+        slow[k][-1]()
 
 def buffers(ring, columns):
     dma, reg = pltpu.SemaphoreType.DMA, pltpu.SemaphoreType.REGULAR
@@ -409,20 +590,42 @@
     ends = [pltpu.VMEM((ring, 4, ROWS, columns), low), pltpu.VMEM((ring, 3, ROWS, columns), low)]
     return block + halves + quarters + ends + [dma((ring, 2)), dma((ring, 4)), dma((ring, 4)), dma((ring, 6)), reg((5,)), reg((3,))]
 
-def reduce_products(lefts, rights, pieces, small, width=1280, cid=2):
-    n = len(pieces)
+def slow_buffers(m, columns):
+    dma, half, low = pltpu.SemaphoreType.DMA, columns // 2, jnp.bfloat16
+    lead = [(2, m, 4, 2, 2), (m, 4, 2, 2), (m, 3, 2, 2), (m, 3, 2, 2), (m, 2, 2)]
+    return (
+        [pltpu.VMEM((*shape, ROWS, columns), low) for shape in lead]
+        + [pltpu.VMEM((m, 2, ROWS, half), low)] * 4
+        + [pltpu.VMEM((m, ROWS, half), low)] * 2
+        + [dma((m, 2)), dma((m, 6)), dma((m, 6)), dma((m, 8))]
+    )
+
+
+def reduce_products(lefts, rights, pieces, m, small, width=1280, cid=2):
+    n = len(pieces) - m
     small_width = small.shape[-1]
     tokens = rights[0].shape[0]
     hbm, vmem = pl.BlockSpec(memory_space=pl.ANY), pl.BlockSpec(memory_space=pltpu.VMEM)
     return pl.pallas_call(
-        functools.partial(reduce_kernel, tuple(pieces), len(lefts), len(rights), n, width, small_width),
-        out_shape=[jax.ShapeDtypeStruct((n, ROWS, width), jnp.float32), jax.ShapeDtypeStruct((ROWS, small_width), jnp.float32)],
+        functools.partial(reduce_kernel, tuple(pieces), len(lefts), len(rights), n, m, width, small_width),
+        out_shape=[
+            jax.ShapeDtypeStruct((n + m, ROWS, width), jnp.float32),
+            jax.ShapeDtypeStruct((ROWS, small_width), jnp.float32),
+        ],
         in_specs=[hbm] * (len(lefts) + len(rights)) + [vmem],
         out_specs=[vmem, vmem],
-        scratch_shapes=[pltpu.VMEM((2, tokens, 32 * ROWS), jnp.bfloat16), pltpu.VMEM((2, tokens, width), jnp.bfloat16),
-                        pltpu.VMEM((32 * ROWS, tokens), jnp.bfloat16),
-                        pltpu.SemaphoreType.DMA((2, 2))] + buffers(RING, width) + buffers(1, small_width),
-        compiler_params=pltpu.CompilerParams(collective_id=cid, has_side_effects=True, vmem_limit_bytes=60 * 1024 * 1024),
+        scratch_shapes=[
+            pltpu.VMEM((3, tokens, 32 * ROWS), jnp.bfloat16),
+            pltpu.VMEM((3, tokens, width), jnp.bfloat16),
+            pltpu.VMEM((32 * ROWS, tokens), jnp.bfloat16),
+            pltpu.SemaphoreType.DMA((3, 2)),
+        ]
+        + buffers(RING, width)
+        + buffers(1, small_width)
+        + slow_buffers(m, width),
+        compiler_params=pltpu.CompilerParams(
+            collective_id=cid, has_side_effects=True, vmem_limit_bytes=60 * 1024 * 1024
+        ),
         name="reduce_products",
     )(*lefts, *rights, small)
 
@@ -825,8 +1028,14 @@
     pieces += [(3, 3, 0)] + [(4, 4 + j, 0) for j in range(3)] + [(5, 7, 0)]
     lefts = [stream_low, grad_ffn_out, normed_ffn, attn_mix, normed_attn, tok_act]
     rights = [grad_head_pre, ffn_act, grad_ffn_pre, grad_attn_out, *grad_qkv_pre, grad_tok_out]
+    down_at = 1
     if fast:
-        shares, small_share = reduce_products(lefts, rights, pieces, owned(small))
+        slow = [down_at, down_at + 1]
+        order = [i for i in range(len(pieces)) if i not in slow] + slow
+        summed_shares, small_share = reduce_products(
+            lefts, rights, [pieces[i] for i in order], len(slow), owned(small)
+        )
+        shares = [summed_shares[order.index(i)] for i in range(len(pieces))]
     else:
         shares = [
             summed(bilinear_flipped(lefts[i], rights[j][:, start : start + D])) for i, j, start in pieces
@@ -834,7 +1043,6 @@
         small_share = summed(small)
     head_share = lax.all_to_all(head_share, "head", split_axis=0, concat_axis=0)
     head_share = head_share.transpose(1, 0, 2, 3).reshape(readout_params.shape)
-    down_at = 1
     up_at = down_at + wide
     wo_at = up_at + wide
     square_share = jnp.stack(

time: 670 us -> 652 us (0.973)
  Pallas kernels: 456 us -> 439 us
    pallas_call x1, Pallas kernels: 231 us -> 213 us  [reduce_products(): pl.pallas_call(functools.partial(reduce_kernel, tuple(pieces), len(lefts)...]
  transfers between devices with their start and end apart: 6 -> 6, of which waited for: 1 -> 1; matrix products, arithmetic and copies ran while one was open for 24% -> 24% of each run, Pallas kernels for 69% -> 68%
where the time goes in v5:
time: 652 us; the launch traced here: 647 us
  Pallas kernels  439 us (67%)
  matrix products  117 us (18%)
  local copies, waits for them, and re-layouts  37.9 us (6%)
  other arithmetic  17.6 us (3%)
  starting transfers between devices  17 us (3%)
  between operations  15.9 us (2%)
    pallas_call x1, Pallas kernels, reduce_products(): pl.pallas_call(functools.partial(reduce_kernel, tuple(pieces), len(lefts)...  213 us
    pallas_call x1, Pallas kernels, gather(): pl.pallas_call(functools.partial(gather_kernel, tuple(early), tuple(late)...  189 us
    dot_general x11, matrix products, matrix_multiply(): return jnp.dot(left_mat, right_mat, preferred_element_type=jnp.float32)  60.4 us
    dot_general x12, matrix products, flipped_bilinear(): lax.dot_general(left_mat, right_mat, (((1,), (1,)), ((), ())), preferred_...  55.8 us
    pallas_call x2, Pallas kernels, attention_call(): pl.pallas_call(kernel, grid=(HEADS // STEP_HEADS,), out_shape=out_shape,...  36.7 us
    unnamed x173, local copies, waits for them, and re-layouts  19.1 us
  transfers between devices with their start and end apart: 6, of which 1 were waited for; matrix products, arithmetic and copies ran while one was open for 24% of the time, Pallas kernels for 68%

profile of v5, /device:TPU:0, one launch (start us, length us, event | category | flops | bytes accessed | tf_op | source)
XLA Modules:
  0.0 647.4 jit_solution(6953558093980286913)
XLA Ops:
  7.2 2.2 copy.171
  9.5 4.3 all-to-all-start
  13.7 1.3 convert_element_type.87
  18.5 189.0 %gather_weights.1 = (bf16[4,2,2,2,40,1536]{5,4,3,2,1,0:T(8,128)(2,1)}, bf16[4,2,2,2,40,3840]{5,4,3,2,1,0:T(8,128)(2,1)}, bf16[4,2,2,2,40,1280]{5,4,3,2,1,0:T(8,1...) custom-call(bf16[40,1536]{1,0:T(8,128)(2,1)} %concatenate.31.refs_0_, ...), custom_call_target="tpu_custom_call" | custom-call | tf_op jit(solution)/shard_map/gather_weights/pallas_call | solution.py:180
  208.8 1.2 copy.172
  210.1 4.3 all-to-all-start.2
  216.0 3.5 multiply_convert_fusion.5
  219.5 1.9 fusion.16
  222.9 1.2 slice-done.9
  224.1 1.4 slice-done.10
  225.5 5.2 fusion.51.query_in.key_in.value_in
  230.8 15.5 %attend.1 = (bf16[512,1280]{1,0:T(8,128)(2,1)S(1)}, f32[16,1,512]{2,1,0:T(1,128)S(1)}) custom-call(f32[512,3840]{1,0:T(8,128)S(1)} %fusion.51.query_in.key_in.value_in, f32[512,3840]{1,0:T(8,128)S(1)} %fusion.51.query_in.key_in.value_in, f32[512,3840]{1,0:T(8,128)S(1)} %fusion.51.query_in.key_in.value_in, f32[40,512]{1,0:T(8,128)S(1)} %get-tuple-element.201.cosines, ...), custom_call_target="tpu_custom_call" | custom-call | flops 2684354560 | bytes 13107200 | tf_op jit(solution)/shard_map/attend/pallas_call | solution.py:828
  246.4 4.4 multiply_reduce_fusion.4
  251.2 11.4 %multiply_convert_fusion.1 = (bf16[512,5120]{1,0:T(8,128)(2,1)}, f32[512,5120]{1,0:T(8,128)}) fusion(bf16[512,1280]{1,0:T(8,128)(2,1)S(1)} %multiply_convert_fusion.3.refs_2_, bf16[1280,5120]{1,0:T(8,128)(2,1)S(1)} %bitcast.182), kind=kOutput, calls=%fused_computation.2 | convolution fusion | flops 6723993600 | bytes 30146560 | tf_op jit(solution)/shard_map/dot_general | solution.py:645
  262.7 13.7 %fusion.9.refs_0_ = bf16[512,1280]{1,0:T(8,128)(2,1)S(1)} fusion(f32[512,1280]{1,0:T(8,128)S(1)} %get-tuple-element.207, bf16[512,5120]{1,0:T(8,128)(2,1)} %get-tuple-element.208.refs_7_, bf16[1280,5120]{1,0:T(8,128)(2,1)} %bitcast.183), kind=kOutput, calls=%fused_computation.28 | convolution fusion | flops 6712197120 | bytes 22282240 | tf_op jit(solution)/shard_map/dot_general | solution.py:649
  279.8 5.9 fusion.23
  285.7 2.4 copy.155
  288.1 1.6 pad_maximum_fusion
  289.6 2.0 copy.157
  291.6 8.4 %convolution_convert_fusion = bf16[2560,1280]{1,0:T(8,128)(2,1)} fusion(bf16[2560,512]{1,0:T(8,128)(2,1)} %bitcast.163, bf16[512,1280]{0,1:T(8,128)(2,1)} %bitcast.25), kind=kOutput, calls=%fused_computation | convolution fusion | flops 3358720000 | bytes 10485760 | tf_op jit(solution)/shard_map/dot_general | solution.py:645
  300.0 5.1 fusion.13
  305.1 1.9 fusion.7
  307.0 1.5 copy.141
  308.5 4.5 all-to-all-start.1
  313.0 4.5 convolution_bitcast_fusion.1
  317.5 5.1 fusion.50
  322.6 3.4 fusion.48
  327.1 13.0 %multiply_convert_fusion.refs_8_ = bf16[512,5120]{1,0:T(8,128)(2,1)} fusion(f32[512,5120]{1,0:T(8,128)} %get-tuple-element.209, bf16[512,1280]{1,0:T(8,128)(2,1)S(1)} %get-tuple-element.210.refs_1_, bf16[1280,5120]{1,0:T(8,128)(2,1)S(1)} %bitcast.186), kind=kOutput, calls=%fused_computation.1 | convolution fusion | flops 6734479360 | bytes 30146560 | tf_op jit(solution)/shard_map/dot_general | solution.py:645
  340.1 14.5 %multiply_reduce_fusion = (bf16[1280]{0:T(1024)(128)(2,1)S(1)}, f32[512]{0:T(512)S(1)}, f32[512,1280]{1,0:T(8,128)}) fusion(f32[512,1280]{1,0:T(8,128)S(1)} %copy-done.17, f32[512]{0:T(512)S(1)} %fusion.39, f32[1280]{0:T(1024)S(1)} %get-tuple-element.152, bf16[512,5120]{1,0:T(8,128)(2,1)} %multiply_convert_fusion.refs_8_, bf16[1280,5120]{1,0:T(8,128)(2,1)} %bitcast.179), kind=kOutput, calls=%fused_computation.45 | convolution fusion | flops 6714817024 | bytes 23604736 | tf_op jit(solution)/shard_map/dot_general | solution.py:649
  354.6 3.4 fusion.45
  358.2 1.9 convolution_convert_fusion.1.grad_mixed
  360.1 3.3 copy-done.1
  363.4 21.1 %attend_back.1 = (bf16[512,1280]{1,0:T(8,128)(2,1)S(1)}, bf16[512,1280]{1,0:T(8,128)(2,1)S(1)}, bf16[512,1280]{1,0:T(8,128)(2,1)S(1)}) custom-call(f32[512,3840]{1,0:T(8,128)S(1)} %copy-done.1, f32[512,3840]{1,0:T(8,128)S(1)} %copy-done.1, f32[512,3840]{1,0:T(8,128)S(1)} %copy-done.1, f32[40,512]{1,0:T(8,128)S(1)} %copy-done.9, f32[40,512]{1,0:T(8,128)S(1)} %copy-done.7, ...), custom_call_target="tpu_custom_call" | custom-call | flops 2684354560 | bytes 13107200 | tf_op jit(solution)/shard_map/attend_back/pallas_call | solution.py:828
  384.6 1.9 fusion.3
  386.6 1.9 convolution_add_fusion.4
  388.6 2.3 multiply_reduce_fusion.1
  391.8 1.8 copy-done.44
  394.4 2.3 fusion.49
  399.5 213.3 %reduce_products.1 = (f32[14,40,1280]{2,1,0:T(8,128)}, f32[40,256]{1,0:T(8,128)}) custom-call(bf16[512,1280]{1,0:T(8,128)(2,1)} %copy-done.23, bf16[512,1280]{1,0:T(8,128)(2,1)} %copy-done.31, bf16[512,1280]{1,0:T(8,128)(2,1)} %copy-done.21, bf16[512,1280]{1,0:T(8,128)(2,1)} %copy-done.2, bf16[512,1280]{1,0:T(8,128)(2,1)} %copy-done.20, ...), custom_call_target="tpu_custom_call" | custom-call | tf_op jit(solution)/shard_map/reduce_products/pallas_call | solution.py:609
  612.8 1.6 fusion.30
  614.5 1.6 fusion.27
  618.6 2.9 multiply_add_fusion
  622.3 2.2 multiply_add_fusion.2
  624.6 1.3 reshape.138
  626.7 3.6 all-to-all-start.3
  633.0 2.6 copy.166
  635.6 3.2 all-to-all-done.3
  638.8 1.2 multiply_add_fusion.4
  (235 shorter events, 23.9 us)
Async XLA Ops:
  7.2 8.6 %copy-start.45 = (f32[2,40,64]{2,1,0:T(8,128)S(1)}, f32[2,40,64]{2,1,0:T(8,128)}, u32[]{:S(2)}) copy-start(f32[2,40,64]{2,1,0:T(8,128)} %param.29) | copy-start | bytes 61444
  7.2 8.6 %copy-start.60 = (f32[5,40]{1,0:T(8,128)S(1)}, f32[5,40]{1,0:T(8,128)}, u32[]{:S(2)}) copy-start(f32[5,40]{1,0:T(8,128)} %param.32) | copy-start | bytes 2404
  7.2 8.7 %copy-start.18 = (f32[2,40,5120]{2,1,0:T(8,128)S(1)}, f32[2,40,5120]{2,1,0:T(8,128)}, u32[]{:S(2)}) copy-start(f32[2,40,5120]{2,1,0:T(8,128)} %param.26) | copy-start | bytes 4915204
  9.5 200.6 %all-to-all-start = ((bf16[2,160,320]{2,0,1:T(2,128)(2,1)}), bf16[2,160,320]{2,0,1:T(2,128)(2,1)S(1)}, u32[]{:S(2)}, u32[]{:S(2)}) async-start(bf16[2,160,320]{2,0,1:T(2,128)(2,1)} %copy.171), calls=%async_computation | async-start | bytes 491520 | tf_op jit(solution)/shard_map/all_to_all | solution.py:930
  16.0 192.6 %copy-start.10 = (s32[512]{0:T(512)S(1)}, s32[512]{0:T(512)}, u32[]{:S(2)}) copy-start(s32[512]{0:T(512)} %param.21) | copy-start | bytes 6148
  16.0 192.8 %copy-start.32 = (bf16[2048,320]{0,1:T(8,128)(2,1)S(1)}, bf16[2048,320]{0,1:T(8,128)(2,1)}, u32[]{:S(2)}) copy-start(bf16[2048,320]{0,1:T(8,128)(2,1)} %param.22) | copy-start | bytes 3932164
  210.0 5.9 copy-start.35
  210.0 6.0 copy-start.53
  210.1 12.5 %copy-start.51 = (f32[1280]{0:T(1024)}, f32[1280]{0:T(1024)S(1)}, u32[]{:S(2)}) copy-start(f32[1280]{0:T(1024)S(1)} %get-tuple-element.153) | copy-start | bytes 15364
  210.1 81.5 %all-to-all-start.2 = ((bf16[4,512,320]{1,2,0:T(8,128)(2,1)}), bf16[4,512,320]{1,2,0:T(8,128)(2,1)}, u32[]{:S(2)}, u32[]{:S(2)}) async-start(bf16[4,512,320]{1,2,0:T(8,128)(2,1)} %bitcast.153), calls=%async_computation.2 | async-start | bytes 2621440 | tf_op jit(solution)/shard_map/all_to_all | solution.py:931
  214.4 85.6 %all-gather.2.cloned.1.call-start = ((), (), s32[]{:S(2)}) async-start(), calls=%async_computation.5 | async-start | bytes 6758400 | tf_op jit(solution)/shard_map/all_gather | solution.py:897
  215.7 408.9 %reduce-scatter.2.cloned.1.call-start = ((), (), s32[]{:S(2)}) async-start(), calls=%async_computation.6 | async-start | bytes 6758400 | tf_op jit(solution)/shard_map/reduce_scatter | solution.py:889
  216.0 5.4 copy-start.37
  216.0 5.4 copy-start.39
  222.1 8.6 %copy-start.58 = (f32[512]{0:T(512)}, f32[512]{0:T(512)S(1)}, u32[]{:S(2)}) copy-start(f32[512]{0:T(512)S(1)} %get-tuple-element.204) | copy-start | bytes 6148
  222.2 24.2 %copy-start.12 = (f32[512,1280]{1,0:T(8,128)}, f32[512,1280]{1,0:T(8,128)S(1)}, u32[]{:S(2)}) copy-start(f32[512,1280]{1,0:T(8,128)S(1)} %get-tuple-element.205) | copy-start | bytes 7864324
  222.2 8.6 %copy-start.56 = (f32[512]{0:T(512)}, f32[512]{0:T(512)S(1)}, u32[]{:S(2)}) copy-start(f32[512]{0:T(512)S(1)} %fusion.38) | copy-start | bytes 6148
  222.6 8.2 %copy-start.6 = (f32[40,512]{1,0:T(8,128)}, f32[40,512]{1,0:T(8,128)S(1)}, u32[]{:S(2)}) copy-start(f32[40,512]{1,0:T(8,128)S(1)} %get-tuple-element.200.sines) | copy-start | bytes 245764
  222.6 8.2 %copy-start.8 = (f32[40,512]{1,0:T(8,128)}, f32[40,512]{1,0:T(8,128)S(1)}, u32[]{:S(2)}) copy-start(f32[40,512]{1,0:T(8,128)S(1)} %get-tuple-element.201.cosines) | copy-start | bytes 245764
  222.9 7.9 %copy-start.20 = (bf16[512,1280]{1,0:T(8,128)(2,1)}, bf16[512,1280]{1,0:T(8,128)(2,1)S(1)}, u32[]{:S(2)}) copy-start(bf16[512,1280]{1,0:T(8,128)(2,1)S(1)} %multiply_convert_fusion.4.refs_4_) | copy-start | bytes 3932164
  230.8 15.6 %copy-start = (f32[512,3840]{1,0:T(8,128)}, f32[512,3840]{1,0:T(8,128)S(1)}, u32[]{:S(2)}) copy-start(f32[512,3840]{1,0:T(8,128)S(1)} %fusion.51.query_in.key_in.value_in) | copy-start | bytes 23592964
  230.8 20.4 %slice-start = ((s8[13107200]{0:T(1024)(128)(4,1)}), s8[4194304]{0:T(1024)(128)(4,1)S(1)}, s32[]{:S(2)}) async-start(s8[13107200]{0:T(1024)(128)(4,1)} %bitcast.180), calls=%async_computation.7 | async-start | bytes 8388608
  230.8 20.4 %slice-start.1 = ((s8[13107200]{0:T(1024)(128)(4,1)}), s8[4194304]{0:T(1024)(128)(4,1)S(1)}, s32[]{:S(2)}) async-start(s8[13107200]{0:T(1024)(128)(4,1)} %bitcast.180), calls=%async_computation.8 | async-start | bytes 8388608
  230.8 20.4 %slice-start.2 = ((s8[13107200]{0:T(1024)(128)(4,1)}), s8[4194304]{0:T(1024)(128)(4,1)S(1)}, s32[]{:S(2)}) async-start(s8[13107200]{0:T(1024)(128)(4,1)} %bitcast.180), calls=%async_computation.9 | async-start | bytes 8388608
  250.9 11.8 %copy-start.16 = (f32[512,1280]{1,0:T(8,128)}, f32[512,1280]{1,0:T(8,128)S(1)}, u32[]{:S(2)}) copy-start(f32[512,1280]{1,0:T(8,128)S(1)} %get-tuple-element.207) | copy-start | bytes 7864324
  251.2 11.5 %copy-start.21 = (bf16[512,1280]{1,0:T(8,128)(2,1)}, bf16[512,1280]{1,0:T(8,128)(2,1)S(1)}, u32[]{:S(2)}) copy-start(bf16[512,1280]{1,0:T(8,128)(2,1)S(1)} %multiply_convert_fusion.3.refs_2_) | copy-start | bytes 3932164
  262.7 14.6 %copy-start.61 = (f32[5,40]{1,0:T(8,128)S(1)}, f32[5,40]{1,0:T(8,128)}, u32[]{:S(2)}) copy-start(f32[5,40]{1,0:T(8,128)} %param.34) | copy-start | bytes 2404
  262.7 15.3 %copy-start.62 = (f32[5,40]{1,0:T(8,128)S(1)}, f32[5,40]{1,0:T(8,128)}, u32[]{:S(2)}) copy-start(f32[5,40]{1,0:T(8,128)} %param.33) | copy-start | bytes 2404
  276.4 28.7 %copy-start.23 = (bf16[512,1280]{1,0:T(8,128)(2,1)}, bf16[512,1280]{1,0:T(8,128)(2,1)S(1)}, u32[]{:S(2)}) copy-start(bf16[512,1280]{1,0:T(8,128)(2,1)S(1)} %fusion.9.refs_0_) | copy-start | bytes 3932164
  308.5 318.2 %all-to-all-start.1 = ((bf16[512,4,320]{0,2,1:T(8,128)(2,1)}), bf16[512,4,320]{0,2,1:T(8,128)(2,1)}, u32[]{:S(2)}, u32[]{:S(2)}) async-start(bf16[512,4,320]{0,2,1:T(8,128)(2,1)} %bitcast.22), calls=%async_computation.1 | async-start | bytes 2621440 | tf_op jit(solution)/shard_map/all_to_all | solution.py:982
  317.4 5.2 copy-start.65
  317.5 9.6 %slice-start.4 = ((s8[13107200]{0:T(1024)(128)(4,1)}), s8[4194304]{0:T(1024)(128)(4,1)S(1)}, s32[]{:S(2)}) async-start(s8[13107200]{0:T(1024)(128)(4,1)} %bitcast.184), calls=%async_computation.11 | async-start | bytes 8388608
  317.5 9.6 %slice-start.5 = ((s8[13107200]{0:T(1024)(128)(4,1)}), s8[4194304]{0:T(1024)(128)(4,1)S(1)}, s32[]{:S(2)}) async-start(s8[13107200]{0:T(1024)(128)(4,1)} %bitcast.184), calls=%async_computation.12 | async-start | bytes 8388608
  317.5 9.6 %slice-start.6 = ((s8[13107200]{0:T(1024)(128)(4,1)}), s8[4194304]{0:T(1024)(128)(4,1)S(1)}, s32[]{:S(2)}) async-start(s8[13107200]{0:T(1024)(128)(4,1)} %bitcast.184), calls=%async_computation.13 | async-start | bytes 8388608
  327.1 13.0 %copy-start.17 = (f32[512,1280]{1,0:T(8,128)S(1)}, f32[512,1280]{1,0:T(8,128)}, u32[]{:S(2)}) copy-start(f32[512,1280]{1,0:T(8,128)} %copy-done.16) | copy-start | bytes 7864324
  358.2 26.5 %slice-start.11 = ((s8[9830400]{0:T(1024)(128)(4,1)}), s8[4194304]{0:T(1024)(128)(4,1)S(1)}, s32[]{:S(2)}) async-start(s8[9830400]{0:T(1024)(128)(4,1)} %bitcast.190), calls=%async_computation.18 | async-start | bytes 8388608
  363.4 21.2 %slice-start.12 = ((s8[9830400]{0:T(1024)(128)(4,1)}), s8[4194304]{0:T(1024)(128)(4,1)S(1)}, s32[]{:S(2)}) async-start(s8[9830400]{0:T(1024)(128)(4,1)} %bitcast.190), calls=%async_computation.19 | async-start | bytes 8388608
  363.4 21.2 %slice-start.13 = ((s8[9830400]{0:T(1024)(128)(4,1)}), s8[1441792]{0:T(1024)(128)(4,1)S(1)}, s32[]{:S(2)}) async-start(s8[9830400]{0:T(1024)(128)(4,1)} %bitcast.190), calls=%async_computation.20 | async-start | bytes 2883584
  391.8 5.4 copy-start.14
  399.5 214.9 %copy-start.15 = (bf16[512,1280]{1,0:T(8,128)(2,1)S(1)}, bf16[512,1280]{1,0:T(8,128)(2,1)}, u32[]{:S(2)}) copy-start(bf16[512,1280]{1,0:T(8,128)(2,1)} %copy-done.14) | copy-start | bytes 3932164
  624.5 5.8 copy-start.48
  624.5 5.8 copy-start.49
  624.5 5.8 copy-start.50
  624.5 7.9 %copy-start.36 = (s32[512,32]{0,1:T(8,128)S(1)}, s32[512,32]{0,1:T(8,128)}, u32[]{:S(2)}) copy-start(s32[512,32]{0,1:T(8,128)} %param.20) | copy-start | bytes 196612
  626.7 12.1 %copy-start.26 = (f32[2,160,320]{2,1,0:T(8,128)S(1)}, f32[2,160,320]{2,1,0:T(8,128)}, u32[]{:S(2)}) copy-start(f32[2,160,320]{2,1,0:T(8,128)} %param.35) | copy-start | bytes 1228804
  626.7 12.1 %copy-start.41 = (f32[2,160,320]{2,1,0:T(8,128)S(1)}, f32[2,160,320]{2,1,0:T(8,128)}, u32[]{:S(2)}) copy-start(f32[2,160,320]{2,1,0:T(8,128)} %param.37) | copy-start | bytes 1228804
  626.7 12.1 %copy-start.42 = (f32[2,160,320]{2,1,0:T(8,128)S(1)}, f32[2,160,320]{2,1,0:T(8,128)}, u32[]{:S(2)}) copy-start(f32[2,160,320]{2,1,0:T(8,128)} %param.36) | copy-start | bytes 1228804
  626.7 12.0 %all-to-all-start.3 = ((f32[4,2,40,320]{3,2,1,0:T(8,128)}), f32[4,2,40,320]{3,2,1,0:T(8,128)S(1)}, u32[]{:S(2)}, u32[]{:S(2)}) async-start(f32[4,2,40,320]{3,2,1,0:T(8,128)} %bitcast.154), calls=%async_computation.4 | async-start | bytes 983040 | tf_op jit(solution)/shard_map/all_to_all | solution.py:1044
  (40 other events, 119.9 us)
Sparse Core Ops, SparseCore 0:
  218.7 73.0 all-gather.1
  300.1 155.5 reduce-scatter.1
